TPU v7x, 512 devices: a whole 4x4x16 slice. The times are simulated.
512 devices in a mesh: seq: 32 (over z, core), head: 16 (over y, x).
Axes of the slice: x: 4, y: 4, z: 16, core: 2. Of those that a mesh axis runs over, the one named last changes fastest.
Arguments:
- queries: bfloat16 [4096, 8192], P('seq', 'head'), may hold values from -6 to 6
- key_value: bfloat16 [4096, 2048], P('seq', 'head'), may hold values from -6 to 6
- grad_out: bfloat16 [4096, 8192], P('seq', 'head'), may hold values from -60 to 60
- ssm_grad: bfloat16 [4096, 8192], P('seq', 'head'), may hold values from -60 to 60
- b_proj: bfloat16 [4096, 128], P('seq'), may hold values from -1.5 to 1.5
- c_proj: bfloat16 [4096, 128], P('seq'), may hold values from -1.5 to 1.5
- decay_log: float32 [128, 4096], P('head', 'seq'), may hold values from -1.2 to 0
- skip_gain: float32 [128], P('head'), may hold values from 1 to 16
Outputs:
- grad_queries: bfloat16 [4096, 8192], P('seq', 'head')
- grad_key_value: bfloat16 [4096, 2048], P('seq', 'head')
- grad_ssm_in: bfloat16 [4096, 8192], P('seq', 'head')
All inputs are finite; a program needn't handle non-finite values. Where the computation divides by a largest or mean magnitude, that divisor is 1e-20 or more.
Results may differ from a plain program's by a relative error of at most 0.012.
Values may be sent and summed in bfloat16 or wider, within the bound.
No kernel may reach another device: no remote copies, remote signals or barrier semaphores. Data moves between devices by JAX's collectives and lax.ppermute only.
A program may use at most 64 MiB of HBM per device.

v0:
```python
import math

import jax
import jax.numpy as jnp
from jax import lax
from jax.experimental import pallas as pl
from jax.experimental.pallas import tpu as pltpu
from jax.sharding import Mesh
from jax.sharding import PartitionSpec as P


SEQ = ("hi", "lo", "c")
HEAD = ("y", "xh", "xp")
SIZES = (4, 4, 2, 4, 2, 2)
CHIPS = 16
TOK = 128
SSM_HEADS = 8
SSM_DIM = 64
SCALE = 1.0 / math.sqrt(128)
EPSILON = 1e-6
HIGHEST = lax.Precision.HIGHEST
f32 = jnp.float32
bf16 = jnp.bfloat16


def dot(a, b, dims, precision=None):
    return lax.dot_general(a, b, (dims, ((), ())), precision=precision, preferred_element_type=f32)


NN = ((1,), (0,))
NT = ((1,), (1,))
TN = ((0,), (0,))


def heads_to_rows(x):
    return jnp.concatenate([x[:, 128 * h : 128 * (h + 1)] for h in range(4)], axis=0)


def attention_kernel(pos_ref, q_ref, do_ref, *refs):
    pieces, (dq_ref, dkv_ref, peak_ref, kv_ref, p_ref, dp_ref, outt_ref, dqt_ref, sems) = refs[:4], refs[4:]
    copies = [pltpu.make_async_copy(piece, kv_ref.at[r], sems.at[r]) for r, piece in enumerate(pieces)]
    for copy in copies:
        copy.start()
    chip, core = pos_ref[0], pos_ref[1]
    lane_group = lax.rem(chip, 4)
    q = heads_to_rows(q_ref[...])
    do = heads_to_rows(do_ref[...])
    width = q.shape[0]

    def place(z):
        return lax.rem(lax.rem(z, 4) - lane_group + 4, 4), z // 4

    def rows_at(z):
        return pl.ds(pl.multiple_of(z * 2 * TOK, 2 * TOK), 2 * TOK)

    def both_cores(z, part):
        rel, hi = place(z)
        return jnp.concatenate([kv_ref[rel, 0, hi, part], kv_ref[rel, 1, hi, part]], axis=0)

    def partial_rows(x, op):
        return op(x.reshape(2 * TOK // 8, 8, width), axis=0)

    def score_step(z, carry, masked):
        old, total = carry
        s = dot(both_cores(z, 0), q, NT) * SCALE
        if masked:
            key = lax.broadcasted_iota(jnp.int32, s.shape, 0)
            query = lax.rem(lax.broadcasted_iota(jnp.int32, s.shape, 1), TOK) + core * TOK
            s = jnp.where(key <= query, s, -1e30)
        top = jnp.maximum(old, jnp.max(partial_rows(s, jnp.max), axis=0, keepdims=True))
        p_ref[rows_at(z), :] = s
        return top, total * jnp.exp(old - top) + partial_rows(jnp.exp(s - top), jnp.sum)

    for copy in copies:
        copy.wait()
    carry = score_step(chip, (jnp.full((1, width), -1e30, f32), jnp.zeros((8, width), f32)), True)
    top, total = lax.fori_loop(0, chip, lambda z, c: score_step(z, c, False), carry)
    lse = top + jnp.log(jnp.sum(total, axis=0, keepdims=True))
    outt_ref[...] = jnp.zeros_like(outt_ref)
    dqt_ref[...] = jnp.zeros_like(dqt_ref)

    def output_step(z, _):
        rel, hi = place(z)
        p = jnp.exp(p_ref[rows_at(z), :] - lse)
        p_ref[rows_at(z), :] = p
        p_b = p.astype(bf16)
        values = both_cores(z, 1)
        outt_ref[...] += dot(values, p_b, TN)
        dp_ref[rows_at(z), :] = dot(values, do, NT)
        dv = dot(p_b, do, NN).astype(bf16)
        dkv_ref[0, rel, hi, 1] = dv[:TOK]
        dkv_ref[1, rel, hi, 1] = dv[TOK:]
        return 0

    lax.fori_loop(0, chip + 1, output_step, 0)
    dot_rows = jnp.concatenate([do_ref[:, 128 * h : 128 * (h + 1)].astype(f32).T for h in range(4)], axis=1)
    delta = jnp.sum(dot_rows * outt_ref[...].astype(bf16).astype(f32), axis=0, keepdims=True)

    def gradient_step(z, _):
        rel, hi = place(z)
        ds = (p_ref[rows_at(z), :] * (dp_ref[rows_at(z), :] - delta)).astype(bf16)
        dk = (dot(ds, q, NN) * SCALE).astype(bf16)
        dkv_ref[0, rel, hi, 0] = dk[:TOK]
        dkv_ref[1, rel, hi, 0] = dk[TOK:]
        dqt_ref[...] += dot(both_cores(z, 0), ds, TN)
        return 0

    lax.fori_loop(0, chip + 1, gradient_step, 0)

    def clear_step(z, _):
        rel, hi = place(z)
        for c in range(2):
            for part in range(2):
                dkv_ref[c, rel, hi, part] = jnp.zeros((TOK, 128), bf16)
        return 0

    lax.fori_loop(chip + 1, CHIPS, clear_step, 0)
    dqt = dqt_ref[...] * SCALE
    for h in range(4):
        dq_ref[:, 128 * h : 128 * (h + 1)] = dqt[:, TOK * h : TOK * (h + 1)].T
    peak_ref[...] = jnp.broadcast_to(jnp.max(jnp.abs(dqt), keepdims=True), peak_ref.shape)


def spread_heads():
    shape = (SSM_HEADS, SSM_HEADS * SSM_DIM)
    row = lax.broadcasted_iota(jnp.int32, shape, 0)
    lane = lax.broadcasted_iota(jnp.int32, shape, 1)
    return (lane // SSM_DIM == row).astype(f32)


def running_decay(decay):
    row = lax.broadcasted_iota(jnp.int32, (TOK, TOK), 0)
    col = lax.broadcasted_iota(jnp.int32, (TOK, TOK), 1)
    lower = (col <= row).astype(f32)
    wide = dot(decay, spread_heads(), TN, HIGHEST)
    return dot(lower, wide, NN, HIGHEST)


def state_kernel(dy_ref, c_ref, decay_ref, out_ref):
    wide = running_decay(decay_ref[...])
    weighted = dy_ref[...].astype(f32) * jnp.exp(wide)
    states = dot(weighted.astype(bf16), c_ref[...], TN).astype(bf16)
    row = lax.broadcasted_iota(jnp.int32, (8, 128), 0)
    for k in range(2 * CHIPS):
        head = k * 16 // SSM_DIM
        total = jnp.broadcast_to(wide[TOK - 1 :, head * SSM_DIM : head * SSM_DIM + 1], (8, 128))
        high = total.astype(bf16).astype(f32)
        out_ref[k, :16, :] = states[16 * k : 16 * (k + 1), :]
        out_ref[k, 16:, :] = jnp.where(row == 0, high, total - high).astype(bf16)


def scan_kernel(state_ref, out_ref):
    flow = jnp.zeros((16, 128), f32)
    for k in reversed(range(2 * CHIPS)):
        out_ref[k] = flow.astype(bf16)
        total = state_ref[k, 16:, :].astype(f32)
        flow = state_ref[k, :16, :].astype(f32) + jnp.exp(total[:1] + total[1:2]) * flow


def ssm_kernel(dy_ref, b_ref, c_ref, decay_ref, skip_ref, flow_ref, dx_ref, peak_ref):
    decay = decay_ref[...]
    dy = dy_ref[...]
    wide = running_decay(decay)
    row = lax.broadcasted_iota(jnp.int32, (TOK, TOK), 0)
    col = lax.broadcasted_iota(jnp.int32, (TOK, TOK), 1)
    narrow = dot(decay, (row <= col).astype(f32), NN, HIGHEST)
    pairs = dot(b_ref[...], c_ref[...], NT)
    skip = jnp.sum(spread_heads() * skip_ref[...], axis=0, keepdims=True)
    carried = dot(b_ref[...], flow_ref[...], NT) * jnp.exp(wide[TOK - 1 :, :] - wide)
    rest = carried + skip * dy.astype(f32)
    top = jnp.zeros((1, 1), f32)
    for j in range(SSM_HEADS // 2):
        cols = slice(128 * j, 128 * (j + 1))
        both = dy[:, cols]
        out = rest[:, cols]
        for k in range(2):
            h = 2 * j + k
            span = narrow[h : h + 1, :] - wide[:, h * SSM_DIM : h * SSM_DIM + 1]
            weight = jnp.where(col >= row, jnp.exp(jnp.minimum(span, 0.0)), 0.0)
            kept = jnp.where(col // SSM_DIM == k, both, jnp.zeros_like(both))
            out = out + dot((pairs * weight).astype(bf16), kept, NN)
        dx_ref[:, cols] = out
        top = jnp.maximum(top, jnp.max(jnp.abs(out), keepdims=True))
    peak_ref[...] = jnp.broadcast_to(top, peak_ref.shape)


def call(body, out_shape, *args, scratch=(), scalars=0, raw=0):
    specs = [pl.BlockSpec(memory_space=pltpu.SMEM)] * scalars
    specs += [pl.BlockSpec(memory_space=pltpu.VMEM)] * (len(args) - scalars - raw)
    specs += [pl.BlockSpec(memory_space=pl.ANY)] * raw
    return pl.pallas_call(
        body,
        out_shape=out_shape,
        in_specs=specs,
        out_specs=jax.tree.map(lambda _: pl.BlockSpec(memory_space=pltpu.VMEM), out_shape),
        scratch_shapes=scratch,
    )(*args)


def swap_all(x, axes):
    return lax.all_to_all(x, axes, 0, 0, tiled=True)


def along_z(x, step):
    route = []
    for chip in range(CHIPS):
        for core in range(2):
            move = step if step != 2 or core == 0 else -2
            route.append((2 * chip + core, 2 * ((chip + move) % CHIPS) + core))
    return lax.ppermute(x, SEQ, route)


def peak_kernel(far_ref, peak_q_ref, peak_x_ref, own_ref, out_ref):
    own = jnp.sum(far_ref[...].astype(f32), axis=0)
    own_ref[...] = own
    lane = lax.broadcasted_iota(jnp.int32, out_ref.shape, 1)
    peak_kv = jnp.max(jnp.abs(own), keepdims=True)
    out_ref[...] = jnp.where(lane == 0, peak_q_ref[:1], jnp.where(lane == 1, peak_kv, peak_x_ref[:1]))


def merge_kernel(peaks_ref, out_ref):
    out_ref[...] = jnp.broadcast_to(jnp.max(peaks_ref[...], axis=0, keepdims=True), out_ref.shape)


def scale_kernel(peaks_ref, dq_ref, dkv_ref, dx_ref, q_ref, kv_ref, x_ref):
    peaks = jnp.max(peaks_ref[...], axis=0, keepdims=True) + EPSILON
    q_ref[...] = (dq_ref[...] / peaks[:, 0:1]).astype(bf16)
    kv_ref[...] = (dkv_ref[...] / peaks[:, 1:2]).astype(bf16)
    x_ref[...] = (dx_ref[...] / peaks[:, 2:3]).astype(bf16)


def step(queries, key_value, grad_out, ssm_grad, b_proj, c_proj, decay_log, skip_gain):
    chip = lax.axis_index(("hi", "lo"))
    pos = jnp.stack([chip, lax.axis_index("c")]).astype(jnp.int32)
    struct = jax.ShapeDtypeStruct

    column = swap_all(jnp.tile(key_value, (8, 1)), ("hi", "xp"))
    two = along_z(column, 2)
    after = along_z(column, -1)
    before = along_z(column, 1)

    state = call(state_kernel, struct((2 * CHIPS, 24, 128), bf16), ssm_grad, c_proj, decay_log)
    states = swap_all(state, SEQ)
    flows = call(scan_kernel, struct((2 * CHIPS, 16, 128), bf16), states)
    flow = swap_all(flows, SEQ)

    pieces = []
    for piece in (column, after, two, before):
        pieces.append(lax.all_gather(piece, "c", axis=0, tiled=True).reshape(2, 4, 2, TOK, 128))
    dq, dkv, peak_q = call(
        attention_kernel,
        (struct((TOK, 512), f32), struct((2, 4, 4, 2, TOK, 128), bf16), struct((8, 128), f32)),
        pos,
        queries,
        grad_out,
        *pieces,
        scratch=(
            pltpu.VMEM((4, 2, 4, 2, TOK, 128), bf16),
            pltpu.VMEM((256 * CHIPS, 512), f32),
            pltpu.VMEM((256 * CHIPS, 512), f32),
            pltpu.VMEM((128, 512), f32),
            pltpu.VMEM((128, 512), f32),
            pltpu.SemaphoreType.DMA((4,)),
        ),
        scalars=1,
        raw=4,
    )

    both = swap_all(dkv.reshape(2 * 4096, 128), "c").reshape(2, 4, 1024, 128).astype(f32)
    chip_sum = (both[0] + both[1]).astype(bf16)
    from_two = along_z(chip_sum[2], 2)
    from_before = along_z(chip_sum[1], 1)
    from_after = along_z(chip_sum[3], -1)
    near = (
        (chip_sum[0].astype(f32) + from_before.astype(f32)) + (from_after.astype(f32) + from_two.astype(f32))
    ).astype(bf16)
    far = swap_all(near, ("hi", "xp")).reshape(8, TOK, 128)
    dx, peak_x = call(
        ssm_kernel,
        (struct((TOK, 512), f32), struct((8, 128), f32)),
        ssm_grad,
        b_proj,
        c_proj,
        decay_log,
        skip_gain.reshape(SSM_HEADS, 1),
        flow.reshape(512, 128),
    )

    dkv_own, peaks = call(peak_kernel, (struct((TOK, 128), f32), struct((32, 128), f32)), far, peak_q, peak_x)
    peaks = swap_all(peaks, SEQ)
    peaks = call(merge_kernel, struct((16, 128), f32), peaks)
    peaks = swap_all(peaks, HEAD)
    return call(
        scale_kernel,
        (struct((TOK, 512), bf16), struct((TOK, 128), bf16), struct((TOK, 512), bf16)),
        peaks,
        dq,
        dkv_own,
        dx,
    )


def solution(mesh):
    finer = Mesh(mesh.devices.reshape(SIZES), SEQ + HEAD)
    tokens = P(SEQ, HEAD)
    return jax.shard_map(
        step,
        mesh=finer,
        in_specs=(tokens, tokens, tokens, tokens, P(SEQ, None), P(SEQ, None), P(HEAD, SEQ), P(HEAD)),
        out_specs=(tokens, tokens, tokens),
        check_vma=False,
    )
```

profile of v0, /device:TPU:1, one launch (start us, length us, event | category | flops | bytes accessed | tf_op | source)
XLA Modules:
  0.0 196.0 jit_solution(13297886339973800417)
XLA Ops:
  0.6 0.8 tile.2
  1.4 30.4 %all_to_all.59 = bf16[8,128,128]{2,1,0:T(8,128)(2,1)S(1)} all-to-all(bf16[8,128,128]{2,1,0:T(8,128)(2,1)S(1)} %tile.2), channel_id=1, replica_groups=mesh['hi'=4,'lo'=4,'c'=2,'y'=4,'xh'=2,'xp'=2] {'hi','xp'}, dimensions={0} | all-to-all | bytes 524288 | tf_op jit(solution)/shard_map/all_to_all | solution.py:201
  31.9 4.5 %collective-permute-start = (bf16[1024,128]{1,0:T(8,128)(2,1)S(1)}, bf16[1024,128]{1,0:T(8,128)(2,1)S(1)}, u32[]{:S(2)}, u32[]{:S(2)}) collective-permute-start(bf16[1024,128]{1,0:T(8,128)(2,1)S(1)} %bitcast.38), channel_id=1, source_target_pairs={{0,480},{16,496},{32,0},{48,16},{64,32},{80,48},{96,64},{112,80},{... | collective-permute-start | bytes 786440 | tf_op jit(solution)/shard_map/ppermute | solution.py:210
  36.4 2.6 %shard_map.104 = bf16[32,24,128]{2,1,0:T(8,128)(2,1)} custom-call(bf16[128,512]{1,0:T(8,128)(2,1)} %dy_ref.3, bf16[128,128]{1,0:T(8,128)(2,1)} %c_ref.3, f32[8,128]{1,0:T(8,128)} %decay_ref.3), custom_call_target="tpu_custom_call" | custom-call | tf_op jit(solution)/shard_map/pallas_call | solution.py:191
  39.0 0.6 pad_add_fusion.pos_ref
  39.6 6.2 %collective-permute-start.1 = (bf16[1024,128]{1,0:T(8,128)(2,1)S(1)}, bf16[1024,128]{1,0:T(8,128)(2,1)S(1)}, u32[]{:S(2)}, u32[]{:S(2)}) collective-permute-start(bf16[1024,128]{1,0:T(8,128)(2,1)S(1)} %bitcast.39), channel_id=1, source_target_pairs={{0,64},{16,464},{32,96},{48,496},{64,128},{80,16},{96,160},{112,48... | collective-permute-start | bytes 786440 | tf_op jit(solution)/shard_map/ppermute | solution.py:210
  45.7 3.4 %collective-permute-start.2 = (bf16[1024,128]{1,0:T(8,128)(2,1)S(1)}, bf16[1024,128]{1,0:T(8,128)(2,1)S(1)}, u32[]{:S(2)}, u32[]{:S(2)}) collective-permute-start(bf16[1024,128]{1,0:T(8,128)(2,1)S(1)} %bitcast.40), channel_id=1, source_target_pairs={{0,32},{16,48},{32,64},{48,80},{64,96},{80,112},{96,128},{112,144}... | collective-permute-start | bytes 786440 | tf_op jit(solution)/shard_map/ppermute | solution.py:210
  49.1 4.9 %all_gather.12 = bf16[2048,128]{1,0:T(8,128)(2,1)} all-gather(bf16[1024,128]{1,0:T(8,128)(2,1)S(1)} %bitcast.41), channel_id=1, replica_groups=mesh['hi'=4,'lo'=4,'c'=2,'y'=4,'xh'=2,'xp'=2] {'c'}, dimensions={0}, use_global_device_ids=true | all-gather | bytes 786432 | tf_op jit(solution)/shard_map/all_gather | solution.py:249
  54.0 0.0 collective-permute-done
  54.0 2.3 %all_gather.13 = bf16[2048,128]{1,0:T(8,128)(2,1)} all-gather(bf16[1024,128]{1,0:T(8,128)(2,1)S(1)} %collective-permute-done), channel_id=1, replica_groups=mesh['hi'=4,'lo'=4,'c'=2,'y'=4,'xh'=2,'xp'=2] {'c'}, dimensions={0}, use_global_device_ids=true | all-gather | bytes 786432 | tf_op jit(solution)/shard_map/all_gather | solution.py:249
  56.3 0.0 collective-permute-done.1
  56.3 4.8 %all_gather.14 = bf16[2048,128]{1,0:T(8,128)(2,1)} all-gather(bf16[1024,128]{1,0:T(8,128)(2,1)S(1)} %collective-permute-done.1), channel_id=1, replica_groups=mesh['hi'=4,'lo'=4,'c'=2,'y'=4,'xh'=2,'xp'=2] {'c'}, dimensions={0}, use_global_device_ids=true | all-gather | bytes 786432 | tf_op jit(solution)/shard_map/all_gather | solution.py:249
  61.1 0.0 collective-permute-done.2
  61.1 3.9 %all_gather.15 = bf16[2048,128]{1,0:T(8,128)(2,1)} all-gather(bf16[1024,128]{1,0:T(8,128)(2,1)S(1)} %collective-permute-done.2), channel_id=1, replica_groups=mesh['hi'=4,'lo'=4,'c'=2,'y'=4,'xh'=2,'xp'=2] {'c'}, dimensions={0}, use_global_device_ids=true | all-gather | bytes 786432 | tf_op jit(solution)/shard_map/all_gather | solution.py:249
  64.9 5.5 %shard_map.103 = (f32[128,512]{1,0:T(8,128)}, bf16[2,4,4,2,128,128]{5,4,3,2,1,0:T(8,128)(2,1)}, f32[8,128]{1,0:T(8,128)}) custom-call(s32[2]{0:T(128)} %pad_add_fusion.pos_ref, bf16[128,512]{1,0:T(8,128)(2,1)} %q_ref.1, bf16[128,512]{1,0:T(8,128)(2,1)} %do_ref.1, bf16[2,4,2,128,128]{4,3,2,1,0:T(8,128)(2,1)} %bitcast.33, ...), custom_call_target="tpu_custom_call" | custom-call | tf_op jit(solution)/shard_map/pallas_call | solution.py:191
  70.4 6.6 %all_to_all.60 = bf16[2,4096,128]{2,1,0:T(8,128)(2,1)S(1)} all-to-all(bf16[2,4096,128]{2,1,0:T(8,128)(2,1)} %bitcast.37), channel_id=1, replica_groups=mesh['hi'=4,'lo'=4,'c'=2,'y'=4,'xh'=2,'xp'=2] {'c'}, dimensions={0} | all-to-all | bytes 4194304 | tf_op jit(solution)/shard_map/all_to_all | solution.py:201
  77.0 16.1 %all-to-all-start.3 = ((bf16[32,24,128]{2,1,0:T(8,128)(2,1)}), bf16[32,24,128]{2,1,0:T(8,128)(2,1)S(1)}, u32[]{:S(2)}, u32[]{:S(2)}) async-start(bf16[32,24,128]{2,1,0:T(8,128)(2,1)} %shard_map.104), calls=%async_computation.3 | async-start | bytes 393216 | tf_op jit(solution)/shard_map/all_to_all | solution.py:201
  93.1 0.3 convert_element_type.30
  93.4 0.2 fusion
  93.6 0.0 copy-start.3
  93.6 0.1 slice_bitcast_fusion.2
  93.7 3.3 %collective-permute-start.3 = (bf16[1024,128]{1,0:T(8,128)(2,1)S(1)}, bf16[1024,128]{1,0:T(8,128)(2,1)S(1)}, u32[]{:S(2)}, u32[]{:S(2)}) collective-permute-start(bf16[1024,128]{1,0:T(8,128)(2,1)S(1)} %get-tuple-element.17), channel_id=1, source_target_pairs={{0,32},{16,48},{32,64},{48,80},{64,96},{80,112},{96,128},{112,144}... | collective-permute-start | bytes 786440 | tf_op jit(solution)/shard_map/ppermute | solution.py:210
  96.9 3.2 %collective-permute-start.4 = (bf16[1024,128]{1,0:T(8,128)(2,1)S(1)}, bf16[1024,128]{1,0:T(8,128)(2,1)S(1)}, u32[]{:S(2)}, u32[]{:S(2)}) collective-permute-start(bf16[1024,128]{1,0:T(8,128)(2,1)S(1)} %get-tuple-element.19), channel_id=1, source_target_pairs={{0,480},{16,496},{32,0},{48,16},{64,32},{80,48},{96,64},{112,80},{... | collective-permute-start | bytes 786440 | tf_op jit(solution)/shard_map/ppermute | solution.py:210
  100.2 4.2 %collective-permute-start.5 = (bf16[1024,128]{1,0:T(8,128)(2,1)S(1)}, bf16[1024,128]{1,0:T(8,128)(2,1)S(1)}, u32[]{:S(2)}, u32[]{:S(2)}) collective-permute-start(bf16[1024,128]{1,0:T(8,128)(2,1)S(1)} %get-tuple-element.18), channel_id=1, source_target_pairs={{0,64},{16,464},{32,96},{48,496},{64,128},{80,16},{96,160},{112,48... | collective-permute-start | bytes 786440 | tf_op jit(solution)/shard_map/ppermute | solution.py:210
  104.4 7.5 %all-to-all-done.3.state_ref = bf16[32,24,128]{2,1,0:T(8,128)(2,1)S(1)} async-done(((bf16[32,24,128]{2,1,0:T(8,128)(2,1)}), bf16[32,24,128]{2,1,0:T(8,128)(2,1)S(1)}, u32[]{:S(2)}, u32[]{:S(2)}) %all-to-all-start.3) | async-done | bytes 196640 | tf_op jit(solution)/shard_map/all_to_all | solution.py:201
  111.9 0.0 copy-start.1
  111.9 0.7 copy-done.1
  112.6 1.7 shard_map.105
  114.2 5.2 %all-to-all-start.4 = ((bf16[32,16,128]{2,1,0:T(8,128)(2,1)}), bf16[32,16,128]{2,1,0:T(8,128)(2,1)S(1)}, u32[]{:S(2)}, u32[]{:S(2)}) async-start(bf16[32,16,128]{2,1,0:T(8,128)(2,1)} %shard_map.105), calls=%async_computation.4 | async-start | bytes 262144 | tf_op jit(solution)/shard_map/all_to_all | solution.py:201
  119.4 0.0 collective-permute-done.3
  119.4 0.0 collective-permute-done.4
  119.4 0.0 collective-permute-done.5
  119.4 0.8 fusion.2
  120.3 15.3 %all-to-all-done.4 = bf16[32,16,128]{2,1,0:T(8,128)(2,1)S(1)} async-done(((bf16[32,16,128]{2,1,0:T(8,128)(2,1)}), bf16[32,16,128]{2,1,0:T(8,128)(2,1)S(1)}, u32[]{:S(2)}, u32[]{:S(2)}) %all-to-all-start.4) | async-done | bytes 131104 | tf_op jit(solution)/shard_map/all_to_all | solution.py:201
  135.6 0.0 copy-start.2
  135.6 3.7 %all-to-all-start.2 = ((bf16[8,128,128]{2,1,0:T(8,128)(2,1)}), bf16[8,128,128]{2,1,0:T(8,128)(2,1)S(1)}, u32[]{:S(2)}, u32[]{:S(2)}) async-start(bf16[8,128,128]{2,1,0:T(8,128)(2,1)} %bitcast.13), calls=%async_computation.2 | async-start | bytes 524288 | tf_op jit(solution)/shard_map/all_to_all | solution.py:201
  139.3 0.0 copy-done.3
  139.3 0.7 copy.12.skip_ref
  140.0 0.0 copy-done.2
  140.0 2.9 %shard_map.106 = (f32[128,512]{1,0:T(8,128)}, f32[8,128]{1,0:T(8,128)}) custom-call(bf16[128,512]{1,0:T(8,128)(2,1)} %dy_ref.3, bf16[128,128]{1,0:T(8,128)(2,1)} %b_ref.1, bf16[128,128]{1,0:T(8,128)(2,1)} %c_ref.3, f32[8,128]{1,0:T(8,128)} %decay_ref.3, f32[8,1]{1,0:T(8,128)} %copy.12.skip_ref, bf16[512,128]{1,0:T(8,128)(2,1)} %bitcast.42), custom_call_target="tpu_custom_call" | custom-call | tf_op jit(solution)/shard_map/pallas_call | solution.py:191
  142.9 10.4 %all-to-all-done.2.far_ref = bf16[8,128,128]{2,1,0:T(8,128)(2,1)S(1)} async-done(((bf16[8,128,128]{2,1,0:T(8,128)(2,1)}), bf16[8,128,128]{2,1,0:T(8,128)(2,1)S(1)}, u32[]{:S(2)}, u32[]{:S(2)}) %all-to-all-start.2) | async-done | bytes 262176 | tf_op jit(solution)/shard_map/all_to_all | solution.py:201
  153.3 0.0 copy-start
  153.3 0.7 copy-done
  154.0 1.7 shard_map.107
  155.7 24.3 %all_to_all.61 = f32[32,1,128]{2,1,0:T(1,128)} all-to-all(f32[32,1,128]{2,1,0:T(1,128)} %bitcast.46), channel_id=1, replica_groups=mesh['hi'=4,'lo'=4,'c'=2,'y'=4,'xh'=2,'xp'=2] {'hi','lo','c'}, dimensions={0} | all-to-all | bytes 32768 | tf_op jit(solution)/shard_map/all_to_all | solution.py:201
  180.0 1.3 shard_map.108
  181.3 12.8 %all_to_all.62 = f32[16,1,128]{2,1,0:T(1,128)} all-to-all(f32[16,1,128]{2,1,0:T(1,128)} %bitcast.45), channel_id=1, replica_groups=mesh['hi'=4,'lo'=4,'c'=2,'y'=4,'xh'=2,'xp'=2] {'y','xh','xp'}, dimensions={0} | all-to-all | bytes 16384 | tf_op jit(solution)/shard_map/all_to_all | solution.py:201
  194.1 1.9 shard_map.109
Async XLA Ops:
  31.9 22.1 %collective-permute-start = (bf16[1024,128]{1,0:T(8,128)(2,1)S(1)}, bf16[1024,128]{1,0:T(8,128)(2,1)S(1)}, u32[]{:S(2)}, u32[]{:S(2)}) collective-permute-start(bf16[1024,128]{1,0:T(8,128)(2,1)S(1)} %bitcast.38), channel_id=1, source_target_pairs={{0,480},{16,496},{32,0},{48,16},{64,32},{80,48},{96,64},{112,80},{... | collective-permute-start | bytes 786440 | tf_op jit(solution)/shard_map/ppermute | solution.py:210
  39.6 16.7 %collective-permute-start.1 = (bf16[1024,128]{1,0:T(8,128)(2,1)S(1)}, bf16[1024,128]{1,0:T(8,128)(2,1)S(1)}, u32[]{:S(2)}, u32[]{:S(2)}) collective-permute-start(bf16[1024,128]{1,0:T(8,128)(2,1)S(1)} %bitcast.39), channel_id=1, source_target_pairs={{0,64},{16,464},{32,96},{48,496},{64,128},{80,16},{96,160},{112,48... | collective-permute-start | bytes 786440 | tf_op jit(solution)/shard_map/ppermute | solution.py:210
  45.7 15.4 %collective-permute-start.2 = (bf16[1024,128]{1,0:T(8,128)(2,1)S(1)}, bf16[1024,128]{1,0:T(8,128)(2,1)S(1)}, u32[]{:S(2)}, u32[]{:S(2)}) collective-permute-start(bf16[1024,128]{1,0:T(8,128)(2,1)S(1)} %bitcast.40), channel_id=1, source_target_pairs={{0,32},{16,48},{32,64},{48,80},{64,96},{80,112},{96,128},{112,144}... | collective-permute-start | bytes 786440 | tf_op jit(solution)/shard_map/ppermute | solution.py:210
  77.0 34.8 %all-to-all-start.3 = ((bf16[32,24,128]{2,1,0:T(8,128)(2,1)}), bf16[32,24,128]{2,1,0:T(8,128)(2,1)S(1)}, u32[]{:S(2)}, u32[]{:S(2)}) async-start(bf16[32,24,128]{2,1,0:T(8,128)(2,1)} %shard_map.104), calls=%async_computation.3 | async-start | bytes 393216 | tf_op jit(solution)/shard_map/all_to_all | solution.py:201
  93.6 45.7 %copy-start.3 = (f32[8]{0:T(128)S(1)}, f32[8]{0:T(128)}, u32[]{:S(2)}) copy-start(f32[8]{0:T(128)} %param.15) | copy-start | bytes 100
  93.7 25.7 %collective-permute-start.3 = (bf16[1024,128]{1,0:T(8,128)(2,1)S(1)}, bf16[1024,128]{1,0:T(8,128)(2,1)S(1)}, u32[]{:S(2)}, u32[]{:S(2)}) collective-permute-start(bf16[1024,128]{1,0:T(8,128)(2,1)S(1)} %get-tuple-element.17), channel_id=1, source_target_pairs={{0,32},{16,48},{32,64},{48,80},{64,96},{80,112},{96,128},{112,144}... | collective-permute-start | bytes 786440 | tf_op jit(solution)/shard_map/ppermute | solution.py:210
  96.9 22.5 %collective-permute-start.4 = (bf16[1024,128]{1,0:T(8,128)(2,1)S(1)}, bf16[1024,128]{1,0:T(8,128)(2,1)S(1)}, u32[]{:S(2)}, u32[]{:S(2)}) collective-permute-start(bf16[1024,128]{1,0:T(8,128)(2,1)S(1)} %get-tuple-element.19), channel_id=1, source_target_pairs={{0,480},{16,496},{32,0},{48,16},{64,32},{80,48},{96,64},{112,80},{... | collective-permute-start | bytes 786440 | tf_op jit(solution)/shard_map/ppermute | solution.py:210
  100.2 19.2 %collective-permute-start.5 = (bf16[1024,128]{1,0:T(8,128)(2,1)S(1)}, bf16[1024,128]{1,0:T(8,128)(2,1)S(1)}, u32[]{:S(2)}, u32[]{:S(2)}) collective-permute-start(bf16[1024,128]{1,0:T(8,128)(2,1)S(1)} %get-tuple-element.18), channel_id=1, source_target_pairs={{0,64},{16,464},{32,96},{48,496},{64,128},{80,16},{96,160},{112,48... | collective-permute-start | bytes 786440 | tf_op jit(solution)/shard_map/ppermute | solution.py:210
  111.9 0.7 copy-start.1
  114.2 21.4 %all-to-all-start.4 = ((bf16[32,16,128]{2,1,0:T(8,128)(2,1)}), bf16[32,16,128]{2,1,0:T(8,128)(2,1)S(1)}, u32[]{:S(2)}, u32[]{:S(2)}) async-start(bf16[32,16,128]{2,1,0:T(8,128)(2,1)} %shard_map.105), calls=%async_computation.4 | async-start | bytes 262144 | tf_op jit(solution)/shard_map/all_to_all | solution.py:201
  135.6 4.4 %copy-start.2 = (bf16[32,16,128]{2,1,0:T(8,128)(2,1)}, bf16[32,16,128]{2,1,0:T(8,128)(2,1)S(1)}, u32[]{:S(2)}) copy-start(bf16[32,16,128]{2,1,0:T(8,128)(2,1)S(1)} %all-to-all-done.4) | copy-start | bytes 393220
  135.6 17.7 %all-to-all-start.2 = ((bf16[8,128,128]{2,1,0:T(8,128)(2,1)}), bf16[8,128,128]{2,1,0:T(8,128)(2,1)S(1)}, u32[]{:S(2)}, u32[]{:S(2)}) async-start(bf16[8,128,128]{2,1,0:T(8,128)(2,1)} %bitcast.13), calls=%async_computation.2 | async-start | bytes 524288 | tf_op jit(solution)/shard_map/all_to_all | solution.py:201
  153.3 0.7 copy-start
where the time goes:
time: 197 us; the launch traced here: 196 us
  blocking collectives  90 us (46%)
  starting transfers between devices  49.7 us (25%)
  waiting for transfers between devices  33.2 us (17%)
  Pallas kernels  17.5 us (9%)
  local copies, waits for them, and re-layouts  2.89 us (1%)
    all_to_all x4, blocking collectives, swap_all(): return lax.all_to_all(x, axes, 0, 0, tiled=True)  74.2 us
    all_to_all x3, waiting for transfers between devices, swap_all(): return lax.all_to_all(x, axes, 0, 0, tiled=True)  33.2 us
    all_to_all x3, starting transfers between devices, swap_all(): return lax.all_to_all(x, axes, 0, 0, tiled=True)  24.9 us
    ppermute x6, starting transfers between devices, along_z(): return lax.ppermute(x, SEQ, route)  24.8 us
    pallas_call x7, Pallas kernels, call(): pl.pallas_call(body, out_shape=out_shape, in_specs=specs, out_specs=jax.t...  17.5 us
    all_gather x4, blocking collectives, step(): lax.all_gather(piece, 'c', axis=0, tiled=True).reshape(2, 4, 2, TOK, 128)  15.8 us
  transfers between devices with their start and end apart: 9, of which 3 were waited for; matrix products, arithmetic and copies ran while one was open for 1% of the time, Pallas kernels for 4%

commit v1 on v0

--- a/solution.py
+++ b/solution.py
@@ -47,74 +47,77 @@
     do = heads_to_rows(do_ref[...])
     width = q.shape[0]
 
+    steps = chip // 2 + 1
+
     def place(z):
         return lax.rem(lax.rem(z, 4) - lane_group + 4, 4), z // 4
 
-    def rows_at(z):
-        return pl.ds(pl.multiple_of(z * 2 * TOK, 2 * TOK), 2 * TOK)
-
-    def both_cores(z, part):
-        rel, hi = place(z)
-        return jnp.concatenate([kv_ref[rel, 0, hi, part], kv_ref[rel, 1, hi, part]], axis=0)
+    def tiles(j):
+        for z in (2 * j, 2 * j + 1):
+            rel, hi = place(z)
+            for c in range(2):
+                yield rel, c, hi
+
+    def rows_at(j):
+        return pl.ds(pl.multiple_of(j * 4 * TOK, 4 * TOK), 4 * TOK)
+
+    def keys_at(j, part):
+        return jnp.concatenate([kv_ref[rel, c, hi, part] for rel, c, hi in tiles(j)], axis=0)
+
+    def store_at(j, part, x):
+        for k, (rel, c, hi) in enumerate(tiles(j)):
+            dkv_ref[c, rel, hi, part] = x[TOK * k : TOK * (k + 1)]
 
     def partial_rows(x, op):
-        return op(x.reshape(2 * TOK // 8, 8, width), axis=0)
-
-    def score_step(z, carry, masked):
+        return op(x.reshape(4 * TOK // 8, 8, width), axis=0)
+
+    def score_step(j, carry, masked):
         old, total = carry
-        s = dot(both_cores(z, 0), q, NT) * SCALE
+        s = dot(keys_at(j, 0), q, NT) * SCALE
         if masked:
-            key = lax.broadcasted_iota(jnp.int32, s.shape, 0)
-            query = lax.rem(lax.broadcasted_iota(jnp.int32, s.shape, 1), TOK) + core * TOK
+            key = lax.broadcasted_iota(jnp.int32, s.shape, 0) + j * 4 * TOK
+            query = lax.rem(lax.broadcasted_iota(jnp.int32, s.shape, 1), TOK) + (2 * chip + core) * TOK
             s = jnp.where(key <= query, s, -1e30)
         top = jnp.maximum(old, jnp.max(partial_rows(s, jnp.max), axis=0, keepdims=True))
-        p_ref[rows_at(z), :] = s
+        p_ref[rows_at(j), :] = s
         return top, total * jnp.exp(old - top) + partial_rows(jnp.exp(s - top), jnp.sum)
 
     for copy in copies:
         copy.wait()
-    carry = score_step(chip, (jnp.full((1, width), -1e30, f32), jnp.zeros((8, width), f32)), True)
-    top, total = lax.fori_loop(0, chip, lambda z, c: score_step(z, c, False), carry)
+    carry = score_step(steps - 1, (jnp.full((1, width), -1e30, f32), jnp.zeros((8, width), f32)), True)
+    top, total = lax.fori_loop(0, steps - 1, lambda j, c: score_step(j, c, False), carry)
     lse = top + jnp.log(jnp.sum(total, axis=0, keepdims=True))
     outt_ref[...] = jnp.zeros_like(outt_ref)
     dqt_ref[...] = jnp.zeros_like(dqt_ref)
 
-    def output_step(z, _):
-        rel, hi = place(z)
-        p = jnp.exp(p_ref[rows_at(z), :] - lse)
-        p_ref[rows_at(z), :] = p
+    def output_step(j, _):
+        p = jnp.exp(p_ref[rows_at(j), :] - lse)
+        p_ref[rows_at(j), :] = p
         p_b = p.astype(bf16)
-        values = both_cores(z, 1)
+        values = keys_at(j, 1)
         outt_ref[...] += dot(values, p_b, TN)
-        dp_ref[rows_at(z), :] = dot(values, do, NT)
-        dv = dot(p_b, do, NN).astype(bf16)
-        dkv_ref[0, rel, hi, 1] = dv[:TOK]
-        dkv_ref[1, rel, hi, 1] = dv[TOK:]
+        dp_ref[rows_at(j), :] = dot(values, do, NT)
+        store_at(j, 1, dot(p_b, do, NN).astype(bf16))
         return 0
 
-    lax.fori_loop(0, chip + 1, output_step, 0)
+    lax.fori_loop(0, steps, output_step, 0)
     dot_rows = jnp.concatenate([do_ref[:, 128 * h : 128 * (h + 1)].astype(f32).T for h in range(4)], axis=1)
     delta = jnp.sum(dot_rows * outt_ref[...].astype(bf16).astype(f32), axis=0, keepdims=True)
 
-    def gradient_step(z, _):
-        rel, hi = place(z)
-        ds = (p_ref[rows_at(z), :] * (dp_ref[rows_at(z), :] - delta)).astype(bf16)
-        dk = (dot(ds, q, NN) * SCALE).astype(bf16)
-        dkv_ref[0, rel, hi, 0] = dk[:TOK]
-        dkv_ref[1, rel, hi, 0] = dk[TOK:]
-        dqt_ref[...] += dot(both_cores(z, 0), ds, TN)
+    def gradient_step(j, _):
+        ds = (p_ref[rows_at(j), :] * (dp_ref[rows_at(j), :] - delta)).astype(bf16)
+        store_at(j, 0, (dot(ds, q, NN) * SCALE).astype(bf16))
+        dqt_ref[...] += dot(keys_at(j, 0), ds, TN)
         return 0
 
-    lax.fori_loop(0, chip + 1, gradient_step, 0)
-
-    def clear_step(z, _):
-        rel, hi = place(z)
-        for c in range(2):
-            for part in range(2):
-                dkv_ref[c, rel, hi, part] = jnp.zeros((TOK, 128), bf16)
+    lax.fori_loop(0, steps, gradient_step, 0)
+
+    def clear_step(j, _):
+        for part in range(2):
+            store_at(j, part, jnp.zeros((4 * TOK, 128), bf16))
         return 0
 
-    lax.fori_loop(chip + 1, CHIPS, clear_step, 0)
+    lax.fori_loop(steps, CHIPS // 2, clear_step, 0)
     dqt = dqt_ref[...] * SCALE
     for h in range(4):
         dq_ref[:, 128 * h : 128 * (h + 1)] = dqt[:, TOK * h : TOK * (h + 1)].T

time: 197 us -> 193 us (0.980)
  starting transfers between devices: 49.7 us -> 45 us
    all_to_all x3, starting transfers between devices: 24.9 us -> 20.3 us  [swap_all(): return lax.all_to_all(x, axes, 0, 0, tiled=True)]
where the time goes in v1:
time: 193 us; the launch traced here: 192 us
  blocking collectives  90.3 us (47%)
  starting transfers between devices  45 us (23%)
  waiting for transfers between devices  32.9 us (17%)
  Pallas kernels  17.9 us (9%)
  local copies, waits for them, and re-layouts  2.89 us (1%)
    all_to_all x4, blocking collectives, swap_all(): return lax.all_to_all(x, axes, 0, 0, tiled=True)  74.5 us
    all_to_all x3, waiting for transfers between devices, swap_all(): return lax.all_to_all(x, axes, 0, 0, tiled=True)  32.9 us
    ppermute x6, starting transfers between devices, along_z(): return lax.ppermute(x, SEQ, route)  24.8 us
    all_to_all x3, starting transfers between devices, swap_all(): return lax.all_to_all(x, axes, 0, 0, tiled=True)  20.3 us
    pallas_call x7, Pallas kernels, call(): pl.pallas_call(body, out_shape=out_shape, in_specs=specs, out_specs=jax.t...  17.9 us
    all_gather x4, blocking collectives, step(): lax.all_gather(piece, 'c', axis=0, tiled=True).reshape(2, 4, 2, TOK, 128)  15.8 us
  transfers between devices with their start and end apart: 9, of which 3 were waited for; matrix products, arithmetic and copies ran while one was open for 1% of the time, Pallas kernels for 4%

profile of v1, /device:TPU:1, one launch (start us, length us, event | category | flops | bytes accessed | tf_op | source)
XLA Modules:
  0.0 191.8 jit_solution(467212791475477181)
XLA Ops:
  0.6 0.8 tile.2
  1.4 30.4 %all_to_all.59 = bf16[8,128,128]{2,1,0:T(8,128)(2,1)S(1)} all-to-all(bf16[8,128,128]{2,1,0:T(8,128)(2,1)S(1)} %tile.2), channel_id=1, replica_groups=mesh['hi'=4,'lo'=4,'c'=2,'y'=4,'xh'=2,'xp'=2] {'hi','xp'}, dimensions={0} | all-to-all | bytes 524288 | tf_op jit(solution)/shard_map/all_to_all | solution.py:204
  31.9 4.5 %collective-permute-start = (bf16[1024,128]{1,0:T(8,128)(2,1)S(1)}, bf16[1024,128]{1,0:T(8,128)(2,1)S(1)}, u32[]{:S(2)}, u32[]{:S(2)}) collective-permute-start(bf16[1024,128]{1,0:T(8,128)(2,1)S(1)} %bitcast.38), channel_id=1, source_target_pairs={{0,480},{16,496},{32,0},{48,16},{64,32},{80,48},{96,64},{112,80},{... | collective-permute-start | bytes 786440 | tf_op jit(solution)/shard_map/ppermute | solution.py:213
  36.4 2.6 %shard_map.104 = bf16[32,24,128]{2,1,0:T(8,128)(2,1)} custom-call(bf16[128,512]{1,0:T(8,128)(2,1)} %dy_ref.3, bf16[128,128]{1,0:T(8,128)(2,1)} %c_ref.3, f32[8,128]{1,0:T(8,128)} %decay_ref.3), custom_call_target="tpu_custom_call" | custom-call | tf_op jit(solution)/shard_map/pallas_call | solution.py:194
  39.0 0.6 pad_add_fusion.pos_ref
  39.6 6.2 %collective-permute-start.1 = (bf16[1024,128]{1,0:T(8,128)(2,1)S(1)}, bf16[1024,128]{1,0:T(8,128)(2,1)S(1)}, u32[]{:S(2)}, u32[]{:S(2)}) collective-permute-start(bf16[1024,128]{1,0:T(8,128)(2,1)S(1)} %bitcast.39), channel_id=1, source_target_pairs={{0,64},{16,464},{32,96},{48,496},{64,128},{80,16},{96,160},{112,48... | collective-permute-start | bytes 786440 | tf_op jit(solution)/shard_map/ppermute | solution.py:213
  45.7 3.4 %collective-permute-start.2 = (bf16[1024,128]{1,0:T(8,128)(2,1)S(1)}, bf16[1024,128]{1,0:T(8,128)(2,1)S(1)}, u32[]{:S(2)}, u32[]{:S(2)}) collective-permute-start(bf16[1024,128]{1,0:T(8,128)(2,1)S(1)} %bitcast.40), channel_id=1, source_target_pairs={{0,32},{16,48},{32,64},{48,80},{64,96},{80,112},{96,128},{112,144}... | collective-permute-start | bytes 786440 | tf_op jit(solution)/shard_map/ppermute | solution.py:213
  49.1 4.9 %all_gather.12 = bf16[2048,128]{1,0:T(8,128)(2,1)} all-gather(bf16[1024,128]{1,0:T(8,128)(2,1)S(1)} %bitcast.41), channel_id=1, replica_groups=mesh['hi'=4,'lo'=4,'c'=2,'y'=4,'xh'=2,'xp'=2] {'c'}, dimensions={0}, use_global_device_ids=true | all-gather | bytes 786432 | tf_op jit(solution)/shard_map/all_gather | solution.py:252
  54.0 0.0 collective-permute-done
  54.0 2.3 %all_gather.13 = bf16[2048,128]{1,0:T(8,128)(2,1)} all-gather(bf16[1024,128]{1,0:T(8,128)(2,1)S(1)} %collective-permute-done), channel_id=1, replica_groups=mesh['hi'=4,'lo'=4,'c'=2,'y'=4,'xh'=2,'xp'=2] {'c'}, dimensions={0}, use_global_device_ids=true | all-gather | bytes 786432 | tf_op jit(solution)/shard_map/all_gather | solution.py:252
  56.3 0.0 collective-permute-done.1
  56.3 4.8 %all_gather.14 = bf16[2048,128]{1,0:T(8,128)(2,1)} all-gather(bf16[1024,128]{1,0:T(8,128)(2,1)S(1)} %collective-permute-done.1), channel_id=1, replica_groups=mesh['hi'=4,'lo'=4,'c'=2,'y'=4,'xh'=2,'xp'=2] {'c'}, dimensions={0}, use_global_device_ids=true | all-gather | bytes 786432 | tf_op jit(solution)/shard_map/all_gather | solution.py:252
  61.1 0.0 collective-permute-done.2
  61.1 3.9 %all_gather.15 = bf16[2048,128]{1,0:T(8,128)(2,1)} all-gather(bf16[1024,128]{1,0:T(8,128)(2,1)S(1)} %collective-permute-done.2), channel_id=1, replica_groups=mesh['hi'=4,'lo'=4,'c'=2,'y'=4,'xh'=2,'xp'=2] {'c'}, dimensions={0}, use_global_device_ids=true | all-gather | bytes 786432 | tf_op jit(solution)/shard_map/all_gather | solution.py:252
  64.9 5.9 %shard_map.103 = (f32[128,512]{1,0:T(8,128)}, bf16[2,4,4,2,128,128]{5,4,3,2,1,0:T(8,128)(2,1)}, f32[8,128]{1,0:T(8,128)}) custom-call(s32[2]{0:T(128)} %pad_add_fusion.pos_ref, bf16[128,512]{1,0:T(8,128)(2,1)} %q_ref.1, bf16[128,512]{1,0:T(8,128)(2,1)} %do_ref.1, bf16[2,4,2,128,128]{4,3,2,1,0:T(8,128)(2,1)} %bitcast.33, ...), custom_call_target="tpu_custom_call" | custom-call | tf_op jit(solution)/shard_map/pallas_call | solution.py:194
  70.8 6.6 %all_to_all.60 = bf16[2,4096,128]{2,1,0:T(8,128)(2,1)S(1)} all-to-all(bf16[2,4096,128]{2,1,0:T(8,128)(2,1)} %bitcast.37), channel_id=1, replica_groups=mesh['hi'=4,'lo'=4,'c'=2,'y'=4,'xh'=2,'xp'=2] {'c'}, dimensions={0} | all-to-all | bytes 4194304 | tf_op jit(solution)/shard_map/all_to_all | solution.py:204
  77.5 11.4 %all-to-all-start.3 = ((bf16[32,24,128]{2,1,0:T(8,128)(2,1)}), bf16[32,24,128]{2,1,0:T(8,128)(2,1)S(1)}, u32[]{:S(2)}, u32[]{:S(2)}) async-start(bf16[32,24,128]{2,1,0:T(8,128)(2,1)} %shard_map.104), calls=%async_computation.3 | async-start | bytes 393216 | tf_op jit(solution)/shard_map/all_to_all | solution.py:204
  88.9 0.3 convert_element_type.30
  89.2 0.2 fusion
  89.4 0.0 copy-start.3
  89.4 0.1 slice_bitcast_fusion.2
  89.5 3.3 %collective-permute-start.3 = (bf16[1024,128]{1,0:T(8,128)(2,1)S(1)}, bf16[1024,128]{1,0:T(8,128)(2,1)S(1)}, u32[]{:S(2)}, u32[]{:S(2)}) collective-permute-start(bf16[1024,128]{1,0:T(8,128)(2,1)S(1)} %get-tuple-element.17), channel_id=1, source_target_pairs={{0,32},{16,48},{32,64},{48,80},{64,96},{80,112},{96,128},{112,144}... | collective-permute-start | bytes 786440 | tf_op jit(solution)/shard_map/ppermute | solution.py:213
  92.7 3.2 %collective-permute-start.4 = (bf16[1024,128]{1,0:T(8,128)(2,1)S(1)}, bf16[1024,128]{1,0:T(8,128)(2,1)S(1)}, u32[]{:S(2)}, u32[]{:S(2)}) collective-permute-start(bf16[1024,128]{1,0:T(8,128)(2,1)S(1)} %get-tuple-element.19), channel_id=1, source_target_pairs={{0,480},{16,496},{32,0},{48,16},{64,32},{80,48},{96,64},{112,80},{... | collective-permute-start | bytes 786440 | tf_op jit(solution)/shard_map/ppermute | solution.py:213
  96.0 4.2 %collective-permute-start.5 = (bf16[1024,128]{1,0:T(8,128)(2,1)S(1)}, bf16[1024,128]{1,0:T(8,128)(2,1)S(1)}, u32[]{:S(2)}, u32[]{:S(2)}) collective-permute-start(bf16[1024,128]{1,0:T(8,128)(2,1)S(1)} %get-tuple-element.18), channel_id=1, source_target_pairs={{0,64},{16,464},{32,96},{48,496},{64,128},{80,16},{96,160},{112,48... | collective-permute-start | bytes 786440 | tf_op jit(solution)/shard_map/ppermute | solution.py:213
  100.2 7.5 %all-to-all-done.3.state_ref = bf16[32,24,128]{2,1,0:T(8,128)(2,1)S(1)} async-done(((bf16[32,24,128]{2,1,0:T(8,128)(2,1)}), bf16[32,24,128]{2,1,0:T(8,128)(2,1)S(1)}, u32[]{:S(2)}, u32[]{:S(2)}) %all-to-all-start.3) | async-done | bytes 196640 | tf_op jit(solution)/shard_map/all_to_all | solution.py:204
  107.7 0.0 copy-start.1
  107.7 0.7 copy-done.1
  108.4 1.7 shard_map.105
  110.0 5.2 %all-to-all-start.4 = ((bf16[32,16,128]{2,1,0:T(8,128)(2,1)}), bf16[32,16,128]{2,1,0:T(8,128)(2,1)S(1)}, u32[]{:S(2)}, u32[]{:S(2)}) async-start(bf16[32,16,128]{2,1,0:T(8,128)(2,1)} %shard_map.105), calls=%async_computation.4 | async-start | bytes 262144 | tf_op jit(solution)/shard_map/all_to_all | solution.py:204
  115.2 0.0 collective-permute-done.3
  115.2 0.0 collective-permute-done.4
  115.2 0.0 collective-permute-done.5
  115.2 0.8 fusion.2
  116.0 15.3 %all-to-all-done.4 = bf16[32,16,128]{2,1,0:T(8,128)(2,1)S(1)} async-done(((bf16[32,16,128]{2,1,0:T(8,128)(2,1)}), bf16[32,16,128]{2,1,0:T(8,128)(2,1)S(1)}, u32[]{:S(2)}, u32[]{:S(2)}) %all-to-all-start.4) | async-done | bytes 131104 | tf_op jit(solution)/shard_map/all_to_all | solution.py:204
  131.4 0.0 copy-start.2
  131.4 3.7 %all-to-all-start.2 = ((bf16[8,128,128]{2,1,0:T(8,128)(2,1)}), bf16[8,128,128]{2,1,0:T(8,128)(2,1)S(1)}, u32[]{:S(2)}, u32[]{:S(2)}) async-start(bf16[8,128,128]{2,1,0:T(8,128)(2,1)} %bitcast.13), calls=%async_computation.2 | async-start | bytes 524288 | tf_op jit(solution)/shard_map/all_to_all | solution.py:204
  135.1 0.0 copy-done.3
  135.1 0.7 copy.12.skip_ref
  135.8 0.0 copy-done.2
  135.8 2.9 %shard_map.106 = (f32[128,512]{1,0:T(8,128)}, f32[8,128]{1,0:T(8,128)}) custom-call(bf16[128,512]{1,0:T(8,128)(2,1)} %dy_ref.3, bf16[128,128]{1,0:T(8,128)(2,1)} %b_ref.1, bf16[128,128]{1,0:T(8,128)(2,1)} %c_ref.3, f32[8,128]{1,0:T(8,128)} %decay_ref.3, f32[8,1]{1,0:T(8,128)} %copy.12.skip_ref, bf16[512,128]{1,0:T(8,128)(2,1)} %bitcast.42), custom_call_target="tpu_custom_call" | custom-call | tf_op jit(solution)/shard_map/pallas_call | solution.py:194
  138.6 10.1 %all-to-all-done.2.far_ref = bf16[8,128,128]{2,1,0:T(8,128)(2,1)S(1)} async-done(((bf16[8,128,128]{2,1,0:T(8,128)(2,1)}), bf16[8,128,128]{2,1,0:T(8,128)(2,1)S(1)}, u32[]{:S(2)}, u32[]{:S(2)}) %all-to-all-start.2) | async-done | bytes 262176 | tf_op jit(solution)/shard_map/all_to_all | solution.py:204
  148.8 0.0 copy-start
  148.8 0.7 copy-done
  149.4 1.7 shard_map.107
  151.2 24.6 %all_to_all.61 = f32[32,1,128]{2,1,0:T(1,128)} all-to-all(f32[32,1,128]{2,1,0:T(1,128)} %bitcast.46), channel_id=1, replica_groups=mesh['hi'=4,'lo'=4,'c'=2,'y'=4,'xh'=2,'xp'=2] {'hi','lo','c'}, dimensions={0} | all-to-all | bytes 32768 | tf_op jit(solution)/shard_map/all_to_all | solution.py:204
  175.8 1.3 shard_map.108
  177.1 12.8 %all_to_all.62 = f32[16,1,128]{2,1,0:T(1,128)} all-to-all(f32[16,1,128]{2,1,0:T(1,128)} %bitcast.45), channel_id=1, replica_groups=mesh['hi'=4,'lo'=4,'c'=2,'y'=4,'xh'=2,'xp'=2] {'y','xh','xp'}, dimensions={0} | all-to-all | bytes 16384 | tf_op jit(solution)/shard_map/all_to_all | solution.py:204
  189.9 1.9 shard_map.109
Async XLA Ops:
  31.9 22.1 %collective-permute-start = (bf16[1024,128]{1,0:T(8,128)(2,1)S(1)}, bf16[1024,128]{1,0:T(8,128)(2,1)S(1)}, u32[]{:S(2)}, u32[]{:S(2)}) collective-permute-start(bf16[1024,128]{1,0:T(8,128)(2,1)S(1)} %bitcast.38), channel_id=1, source_target_pairs={{0,480},{16,496},{32,0},{48,16},{64,32},{80,48},{96,64},{112,80},{... | collective-permute-start | bytes 786440 | tf_op jit(solution)/shard_map/ppermute | solution.py:213
  39.6 16.7 %collective-permute-start.1 = (bf16[1024,128]{1,0:T(8,128)(2,1)S(1)}, bf16[1024,128]{1,0:T(8,128)(2,1)S(1)}, u32[]{:S(2)}, u32[]{:S(2)}) collective-permute-start(bf16[1024,128]{1,0:T(8,128)(2,1)S(1)} %bitcast.39), channel_id=1, source_target_pairs={{0,64},{16,464},{32,96},{48,496},{64,128},{80,16},{96,160},{112,48... | collective-permute-start | bytes 786440 | tf_op jit(solution)/shard_map/ppermute | solution.py:213
  45.7 15.4 %collective-permute-start.2 = (bf16[1024,128]{1,0:T(8,128)(2,1)S(1)}, bf16[1024,128]{1,0:T(8,128)(2,1)S(1)}, u32[]{:S(2)}, u32[]{:S(2)}) collective-permute-start(bf16[1024,128]{1,0:T(8,128)(2,1)S(1)} %bitcast.40), channel_id=1, source_target_pairs={{0,32},{16,48},{32,64},{48,80},{64,96},{80,112},{96,128},{112,144}... | collective-permute-start | bytes 786440 | tf_op jit(solution)/shard_map/ppermute | solution.py:213
  77.5 30.2 %all-to-all-start.3 = ((bf16[32,24,128]{2,1,0:T(8,128)(2,1)}), bf16[32,24,128]{2,1,0:T(8,128)(2,1)S(1)}, u32[]{:S(2)}, u32[]{:S(2)}) async-start(bf16[32,24,128]{2,1,0:T(8,128)(2,1)} %shard_map.104), calls=%async_computation.3 | async-start | bytes 393216 | tf_op jit(solution)/shard_map/all_to_all | solution.py:204
  89.4 45.7 %copy-start.3 = (f32[8]{0:T(128)S(1)}, f32[8]{0:T(128)}, u32[]{:S(2)}) copy-start(f32[8]{0:T(128)} %param.15) | copy-start | bytes 100
  89.5 25.7 %collective-permute-start.3 = (bf16[1024,128]{1,0:T(8,128)(2,1)S(1)}, bf16[1024,128]{1,0:T(8,128)(2,1)S(1)}, u32[]{:S(2)}, u32[]{:S(2)}) collective-permute-start(bf16[1024,128]{1,0:T(8,128)(2,1)S(1)} %get-tuple-element.17), channel_id=1, source_target_pairs={{0,32},{16,48},{32,64},{48,80},{64,96},{80,112},{96,128},{112,144}... | collective-permute-start | bytes 786440 | tf_op jit(solution)/shard_map/ppermute | solution.py:213
  92.7 22.5 %collective-permute-start.4 = (bf16[1024,128]{1,0:T(8,128)(2,1)S(1)}, bf16[1024,128]{1,0:T(8,128)(2,1)S(1)}, u32[]{:S(2)}, u32[]{:S(2)}) collective-permute-start(bf16[1024,128]{1,0:T(8,128)(2,1)S(1)} %get-tuple-element.19), channel_id=1, source_target_pairs={{0,480},{16,496},{32,0},{48,16},{64,32},{80,48},{96,64},{112,80},{... | collective-permute-start | bytes 786440 | tf_op jit(solution)/shard_map/ppermute | solution.py:213
  96.0 19.2 %collective-permute-start.5 = (bf16[1024,128]{1,0:T(8,128)(2,1)S(1)}, bf16[1024,128]{1,0:T(8,128)(2,1)S(1)}, u32[]{:S(2)}, u32[]{:S(2)}) collective-permute-start(bf16[1024,128]{1,0:T(8,128)(2,1)S(1)} %get-tuple-element.18), channel_id=1, source_target_pairs={{0,64},{16,464},{32,96},{48,496},{64,128},{80,16},{96,160},{112,48... | collective-permute-start | bytes 786440 | tf_op jit(solution)/shard_map/ppermute | solution.py:213
  107.7 0.7 copy-start.1
  110.0 21.4 %all-to-all-start.4 = ((bf16[32,16,128]{2,1,0:T(8,128)(2,1)}), bf16[32,16,128]{2,1,0:T(8,128)(2,1)S(1)}, u32[]{:S(2)}, u32[]{:S(2)}) async-start(bf16[32,16,128]{2,1,0:T(8,128)(2,1)} %shard_map.105), calls=%async_computation.4 | async-start | bytes 262144 | tf_op jit(solution)/shard_map/all_to_all | solution.py:204
  131.4 4.4 %copy-start.2 = (bf16[32,16,128]{2,1,0:T(8,128)(2,1)}, bf16[32,16,128]{2,1,0:T(8,128)(2,1)S(1)}, u32[]{:S(2)}) copy-start(bf16[32,16,128]{2,1,0:T(8,128)(2,1)S(1)} %all-to-all-done.4) | copy-start | bytes 393220
  131.4 17.4 %all-to-all-start.2 = ((bf16[8,128,128]{2,1,0:T(8,128)(2,1)}), bf16[8,128,128]{2,1,0:T(8,128)(2,1)S(1)}, u32[]{:S(2)}, u32[]{:S(2)}) async-start(bf16[8,128,128]{2,1,0:T(8,128)(2,1)} %bitcast.13), calls=%async_computation.2 | async-start | bytes 524288 | tf_op jit(solution)/shard_map/all_to_all | solution.py:204
  148.8 0.7 copy-start

commit v2 on v1

--- a/solution.py
+++ b/solution.py
@@ -213,18 +213,6 @@
     return lax.ppermute(x, SEQ, route)
 
 
-def peak_kernel(far_ref, peak_q_ref, peak_x_ref, own_ref, out_ref):
-    own = jnp.sum(far_ref[...].astype(f32), axis=0)
-    own_ref[...] = own
-    lane = lax.broadcasted_iota(jnp.int32, out_ref.shape, 1)
-    peak_kv = jnp.max(jnp.abs(own), keepdims=True)
-    out_ref[...] = jnp.where(lane == 0, peak_q_ref[:1], jnp.where(lane == 1, peak_kv, peak_x_ref[:1]))
-
-
-def merge_kernel(peaks_ref, out_ref):
-    out_ref[...] = jnp.broadcast_to(jnp.max(peaks_ref[...], axis=0, keepdims=True), out_ref.shape)
-
-
 def scale_kernel(peaks_ref, dq_ref, dkv_ref, dx_ref, q_ref, kv_ref, x_ref):
     peaks = jnp.max(peaks_ref[...], axis=0, keepdims=True) + EPSILON
     q_ref[...] = (dq_ref[...] / peaks[:, 0:1]).astype(bf16)
@@ -289,10 +277,13 @@
         flow.reshape(512, 128),
     )
 
-    dkv_own, peaks = call(peak_kernel, (struct((TOK, 128), f32), struct((32, 128), f32)), far, peak_q, peak_x)
-    peaks = swap_all(peaks, SEQ)
-    peaks = call(merge_kernel, struct((16, 128), f32), peaks)
-    peaks = swap_all(peaks, HEAD)
+    dkv_own = jnp.sum(far.astype(f32), axis=0)
+    lane = lax.broadcasted_iota(jnp.int32, (1, 128), 1)
+    early = jnp.where(lane == 0, peak_q[:1], peak_x[:1])
+    early = lax.optimization_barrier(early)
+    peaks = jnp.where(lane == 1, jnp.max(jnp.abs(dkv_own)), early)
+    peaks = jnp.max(swap_all(jnp.tile(peaks, (32, 1)), SEQ), axis=0, keepdims=True)
+    peaks = swap_all(jnp.tile(peaks, (16, 1)), HEAD)
     return call(
         scale_kernel,
         (struct((TOK, 512), bf16), struct((TOK, 128), bf16), struct((TOK, 512), bf16)),

time: 193 us -> 190 us (0.984)
  Pallas kernels: 17.9 us -> 14.9 us
  other arithmetic: 1.9 us -> 3.92 us
    pallas_call x7 -> x5, Pallas kernels: 17.9 us -> 14.9 us  [call(): pl.pallas_call(body, out_shape=out_shape, in_specs=specs, out_specs=jax.t...]
  transfers between devices with their start and end apart: 9 -> 9, of which waited for: 3 -> 3; matrix products, arithmetic and copies ran while one was open for 1% -> 2% of each run, Pallas kernels for 4% -> 4%
where the time goes in v2:
time: 190 us; the launch traced here: 189 us
  blocking collectives  89.8 us (47%)
  starting transfers between devices  45 us (24%)
  waiting for transfers between devices  32.5 us (17%)
  Pallas kernels  14.9 us (8%)
  other arithmetic  3.92 us (2%)
  local copies, waits for them, and re-layouts  2.23 us (1%)
    all_to_all x4, blocking collectives, swap_all(): return lax.all_to_all(x, axes, 0, 0, tiled=True)  74 us
    all_to_all x3, waiting for transfers between devices, swap_all(): return lax.all_to_all(x, axes, 0, 0, tiled=True)  32.5 us
    ppermute x6, starting transfers between devices, along_z(): return lax.ppermute(x, SEQ, route)  24.8 us
    all_to_all x3, starting transfers between devices, swap_all(): return lax.all_to_all(x, axes, 0, 0, tiled=True)  20.3 us
    all_gather x4, blocking collectives, step(): lax.all_gather(piece, 'c', axis=0, tiled=True).reshape(2, 4, 2, TOK, 128)  15.8 us
    pallas_call x5, Pallas kernels, call(): pl.pallas_call(body, out_shape=out_shape, in_specs=specs, out_specs=jax.t...  14.9 us
  transfers between devices with their start and end apart: 9, of which 3 were waited for; matrix products, arithmetic and copies ran while one was open for 2% of the time, Pallas kernels for 4%

profile of v2, /device:TPU:1, one launch (start us, length us, event | category | flops | bytes accessed | tf_op | source)
XLA Modules:
  0.0 189.2 jit_solution(9461231625308318283)
XLA Ops:
  0.6 0.8 tile.6
  1.4 30.4 %all_to_all.51 = bf16[8,128,128]{2,1,0:T(8,128)(2,1)S(1)} all-to-all(bf16[8,128,128]{2,1,0:T(8,128)(2,1)S(1)} %tile.6), channel_id=1, replica_groups=mesh['hi'=4,'lo'=4,'c'=2,'y'=4,'xh'=2,'xp'=2] {'hi','xp'}, dimensions={0} | all-to-all | bytes 524288 | tf_op jit(solution)/shard_map/all_to_all | solution.py:204
  31.9 4.5 %collective-permute-start = (bf16[1024,128]{1,0:T(8,128)(2,1)S(1)}, bf16[1024,128]{1,0:T(8,128)(2,1)S(1)}, u32[]{:S(2)}, u32[]{:S(2)}) collective-permute-start(bf16[1024,128]{1,0:T(8,128)(2,1)S(1)} %bitcast.34), channel_id=1, source_target_pairs={{0,480},{16,496},{32,0},{48,16},{64,32},{80,48},{96,64},{112,80},{... | collective-permute-start | bytes 786440 | tf_op jit(solution)/shard_map/ppermute | solution.py:213
  36.4 2.6 %shard_map.104 = bf16[32,24,128]{2,1,0:T(8,128)(2,1)} custom-call(bf16[128,512]{1,0:T(8,128)(2,1)} %dy_ref.3, bf16[128,128]{1,0:T(8,128)(2,1)} %c_ref.3, f32[8,128]{1,0:T(8,128)} %decay_ref.3), custom_call_target="tpu_custom_call" | custom-call | tf_op jit(solution)/shard_map/pallas_call | solution.py:194
  39.0 0.6 pad_add_fusion.pos_ref
  39.6 6.2 %collective-permute-start.1 = (bf16[1024,128]{1,0:T(8,128)(2,1)S(1)}, bf16[1024,128]{1,0:T(8,128)(2,1)S(1)}, u32[]{:S(2)}, u32[]{:S(2)}) collective-permute-start(bf16[1024,128]{1,0:T(8,128)(2,1)S(1)} %bitcast.35), channel_id=1, source_target_pairs={{0,64},{16,464},{32,96},{48,496},{64,128},{80,16},{96,160},{112,48... | collective-permute-start | bytes 786440 | tf_op jit(solution)/shard_map/ppermute | solution.py:213
  45.7 3.4 %collective-permute-start.2 = (bf16[1024,128]{1,0:T(8,128)(2,1)S(1)}, bf16[1024,128]{1,0:T(8,128)(2,1)S(1)}, u32[]{:S(2)}, u32[]{:S(2)}) collective-permute-start(bf16[1024,128]{1,0:T(8,128)(2,1)S(1)} %bitcast.36), channel_id=1, source_target_pairs={{0,32},{16,48},{32,64},{48,80},{64,96},{80,112},{96,128},{112,144}... | collective-permute-start | bytes 786440 | tf_op jit(solution)/shard_map/ppermute | solution.py:213
  49.1 4.9 %all_gather.12 = bf16[2048,128]{1,0:T(8,128)(2,1)} all-gather(bf16[1024,128]{1,0:T(8,128)(2,1)S(1)} %bitcast.37), channel_id=1, replica_groups=mesh['hi'=4,'lo'=4,'c'=2,'y'=4,'xh'=2,'xp'=2] {'c'}, dimensions={0}, use_global_device_ids=true | all-gather | bytes 786432 | tf_op jit(solution)/shard_map/all_gather | solution.py:240
  54.0 0.0 collective-permute-done
  54.0 2.3 %all_gather.13 = bf16[2048,128]{1,0:T(8,128)(2,1)} all-gather(bf16[1024,128]{1,0:T(8,128)(2,1)S(1)} %collective-permute-done), channel_id=1, replica_groups=mesh['hi'=4,'lo'=4,'c'=2,'y'=4,'xh'=2,'xp'=2] {'c'}, dimensions={0}, use_global_device_ids=true | all-gather | bytes 786432 | tf_op jit(solution)/shard_map/all_gather | solution.py:240
  56.3 0.0 collective-permute-done.1
  56.3 4.8 %all_gather.14 = bf16[2048,128]{1,0:T(8,128)(2,1)} all-gather(bf16[1024,128]{1,0:T(8,128)(2,1)S(1)} %collective-permute-done.1), channel_id=1, replica_groups=mesh['hi'=4,'lo'=4,'c'=2,'y'=4,'xh'=2,'xp'=2] {'c'}, dimensions={0}, use_global_device_ids=true | all-gather | bytes 786432 | tf_op jit(solution)/shard_map/all_gather | solution.py:240
  61.1 0.0 collective-permute-done.2
  61.1 3.9 %all_gather.15 = bf16[2048,128]{1,0:T(8,128)(2,1)} all-gather(bf16[1024,128]{1,0:T(8,128)(2,1)S(1)} %collective-permute-done.2), channel_id=1, replica_groups=mesh['hi'=4,'lo'=4,'c'=2,'y'=4,'xh'=2,'xp'=2] {'c'}, dimensions={0}, use_global_device_ids=true | all-gather | bytes 786432 | tf_op jit(solution)/shard_map/all_gather | solution.py:240
  65.0 5.9 %shard_map.103 = (f32[128,512]{1,0:T(8,128)}, bf16[2,4,4,2,128,128]{5,4,3,2,1,0:T(8,128)(2,1)}, f32[8,128]{1,0:T(8,128)}) custom-call(s32[2]{0:T(128)} %pad_add_fusion.pos_ref, bf16[128,512]{1,0:T(8,128)(2,1)} %q_ref.1, bf16[128,512]{1,0:T(8,128)(2,1)} %do_ref.1, bf16[2,4,2,128,128]{4,3,2,1,0:T(8,128)(2,1)} %bitcast.29, ...), custom_call_target="tpu_custom_call" | custom-call | tf_op jit(solution)/shard_map/pallas_call | solution.py:194
  70.9 6.6 %all_to_all.52 = bf16[2,4096,128]{2,1,0:T(8,128)(2,1)S(1)} all-to-all(bf16[2,4096,128]{2,1,0:T(8,128)(2,1)} %bitcast.33), channel_id=1, replica_groups=mesh['hi'=4,'lo'=4,'c'=2,'y'=4,'xh'=2,'xp'=2] {'c'}, dimensions={0} | all-to-all | bytes 4194304 | tf_op jit(solution)/shard_map/all_to_all | solution.py:204
  77.5 11.4 %all-to-all-start.3 = ((bf16[32,24,128]{2,1,0:T(8,128)(2,1)}), bf16[32,24,128]{2,1,0:T(8,128)(2,1)S(1)}, u32[]{:S(2)}, u32[]{:S(2)}) async-start(bf16[32,24,128]{2,1,0:T(8,128)(2,1)} %shard_map.104), calls=%async_computation.3 | async-start | bytes 393216 | tf_op jit(solution)/shard_map/all_to_all | solution.py:204
  88.9 0.3 convert_element_type.33
  89.2 0.2 fusion
  89.4 0.0 copy-start.3
  89.4 0.1 slice_bitcast_fusion.2
  89.5 3.3 %collective-permute-start.3 = (bf16[1024,128]{1,0:T(8,128)(2,1)S(1)}, bf16[1024,128]{1,0:T(8,128)(2,1)S(1)}, u32[]{:S(2)}, u32[]{:S(2)}) collective-permute-start(bf16[1024,128]{1,0:T(8,128)(2,1)S(1)} %get-tuple-element.13), channel_id=1, source_target_pairs={{0,32},{16,48},{32,64},{48,80},{64,96},{80,112},{96,128},{112,144}... | collective-permute-start | bytes 786440 | tf_op jit(solution)/shard_map/ppermute | solution.py:213
  92.8 3.2 %collective-permute-start.4 = (bf16[1024,128]{1,0:T(8,128)(2,1)S(1)}, bf16[1024,128]{1,0:T(8,128)(2,1)S(1)}, u32[]{:S(2)}, u32[]{:S(2)}) collective-permute-start(bf16[1024,128]{1,0:T(8,128)(2,1)S(1)} %get-tuple-element.15), channel_id=1, source_target_pairs={{0,480},{16,496},{32,0},{48,16},{64,32},{80,48},{96,64},{112,80},{... | collective-permute-start | bytes 786440 | tf_op jit(solution)/shard_map/ppermute | solution.py:213
  96.0 4.2 %collective-permute-start.5 = (bf16[1024,128]{1,0:T(8,128)(2,1)S(1)}, bf16[1024,128]{1,0:T(8,128)(2,1)S(1)}, u32[]{:S(2)}, u32[]{:S(2)}) collective-permute-start(bf16[1024,128]{1,0:T(8,128)(2,1)S(1)} %get-tuple-element.14), channel_id=1, source_target_pairs={{0,64},{16,464},{32,96},{48,496},{64,128},{80,16},{96,160},{112,48... | collective-permute-start | bytes 786440 | tf_op jit(solution)/shard_map/ppermute | solution.py:213
  100.2 7.5 %all-to-all-done.3.state_ref = bf16[32,24,128]{2,1,0:T(8,128)(2,1)S(1)} async-done(((bf16[32,24,128]{2,1,0:T(8,128)(2,1)}), bf16[32,24,128]{2,1,0:T(8,128)(2,1)S(1)}, u32[]{:S(2)}, u32[]{:S(2)}) %all-to-all-start.3) | async-done | bytes 196640 | tf_op jit(solution)/shard_map/all_to_all | solution.py:204
  107.7 0.0 copy-start
  107.7 0.7 copy-done
  108.4 1.7 shard_map.105
  110.0 5.2 %all-to-all-start.4 = ((bf16[32,16,128]{2,1,0:T(8,128)(2,1)}), bf16[32,16,128]{2,1,0:T(8,128)(2,1)S(1)}, u32[]{:S(2)}, u32[]{:S(2)}) async-start(bf16[32,16,128]{2,1,0:T(8,128)(2,1)} %shard_map.105), calls=%async_computation.4 | async-start | bytes 262144 | tf_op jit(solution)/shard_map/all_to_all | solution.py:204
  115.2 0.0 collective-permute-done.3
  115.2 0.0 collective-permute-done.4
  115.2 0.0 collective-permute-done.5
  115.2 0.8 fusion.2
  116.1 15.3 %all-to-all-done.4 = bf16[32,16,128]{2,1,0:T(8,128)(2,1)S(1)} async-done(((bf16[32,16,128]{2,1,0:T(8,128)(2,1)}), bf16[32,16,128]{2,1,0:T(8,128)(2,1)S(1)}, u32[]{:S(2)}, u32[]{:S(2)}) %all-to-all-start.4) | async-done | bytes 131104 | tf_op jit(solution)/shard_map/all_to_all | solution.py:204
  131.4 3.7 %all-to-all-start.2 = ((bf16[8,128,128]{2,1,0:T(8,128)(2,1)}), bf16[8,128,128]{2,1,0:T(8,128)(2,1)S(1)}, u32[]{:S(2)}, u32[]{:S(2)}) async-start(bf16[8,128,128]{2,1,0:T(8,128)(2,1)} %bitcast.13), calls=%async_computation.2 | async-start | bytes 524288 | tf_op jit(solution)/shard_map/all_to_all | solution.py:204
  135.1 0.0 copy-done.3
  135.1 0.7 copy.14.skip_ref
  135.8 0.0 copy-done.2
  135.8 2.9 %shard_map.106 = (f32[128,512]{1,0:T(8,128)}, f32[8,128]{1,0:T(8,128)}) custom-call(bf16[128,512]{1,0:T(8,128)(2,1)} %dy_ref.3, bf16[128,128]{1,0:T(8,128)(2,1)} %b_ref.1, bf16[128,128]{1,0:T(8,128)(2,1)} %c_ref.3, f32[8,128]{1,0:T(8,128)} %decay_ref.3, f32[8,1]{1,0:T(8,128)} %copy.14.skip_ref, bf16[512,128]{1,0:T(8,128)(2,1)} %bitcast.38), custom_call_target="tpu_custom_call" | custom-call | tf_op jit(solution)/shard_map/pallas_call | solution.py:194
  138.7 0.7 compare_select_fusion
  139.4 9.7 %all-to-all-done.2 = bf16[8,128,128]{2,1,0:T(8,128)(2,1)S(1)} async-done(((bf16[8,128,128]{2,1,0:T(8,128)(2,1)}), bf16[8,128,128]{2,1,0:T(8,128)(2,1)S(1)}, u32[]{:S(2)}, u32[]{:S(2)}) %all-to-all-start.2) | async-done | bytes 262176 | tf_op jit(solution)/shard_map/all_to_all | solution.py:204
  149.1 0.0 copy-start.1
  149.1 0.6 abs_reduce_fusion
  149.7 0.6 fusion.3
  150.4 24.1 %all_to_all.53 = f32[32,1,128]{2,1,0:T(1,128)S(1)} all-to-all(f32[32,1,128]{2,1,0:T(1,128)S(1)} %tile.7), channel_id=1, replica_groups=mesh['hi'=4,'lo'=4,'c'=2,'y'=4,'xh'=2,'xp'=2] {'hi','lo','c'}, dimensions={0} | all-to-all | bytes 32768 | tf_op jit(solution)/shard_map/all_to_all | solution.py:204
  174.5 12.8 %all_to_all.54 = f32[16,1,128]{2,1,0:T(1,128)} all-to-all(f32[16,1,128]{2,1,0:T(1,128)S(1)} %tile.8), channel_id=1, replica_groups=mesh['hi'=4,'lo'=4,'c'=2,'y'=4,'xh'=2,'xp'=2] {'y','xh','xp'}, dimensions={0} | all-to-all | bytes 16384 | tf_op jit(solution)/shard_map/all_to_all | solution.py:204
  187.4 0.0 copy-done.1
  187.4 1.9 shard_map.107
  (5 shorter events, 0.1 us)
Async XLA Ops:
  31.9 22.1 %collective-permute-start = (bf16[1024,128]{1,0:T(8,128)(2,1)S(1)}, bf16[1024,128]{1,0:T(8,128)(2,1)S(1)}, u32[]{:S(2)}, u32[]{:S(2)}) collective-permute-start(bf16[1024,128]{1,0:T(8,128)(2,1)S(1)} %bitcast.34), channel_id=1, source_target_pairs={{0,480},{16,496},{32,0},{48,16},{64,32},{80,48},{96,64},{112,80},{... | collective-permute-start | bytes 786440 | tf_op jit(solution)/shard_map/ppermute | solution.py:213
  39.6 16.7 %collective-permute-start.1 = (bf16[1024,128]{1,0:T(8,128)(2,1)S(1)}, bf16[1024,128]{1,0:T(8,128)(2,1)S(1)}, u32[]{:S(2)}, u32[]{:S(2)}) collective-permute-start(bf16[1024,128]{1,0:T(8,128)(2,1)S(1)} %bitcast.35), channel_id=1, source_target_pairs={{0,64},{16,464},{32,96},{48,496},{64,128},{80,16},{96,160},{112,48... | collective-permute-start | bytes 786440 | tf_op jit(solution)/shard_map/ppermute | solution.py:213
  45.7 15.4 %collective-permute-start.2 = (bf16[1024,128]{1,0:T(8,128)(2,1)S(1)}, bf16[1024,128]{1,0:T(8,128)(2,1)S(1)}, u32[]{:S(2)}, u32[]{:S(2)}) collective-permute-start(bf16[1024,128]{1,0:T(8,128)(2,1)S(1)} %bitcast.36), channel_id=1, source_target_pairs={{0,32},{16,48},{32,64},{48,80},{64,96},{80,112},{96,128},{112,144}... | collective-permute-start | bytes 786440 | tf_op jit(solution)/shard_map/ppermute | solution.py:213
  77.5 30.2 %all-to-all-start.3 = ((bf16[32,24,128]{2,1,0:T(8,128)(2,1)}), bf16[32,24,128]{2,1,0:T(8,128)(2,1)S(1)}, u32[]{:S(2)}, u32[]{:S(2)}) async-start(bf16[32,24,128]{2,1,0:T(8,128)(2,1)} %shard_map.104), calls=%async_computation.3 | async-start | bytes 393216 | tf_op jit(solution)/shard_map/all_to_all | solution.py:204
  89.4 45.7 %copy-start.3 = (f32[8]{0:T(128)S(1)}, f32[8]{0:T(128)}, u32[]{:S(2)}) copy-start(f32[8]{0:T(128)} %param.15) | copy-start | bytes 100
  89.5 25.7 %collective-permute-start.3 = (bf16[1024,128]{1,0:T(8,128)(2,1)S(1)}, bf16[1024,128]{1,0:T(8,128)(2,1)S(1)}, u32[]{:S(2)}, u32[]{:S(2)}) collective-permute-start(bf16[1024,128]{1,0:T(8,128)(2,1)S(1)} %get-tuple-element.13), channel_id=1, source_target_pairs={{0,32},{16,48},{32,64},{48,80},{64,96},{80,112},{96,128},{112,144}... | collective-permute-start | bytes 786440 | tf_op jit(solution)/shard_map/ppermute | solution.py:213
  92.8 22.5 %collective-permute-start.4 = (bf16[1024,128]{1,0:T(8,128)(2,1)S(1)}, bf16[1024,128]{1,0:T(8,128)(2,1)S(1)}, u32[]{:S(2)}, u32[]{:S(2)}) collective-permute-start(bf16[1024,128]{1,0:T(8,128)(2,1)S(1)} %get-tuple-element.15), channel_id=1, source_target_pairs={{0,480},{16,496},{32,0},{48,16},{64,32},{80,48},{96,64},{112,80},{... | collective-permute-start | bytes 786440 | tf_op jit(solution)/shard_map/ppermute | solution.py:213
  96.0 19.2 %collective-permute-start.5 = (bf16[1024,128]{1,0:T(8,128)(2,1)S(1)}, bf16[1024,128]{1,0:T(8,128)(2,1)S(1)}, u32[]{:S(2)}, u32[]{:S(2)}) collective-permute-start(bf16[1024,128]{1,0:T(8,128)(2,1)S(1)} %get-tuple-element.14), channel_id=1, source_target_pairs={{0,64},{16,464},{32,96},{48,496},{64,128},{80,16},{96,160},{112,48... | collective-permute-start | bytes 786440 | tf_op jit(solution)/shard_map/ppermute | solution.py:213
  107.7 0.7 copy-start
  110.0 21.4 %all-to-all-start.4 = ((bf16[32,16,128]{2,1,0:T(8,128)(2,1)}), bf16[32,16,128]{2,1,0:T(8,128)(2,1)S(1)}, u32[]{:S(2)}, u32[]{:S(2)}) async-start(bf16[32,16,128]{2,1,0:T(8,128)(2,1)} %shard_map.105), calls=%async_computation.4 | async-start | bytes 262144 | tf_op jit(solution)/shard_map/all_to_all | solution.py:204
  131.4 4.4 %copy-start.2 = (bf16[32,16,128]{2,1,0:T(8,128)(2,1)}, bf16[32,16,128]{2,1,0:T(8,128)(2,1)S(1)}, u32[]{:S(2)}) copy-start(bf16[32,16,128]{2,1,0:T(8,128)(2,1)S(1)} %all-to-all-done.4) | copy-start | bytes 393220
  131.4 17.7 %all-to-all-start.2 = ((bf16[8,128,128]{2,1,0:T(8,128)(2,1)}), bf16[8,128,128]{2,1,0:T(8,128)(2,1)S(1)}, u32[]{:S(2)}, u32[]{:S(2)}) async-start(bf16[8,128,128]{2,1,0:T(8,128)(2,1)} %bitcast.13), calls=%async_computation.2 | async-start | bytes 524288 | tf_op jit(solution)/shard_map/all_to_all | solution.py:204
  149.1 38.2 %copy-start.1 = (f32[128,128]{1,0:T(8,128)}, f32[128,128]{1,0:T(8,128)S(1)}, u32[]{:S(2)}) copy-start(f32[128,128]{1,0:T(8,128)S(1)} %convert_reduce_fusion.dkv_ref) | copy-start | bytes 196612

commit v3 on v2

--- a/solution.py
+++ b/solution.py
@@ -9,9 +9,10 @@
 from jax.sharding import PartitionSpec as P
 
 
-SEQ = ("hi", "lo", "c")
+SEQ = ("z", "c")
 HEAD = ("y", "xh", "xp")
-SIZES = (4, 4, 2, 4, 2, 2)
+SIZES = (16, 2, 4, 2, 2)
+NEAR = (-2, -1, 0, 1, 2)
 CHIPS = 16
 TOK = 128
 SSM_HEADS = 8
@@ -37,36 +38,37 @@
 
 
 def attention_kernel(pos_ref, q_ref, do_ref, *refs):
-    pieces, (dq_ref, dkv_ref, peak_ref, kv_ref, p_ref, dp_ref, outt_ref, dqt_ref, sems) = refs[:4], refs[4:]
-    copies = [pltpu.make_async_copy(piece, kv_ref.at[r], sems.at[r]) for r, piece in enumerate(pieces)]
+    pieces, (dq_ref, dkv_ref, peak_ref, kv_ref, p_ref, dp_ref, outt_ref, dqt_ref, sems) = refs[:6], refs[6:]
+    copies = []
+    for k, piece in enumerate(pieces):
+        count = piece.shape[0]
+        copies.append(pltpu.make_async_copy(piece, kv_ref.at[pl.ds(12 * k, count)], sems.at[k]))
     for copy in copies:
         copy.start()
     chip, core = pos_ref[0], pos_ref[1]
-    lane_group = lax.rem(chip, 4)
     q = heads_to_rows(q_ref[...])
     do = heads_to_rows(do_ref[...])
     width = q.shape[0]
 
     steps = chip // 2 + 1
 
-    def place(z):
-        return lax.rem(lax.rem(z, 4) - lane_group + 4, 4), z // 4
-
     def tiles(j):
         for z in (2 * j, 2 * j + 1):
-            rel, hi = place(z)
+            k = lax.rem(z - chip + 7 + CHIPS, CHIPS)
+            near, far = lax.rem(k, 5), k // 5
             for c in range(2):
-                yield rel, c, hi
+                held = jnp.where(k == 15, 60 + 2 * c, 12 * near + 6 * c + 2 * far)
+                yield held, 2 * CHIPS * c + 2 * jnp.where(k == 15, 15, 3 * near + far)
 
     def rows_at(j):
         return pl.ds(pl.multiple_of(j * 4 * TOK, 4 * TOK), 4 * TOK)
 
     def keys_at(j, part):
-        return jnp.concatenate([kv_ref[rel, c, hi, part] for rel, c, hi in tiles(j)], axis=0)
+        return jnp.concatenate([kv_ref[held + part] for held, _ in tiles(j)], axis=0)
 
     def store_at(j, part, x):
-        for k, (rel, c, hi) in enumerate(tiles(j)):
-            dkv_ref[c, rel, hi, part] = x[TOK * k : TOK * (k + 1)]
+        for k, (_, out) in enumerate(tiles(j)):
+            dkv_ref[out + part] = x[TOK * k : TOK * (k + 1)]
 
     def partial_rows(x, op):
         return op(x.reshape(4 * TOK // 8, 8, width), axis=0)
@@ -204,13 +206,14 @@
     return lax.all_to_all(x, axes, 0, 0, tiled=True)
 
 
-def along_z(x, step):
-    route = []
-    for chip in range(CHIPS):
-        for core in range(2):
-            move = step if step != 2 or core == 0 else -2
-            route.append((2 * chip + core, 2 * ((chip + move) % CHIPS) + core))
+def along_z(x, move, first=0):
+    chips = range(first, CHIPS) if first >= 0 else range(-first)
+    route = [(2 * z + c, 2 * ((z + move) % CHIPS) + c) for z in chips for c in range(2)]
     return lax.ppermute(x, SEQ, route)
+
+
+def swap_pair(x):
+    return lax.ppermute(x, "xp", [(0, 1), (1, 0)])
 
 
 def scale_kernel(peaks_ref, dq_ref, dkv_ref, dx_ref, q_ref, kv_ref, x_ref):
@@ -221,14 +224,21 @@
 
 
 def step(queries, key_value, grad_out, ssm_grad, b_proj, c_proj, decay_log, skip_gain):
-    chip = lax.axis_index(("hi", "lo"))
-    pos = jnp.stack([chip, lax.axis_index("c")]).astype(jnp.int32)
+    keys_here = lax.axis_index("xp") == 0
+    pos = jnp.stack([lax.axis_index("z"), lax.axis_index("c")]).astype(jnp.int32)
     struct = jax.ShapeDtypeStruct
 
-    column = swap_all(jnp.tile(key_value, (8, 1)), ("hi", "xp"))
-    two = along_z(column, 2)
-    after = along_z(column, -1)
-    before = along_z(column, 1)
+    other = swap_pair(key_value)
+    shard = jnp.concatenate(
+        [jnp.where(keys_here, key_value, other), jnp.where(keys_here, other, key_value)], axis=0
+    )
+    below = along_z(shard, 5)
+    above = along_z(shard, -5)
+    across = along_z(shard, 8, -8)
+    three = jnp.concatenate([below, shard, above], axis=0)
+    near = []
+    for d in NEAR:
+        near.append(along_z(three, -d) if d else three)
 
     state = call(state_kernel, struct((2 * CHIPS, 24, 128), bf16), ssm_grad, c_proj, decay_log)
     states = swap_all(state, SEQ)
@@ -236,36 +246,41 @@
     flow = swap_all(flows, SEQ)
 
     pieces = []
-    for piece in (column, after, two, before):
-        pieces.append(lax.all_gather(piece, "c", axis=0, tiled=True).reshape(2, 4, 2, TOK, 128))
+    for piece in near + [across]:
+        pieces.append(lax.all_gather(piece, "c", axis=0, tiled=True).reshape(-1, TOK, 128))
     dq, dkv, peak_q = call(
         attention_kernel,
-        (struct((TOK, 512), f32), struct((2, 4, 4, 2, TOK, 128), bf16), struct((8, 128), f32)),
+        (struct((TOK, 512), f32), struct((4 * CHIPS, TOK, 128), bf16), struct((8, 128), f32)),
         pos,
         queries,
         grad_out,
         *pieces,
         scratch=(
-            pltpu.VMEM((4, 2, 4, 2, TOK, 128), bf16),
+            pltpu.VMEM((4 * CHIPS, TOK, 128), bf16),
             pltpu.VMEM((256 * CHIPS, 512), f32),
             pltpu.VMEM((256 * CHIPS, 512), f32),
             pltpu.VMEM((128, 512), f32),
             pltpu.VMEM((128, 512), f32),
-            pltpu.SemaphoreType.DMA((4,)),
+            pltpu.SemaphoreType.DMA((6,)),
         ),
         scalars=1,
-        raw=4,
-    )
-
-    both = swap_all(dkv.reshape(2 * 4096, 128), "c").reshape(2, 4, 1024, 128).astype(f32)
+        raw=6,
+    )
+
+    both = swap_all(dkv.reshape(2 * 4096, 128), "c").reshape(2, CHIPS, 2 * TOK, 128).astype(f32)
     chip_sum = (both[0] + both[1]).astype(bf16)
-    from_two = along_z(chip_sum[2], 2)
-    from_before = along_z(chip_sum[1], 1)
-    from_after = along_z(chip_sum[3], -1)
-    near = (
-        (chip_sum[0].astype(f32) + from_before.astype(f32)) + (from_after.astype(f32) + from_two.astype(f32))
-    ).astype(bf16)
-    far = swap_all(near, ("hi", "xp")).reshape(8, TOK, 128)
+    parts = [chip_sum[6:9].astype(f32)]
+    for k, d in enumerate(NEAR):
+        if d:
+            parts.append(along_z(chip_sum[3 * k : 3 * k + 3], d).astype(f32))
+    three = (((parts[0] + parts[1]) + (parts[2] + parts[3])) + parts[4]).astype(bf16)
+    from_above = along_z(three[0], -5)
+    from_below = along_z(three[2], 5)
+    from_across = along_z(chip_sum[15], -8, 8)
+    own = (three[1].astype(f32) + from_across.astype(f32)) + (from_above.astype(f32) + from_below.astype(f32))
+    mine = jnp.where(keys_here, own[:TOK], own[TOK:])
+    other = jnp.where(keys_here, own[TOK:], own[:TOK]).astype(bf16)
+    other = swap_pair(other)
     dx, peak_x = call(
         ssm_kernel,
         (struct((TOK, 512), f32), struct((8, 128), f32)),
@@ -277,7 +292,7 @@
         flow.reshape(512, 128),
     )
 
-    dkv_own = jnp.sum(far.astype(f32), axis=0)
+    dkv_own = mine + other.astype(f32)
     lane = lax.broadcasted_iota(jnp.int32, (1, 128), 1)
     early = jnp.where(lane == 0, peak_q[:1], peak_x[:1])
     early = lax.optimization_barrier(early)

time: 190 us -> 201 us (1.058)
  starting transfers between devices: 45 us -> 101 us
  blocking collectives: 89.8 us -> 52.3 us
  waiting for transfers between devices: 32.5 us -> 23.3 us
    ppermute x6 -> x14, starting transfers between devices: 24.8 us -> 64.3 us  [along_z(): return lax.ppermute(x, SEQ, route)]
    all_to_all x4 -> x3, blocking collectives: 74 us -> 35.8 us  [swap_all(): return lax.all_to_all(x, axes, 0, 0, tiled=True)]
    all_to_all x3 -> x2, waiting for transfers between devices: 32.5 us -> 9.61 us  [swap_all(): return lax.all_to_all(x, axes, 0, 0, tiled=True)]
    ppermute x6 -> x14, waiting for transfers between devices: 0.02 us -> 11.1 us  [along_z(): return lax.ppermute(x, SEQ, route)]
    all_to_all x3 -> x2, starting transfers between devices: 20.3 us -> 30.1 us  [swap_all(): return lax.all_to_all(x, axes, 0, 0, tiled=True)]
    ppermute x0 -> x2, starting transfers between devices: none -> 7.05 us  [swap_pair(): return lax.ppermute(x, 'xp', [(0, 1), (1, 0)])]
    ppermute x0 -> x2, waiting for transfers between devices: none -> 2.64 us  [swap_pair(): return lax.ppermute(x, 'xp', [(0, 1), (1, 0)])]
    all_gather x4 -> x6, blocking collectives: 15.8 us -> 16.5 us  [step(): lax.all_gather(piece, 'c', axis=0, tiled=True).reshape(-1, TOK, 128)]
  transfers between devices with their start and end apart: 9 -> 18, of which waited for: 3 -> 6; matrix products, arithmetic and copies ran while one was open for 2% -> 2% of each run, Pallas kernels for 4% -> 2%
where the time goes in v3:
time: 201 us; the launch traced here: 200 us
  starting transfers between devices  101 us (50%)
  blocking collectives  52.3 us (26%)
  waiting for transfers between devices  23.3 us (12%)
  Pallas kernels  14.9 us (7%)
  other arithmetic  4.52 us (2%)
  local copies, waits for them, and re-layouts  2.09 us (1%)
    ppermute x14, starting transfers between devices, along_z(): return lax.ppermute(x, SEQ, route)  64.3 us
    all_to_all x3, blocking collectives, swap_all(): return lax.all_to_all(x, axes, 0, 0, tiled=True)  35.8 us
    all_to_all x2, starting transfers between devices, swap_all(): return lax.all_to_all(x, axes, 0, 0, tiled=True)  30.1 us
    all_gather x6, blocking collectives, step(): lax.all_gather(piece, 'c', axis=0, tiled=True).reshape(-1, TOK, 128)  16.5 us
    pallas_call x5, Pallas kernels, call(): pl.pallas_call(body, out_shape=out_shape, in_specs=specs, out_specs=jax.t...  14.9 us
    ppermute x14, waiting for transfers between devices, along_z(): return lax.ppermute(x, SEQ, route)  11.1 us
    all_to_all x2, waiting for transfers between devices, swap_all(): return lax.all_to_all(x, axes, 0, 0, tiled=True)  9.61 us
    ppermute x2, starting transfers between devices, swap_pair(): return lax.ppermute(x, 'xp', [(0, 1), (1, 0)])  7.05 us
  transfers between devices with their start and end apart: 18, of which 6 were waited for; matrix products, arithmetic and copies ran while one was open for 2% of the time, Pallas kernels for 2%

profile of v3, /device:TPU:1, one launch (start us, length us, event | category | flops | bytes accessed | tf_op | source)
XLA Modules:
  0.0 199.6 jit_solution(16158332573005678849)
XLA Ops:
  0.6 3.9 %collective-permute-start = (bf16[128,128]{1,0:T(8,128)(2,1)}, bf16[128,128]{1,0:T(8,128)(2,1)S(1)}, u32[]{:S(2)}, u32[]{:S(2)}) collective-permute-start(bf16[128,128]{1,0:T(8,128)(2,1)} %param.9), channel_id=1, source_target_pairs={{0,1},{1,0},{2,3},{3,2},{4,5},{5,4},{6,7},{7,6},{8,9},{9,8},{10,11... | collective-permute-start | bytes 98312 | tf_op jit(solution)/shard_map/ppermute | solution.py:216
  4.6 1.5 collective-permute-done
  6.1 0.8 broadcast_select_fusion.1
  6.8 10.4 %collective-permute-start.1 = (bf16[256,128]{1,0:T(8,128)(2,1)S(1)}, bf16[256,128]{1,0:T(8,128)(2,1)S(1)}, u32[]{:S(2)}, u32[]{:S(2)}) collective-permute-start(bf16[256,128]{1,0:T(8,128)(2,1)S(1)} %pad_maximum_fusion.1), channel_id=1, source_target_pairs={{0,160},{16,176},{32,192},{48,208},{64,224},{80,240},{96,256},{112... | collective-permute-start | bytes 196616 | tf_op jit(solution)/shard_map/ppermute | solution.py:212
  17.3 5.9 %collective-permute-start.2 = (bf16[256,128]{1,0:T(8,128)(2,1)S(1)}, bf16[256,128]{1,0:T(8,128)(2,1)S(1)}, u32[]{:S(2)}, u32[]{:S(2)}) collective-permute-start(bf16[256,128]{1,0:T(8,128)(2,1)S(1)} %pad_maximum_fusion.1), channel_id=1, source_target_pairs={{0,352},{16,368},{32,384},{48,400},{64,416},{80,432},{96,448},{112... | collective-permute-start | bytes 196616 | tf_op jit(solution)/shard_map/ppermute | solution.py:212
  23.1 2.6 %shard_map.104 = bf16[32,24,128]{2,1,0:T(8,128)(2,1)} custom-call(bf16[128,512]{1,0:T(8,128)(2,1)} %dy_ref.3, bf16[128,128]{1,0:T(8,128)(2,1)} %c_ref.3, f32[8,128]{1,0:T(8,128)} %decay_ref.3), custom_call_target="tpu_custom_call" | custom-call | tf_op jit(solution)/shard_map/pallas_call | solution.py:196
  25.7 10.7 %collective-permute-start.7 = (bf16[256,128]{1,0:T(8,128)(2,1)S(1)}, bf16[256,128]{1,0:T(8,128)(2,1)S(1)}, u32[]{:S(2)}, u32[]{:S(2)}) collective-permute-start(bf16[256,128]{1,0:T(8,128)(2,1)S(1)} %pad_maximum_fusion.1), channel_id=1, source_target_pairs={{0,256},{16,272},{32,288},{48,304},{64,320},{80,336},{96,352},{112... | collective-permute-start | bytes 196616 | tf_op jit(solution)/shard_map/ppermute | solution.py:212
  36.5 1.9 collective-permute-start.3
  38.4 0.6 pad_add_fusion.pos_ref
  39.0 3.1 %collective-permute-start.4 = (bf16[768,128]{1,0:T(8,128)(2,1)S(1)}, bf16[768,128]{1,0:T(8,128)(2,1)S(1)}, u32[]{:S(2)}, u32[]{:S(2)}) collective-permute-start(bf16[768,128]{1,0:T(8,128)(2,1)S(1)} %pad_maximum_fusion), channel_id=1, source_target_pairs={{0,32},{16,48},{32,64},{48,80},{64,96},{80,112},{96,128},{112,144}... | collective-permute-start | bytes 589832 | tf_op jit(solution)/shard_map/ppermute | solution.py:212
  42.1 3.4 %collective-permute-start.5 = (bf16[768,128]{1,0:T(8,128)(2,1)S(1)}, bf16[768,128]{1,0:T(8,128)(2,1)S(1)}, u32[]{:S(2)}, u32[]{:S(2)}) collective-permute-start(bf16[768,128]{1,0:T(8,128)(2,1)S(1)} %pad_maximum_fusion), channel_id=1, source_target_pairs={{0,480},{16,496},{32,0},{48,16},{64,32},{80,48},{96,64},{112,80},{... | collective-permute-start | bytes 589832 | tf_op jit(solution)/shard_map/ppermute | solution.py:212
  45.5 4.3 %collective-permute-start.6 = (bf16[768,128]{1,0:T(8,128)(2,1)S(1)}, bf16[768,128]{1,0:T(8,128)(2,1)S(1)}, u32[]{:S(2)}, u32[]{:S(2)}) collective-permute-start(bf16[768,128]{1,0:T(8,128)(2,1)S(1)} %pad_maximum_fusion), channel_id=1, source_target_pairs={{0,448},{16,464},{32,480},{48,496},{64,0},{80,16},{96,32},{112,48}... | collective-permute-start | bytes 589832 | tf_op jit(solution)/shard_map/ppermute | solution.py:212
  49.8 5.5 %all_gather.23 = bf16[512,128]{1,0:T(8,128)(2,1)} all-gather(bf16[256,128]{1,0:T(8,128)(2,1)S(1)} %collective-permute-done.7), channel_id=1, replica_groups=mesh['z'=16,'c'=2,'y'=4,'xh'=2,'xp'=2] {'c'}, dimensions={0}, use_global_device_ids=true | all-gather | bytes 196608 | tf_op jit(solution)/shard_map/all_gather | solution.py:250
  55.2 2.2 %all_gather.20 = bf16[1536,128]{1,0:T(8,128)(2,1)} all-gather(bf16[768,128]{1,0:T(8,128)(2,1)S(1)} %pad_maximum_fusion), channel_id=1, replica_groups=mesh['z'=16,'c'=2,'y'=4,'xh'=2,'xp'=2] {'c'}, dimensions={0}, use_global_device_ids=true | all-gather | bytes 589824 | tf_op jit(solution)/shard_map/all_gather | solution.py:250
  57.4 2.2 %all_gather.18 = bf16[1536,128]{1,0:T(8,128)(2,1)} all-gather(bf16[768,128]{1,0:T(8,128)(2,1)S(1)} %collective-permute-done.3), channel_id=1, replica_groups=mesh['z'=16,'c'=2,'y'=4,'xh'=2,'xp'=2] {'c'}, dimensions={0}, use_global_device_ids=true | all-gather | bytes 589824 | tf_op jit(solution)/shard_map/all_gather | solution.py:250
  59.6 2.2 %all_gather.19 = bf16[1536,128]{1,0:T(8,128)(2,1)} all-gather(bf16[768,128]{1,0:T(8,128)(2,1)S(1)} %collective-permute-done.4), channel_id=1, replica_groups=mesh['z'=16,'c'=2,'y'=4,'xh'=2,'xp'=2] {'c'}, dimensions={0}, use_global_device_ids=true | all-gather | bytes 589824 | tf_op jit(solution)/shard_map/all_gather | solution.py:250
  61.9 2.2 %all_gather.21 = bf16[1536,128]{1,0:T(8,128)(2,1)} all-gather(bf16[768,128]{1,0:T(8,128)(2,1)S(1)} %collective-permute-done.5), channel_id=1, replica_groups=mesh['z'=16,'c'=2,'y'=4,'xh'=2,'xp'=2] {'c'}, dimensions={0}, use_global_device_ids=true | all-gather | bytes 589824 | tf_op jit(solution)/shard_map/all_gather | solution.py:250
  64.1 2.2 %all_gather.22 = bf16[1536,128]{1,0:T(8,128)(2,1)} all-gather(bf16[768,128]{1,0:T(8,128)(2,1)S(1)} %collective-permute-done.6), channel_id=1, replica_groups=mesh['z'=16,'c'=2,'y'=4,'xh'=2,'xp'=2] {'c'}, dimensions={0}, use_global_device_ids=true | all-gather | bytes 589824 | tf_op jit(solution)/shard_map/all_gather | solution.py:250
  66.3 5.9 %shard_map.103 = (f32[128,512]{1,0:T(8,128)}, bf16[64,128,128]{2,1,0:T(8,128)(2,1)}, f32[8,128]{1,0:T(8,128)}) custom-call(s32[2]{0:T(128)} %pad_add_fusion.pos_ref, bf16[128,512]{1,0:T(8,128)(2,1)} %q_ref.1, bf16[128,512]{1,0:T(8,128)(2,1)} %do_ref.1, bf16[12,128,128]{2,1,0:T(8,128)(2,1)} %bitcast.45, bf16[12,128,128]{2,1,0:T(8,128)(2,1)} %bitcast.46, ...), custom_call_target="tpu_custom_call" | custom-call | tf_op jit(solution)/shard_map/pallas_call | solution.py:196
  72.2 6.6 %all_to_all.33 = bf16[2,4096,128]{2,1,0:T(8,128)(2,1)S(1)} all-to-all(bf16[2,4096,128]{2,1,0:T(8,128)(2,1)} %bitcast.43), channel_id=1, replica_groups=mesh['z'=16,'c'=2,'y'=4,'xh'=2,'xp'=2] {'c'}, dimensions={0} | all-to-all | bytes 4194304 | tf_op jit(solution)/shard_map/all_to_all | solution.py:206
  78.8 12.5 %all-to-all-start.1 = ((bf16[32,24,128]{2,1,0:T(8,128)(2,1)}), bf16[32,24,128]{2,1,0:T(8,128)(2,1)S(1)}, u32[]{:S(2)}, u32[]{:S(2)}) async-start(bf16[32,24,128]{2,1,0:T(8,128)(2,1)} %shard_map.104), calls=%async_computation.1 | async-start | bytes 393216 | tf_op jit(solution)/shard_map/all_to_all | solution.py:206
  91.3 0.3 convert_element_type.53
  91.6 0.2 fusion
  91.9 3.3 %collective-permute-start.10 = (bf16[3,256,128]{2,1,0:T(8,128)(2,1)S(1)}, bf16[3,256,128]{2,1,0:T(8,128)(2,1)S(1)}, u32[]{:S(2)}, u32[]{:S(2)}) collective-permute-start(bf16[3,256,128]{2,1,0:T(8,128)(2,1)S(1)} %get-tuple-element.17), channel_id=1, source_target_pairs={{0,32},{16,48},{32,64},{48,80},{64,96},{80,112},{96,128},{112,144}... | collective-permute-start | bytes 589832 | tf_op jit(solution)/shard_map/ppermute | solution.py:212
  95.1 4.0 %collective-permute-start.11 = (bf16[3,256,128]{2,1,0:T(8,128)(2,1)S(1)}, bf16[3,256,128]{2,1,0:T(8,128)(2,1)S(1)}, u32[]{:S(2)}, u32[]{:S(2)}) collective-permute-start(bf16[3,256,128]{2,1,0:T(8,128)(2,1)S(1)} %get-tuple-element.16), channel_id=1, source_target_pairs={{0,64},{16,80},{32,96},{48,112},{64,128},{80,144},{96,160},{112,17... | collective-permute-start | bytes 589832 | tf_op jit(solution)/shard_map/ppermute | solution.py:212
  99.1 3.4 %collective-permute-start.8 = (bf16[3,256,128]{2,1,0:T(8,128)(2,1)S(1)}, bf16[3,256,128]{2,1,0:T(8,128)(2,1)S(1)}, u32[]{:S(2)}, u32[]{:S(2)}) collective-permute-start(bf16[3,256,128]{2,1,0:T(8,128)(2,1)S(1)} %get-tuple-element.15), channel_id=1, source_target_pairs={{0,448},{16,464},{32,480},{48,496},{64,0},{80,16},{96,32},{112,48}... | collective-permute-start | bytes 589832 | tf_op jit(solution)/shard_map/ppermute | solution.py:212
  102.6 2.0 %collective-permute-start.9 = (bf16[3,256,128]{2,1,0:T(8,128)(2,1)S(1)}, bf16[3,256,128]{2,1,0:T(8,128)(2,1)S(1)}, u32[]{:S(2)}, u32[]{:S(2)}) collective-permute-start(bf16[3,256,128]{2,1,0:T(8,128)(2,1)S(1)} %get-tuple-element.18), channel_id=1, source_target_pairs={{0,480},{16,496},{32,0},{48,16},{64,32},{80,48},{96,64},{112,80},{... | collective-permute-start | bytes 589832 | tf_op jit(solution)/shard_map/ppermute | solution.py:212
  104.6 1.3 collective-permute-start.12
  105.9 1.3 collective-permute-done.10
  107.2 7.6 %collective-permute-done.11 = bf16[3,256,128]{2,1,0:T(8,128)(2,1)S(1)} collective-permute-done((bf16[3,256,128]{2,1,0:T(8,128)(2,1)S(1)}, bf16[3,256,128]{2,1,0:T(8,128)(2,1)S(1)}, u32[]{:S(2)}, u32[]{:S(2)}) %collective-permute-start.11) | collective-permute-done | bytes 196640 | tf_op jit(solution)/shard_map/ppermute | solution.py:212
  114.8 2.2 %collective-permute-done.9 = bf16[3,256,128]{2,1,0:T(8,128)(2,1)S(1)} collective-permute-done((bf16[3,256,128]{2,1,0:T(8,128)(2,1)S(1)}, bf16[3,256,128]{2,1,0:T(8,128)(2,1)S(1)}, u32[]{:S(2)}, u32[]{:S(2)}) %collective-permute-start.9) | collective-permute-done | bytes 196640 | tf_op jit(solution)/shard_map/ppermute | solution.py:212
  117.1 8.8 %collective-permute-start.13 = (bf16[256,128]{1,0:T(8,128)(2,1)S(1)}, bf16[256,128]{1,0:T(8,128)(2,1)S(1)}, u32[]{:S(2)}, u32[]{:S(2)}) collective-permute-start(bf16[256,128]{1,0:T(8,128)(2,1)S(1)} %get-tuple-element.19), channel_id=1, source_target_pairs={{0,352},{16,368},{32,384},{48,400},{64,416},{80,432},{96,448},{112... | collective-permute-start | bytes 196616 | tf_op jit(solution)/shard_map/ppermute | solution.py:212
  125.9 1.9 collective-permute-start.14
  127.9 0.7 copy-done
  128.5 1.7 shard_map.105
  130.2 17.6 %all-to-all-start.2 = ((bf16[32,16,128]{2,1,0:T(8,128)(2,1)}), bf16[32,16,128]{2,1,0:T(8,128)(2,1)S(1)}, u32[]{:S(2)}, u32[]{:S(2)}) async-start(bf16[32,16,128]{2,1,0:T(8,128)(2,1)} %shard_map.105), calls=%async_computation.2 | async-start | bytes 262144 | tf_op jit(solution)/shard_map/all_to_all | solution.py:206
  147.9 3.1 %collective-permute-start.15 = (bf16[128,128]{1,0:T(8,128)(2,1)S(1)}, bf16[128,128]{1,0:T(8,128)(2,1)S(1)}, u32[]{:S(2)}, u32[]{:S(2)}) collective-permute-start(bf16[128,128]{1,0:T(8,128)(2,1)S(1)} %select_convert_fusion), channel_id=1, source_target_pairs={{0,1},{1,0},{2,3},{3,2},{4,5},{5,4},{6,7},{7,6},{8,9},{9,8},{10,11... | collective-permute-start | bytes 98312 | tf_op jit(solution)/shard_map/ppermute | solution.py:216
  151.0 0.7 copy.14.skip_ref
  151.7 1.1 collective-permute-done.15
  152.9 1.2 abs_reduce_fusion
  154.0 9.6 %all-to-all-done.2 = bf16[32,16,128]{2,1,0:T(8,128)(2,1)S(1)} async-done(((bf16[32,16,128]{2,1,0:T(8,128)(2,1)}), bf16[32,16,128]{2,1,0:T(8,128)(2,1)S(1)}, u32[]{:S(2)}, u32[]{:S(2)}) %all-to-all-start.2) | async-done | bytes 131104 | tf_op jit(solution)/shard_map/all_to_all | solution.py:206
  163.7 0.7 copy-done.1
  164.3 2.9 %shard_map.106 = (f32[128,512]{1,0:T(8,128)}, f32[8,128]{1,0:T(8,128)}) custom-call(bf16[128,512]{1,0:T(8,128)(2,1)} %dy_ref.3, bf16[128,128]{1,0:T(8,128)(2,1)} %b_ref.1, bf16[128,128]{1,0:T(8,128)(2,1)} %c_ref.3, f32[8,128]{1,0:T(8,128)} %decay_ref.3, f32[8,1]{1,0:T(8,128)} %copy.14.skip_ref, bf16[512,128]{1,0:T(8,128)(2,1)} %bitcast.50), custom_call_target="tpu_custom_call" | custom-call | tf_op jit(solution)/shard_map/pallas_call | solution.py:196
  167.2 0.7 compare_select_fusion
  167.9 0.5 fusion.5
  168.5 16.1 %all_to_all.34 = f32[32,1,128]{2,1,0:T(1,128)S(1)} all-to-all(f32[32,1,128]{2,1,0:T(1,128)S(1)} %tile.4), channel_id=1, replica_groups=mesh['z'=16,'c'=2,'y'=4,'xh'=2,'xp'=2] {'z','c'}, dimensions={0} | all-to-all | bytes 32768 | tf_op jit(solution)/shard_map/all_to_all | solution.py:206
  184.6 13.1 %all_to_all.35 = f32[16,1,128]{2,1,0:T(1,128)} all-to-all(f32[16,1,128]{2,1,0:T(1,128)S(1)} %tile.5), channel_id=1, replica_groups=mesh['z'=16,'c'=2,'y'=4,'xh'=2,'xp'=2] {'y','xh','xp'}, dimensions={0} | all-to-all | bytes 16384 | tf_op jit(solution)/shard_map/all_to_all | solution.py:206
  197.7 1.9 shard_map.107
  (27 shorter events, 0.4 us)
Async XLA Ops:
  0.6 5.4 %collective-permute-start = (bf16[128,128]{1,0:T(8,128)(2,1)}, bf16[128,128]{1,0:T(8,128)(2,1)S(1)}, u32[]{:S(2)}, u32[]{:S(2)}) collective-permute-start(bf16[128,128]{1,0:T(8,128)(2,1)} %param.9), channel_id=1, source_target_pairs={{0,1},{1,0},{2,3},{3,2},{4,5},{5,4},{6,7},{7,6},{8,9},{9,8},{10,11... | collective-permute-start | bytes 98312 | tf_op jit(solution)/shard_map/ppermute | solution.py:216
  6.8 29.6 %collective-permute-start.1 = (bf16[256,128]{1,0:T(8,128)(2,1)S(1)}, bf16[256,128]{1,0:T(8,128)(2,1)S(1)}, u32[]{:S(2)}, u32[]{:S(2)}) collective-permute-start(bf16[256,128]{1,0:T(8,128)(2,1)S(1)} %pad_maximum_fusion.1), channel_id=1, source_target_pairs={{0,160},{16,176},{32,192},{48,208},{64,224},{80,240},{96,256},{112... | collective-permute-start | bytes 196616 | tf_op jit(solution)/shard_map/ppermute | solution.py:212
  17.3 19.2 %collective-permute-start.2 = (bf16[256,128]{1,0:T(8,128)(2,1)S(1)}, bf16[256,128]{1,0:T(8,128)(2,1)S(1)}, u32[]{:S(2)}, u32[]{:S(2)}) collective-permute-start(bf16[256,128]{1,0:T(8,128)(2,1)S(1)} %pad_maximum_fusion.1), channel_id=1, source_target_pairs={{0,352},{16,368},{32,384},{48,400},{64,416},{80,432},{96,448},{112... | collective-permute-start | bytes 196616 | tf_op jit(solution)/shard_map/ppermute | solution.py:212
  25.7 24.0 %collective-permute-start.7 = (bf16[256,128]{1,0:T(8,128)(2,1)S(1)}, bf16[256,128]{1,0:T(8,128)(2,1)S(1)}, u32[]{:S(2)}, u32[]{:S(2)}) collective-permute-start(bf16[256,128]{1,0:T(8,128)(2,1)S(1)} %pad_maximum_fusion.1), channel_id=1, source_target_pairs={{0,256},{16,272},{32,288},{48,304},{64,320},{80,336},{96,352},{112... | collective-permute-start | bytes 196616 | tf_op jit(solution)/shard_map/ppermute | solution.py:212
  36.5 21.0 %collective-permute-start.3 = (bf16[768,128]{1,0:T(8,128)(2,1)S(1)}, bf16[768,128]{1,0:T(8,128)(2,1)S(1)}, u32[]{:S(2)}, u32[]{:S(2)}) collective-permute-start(bf16[768,128]{1,0:T(8,128)(2,1)S(1)} %pad_maximum_fusion), channel_id=1, source_target_pairs={{0,64},{16,80},{32,96},{48,112},{64,128},{80,144},{96,160},{112,17... | collective-permute-start | bytes 589832 | tf_op jit(solution)/shard_map/ppermute | solution.py:212
  39.0 20.7 %collective-permute-start.4 = (bf16[768,128]{1,0:T(8,128)(2,1)S(1)}, bf16[768,128]{1,0:T(8,128)(2,1)S(1)}, u32[]{:S(2)}, u32[]{:S(2)}) collective-permute-start(bf16[768,128]{1,0:T(8,128)(2,1)S(1)} %pad_maximum_fusion), channel_id=1, source_target_pairs={{0,32},{16,48},{32,64},{48,80},{64,96},{80,112},{96,128},{112,144}... | collective-permute-start | bytes 589832 | tf_op jit(solution)/shard_map/ppermute | solution.py:212
  42.1 19.8 %collective-permute-start.5 = (bf16[768,128]{1,0:T(8,128)(2,1)S(1)}, bf16[768,128]{1,0:T(8,128)(2,1)S(1)}, u32[]{:S(2)}, u32[]{:S(2)}) collective-permute-start(bf16[768,128]{1,0:T(8,128)(2,1)S(1)} %pad_maximum_fusion), channel_id=1, source_target_pairs={{0,480},{16,496},{32,0},{48,16},{64,32},{80,48},{96,64},{112,80},{... | collective-permute-start | bytes 589832 | tf_op jit(solution)/shard_map/ppermute | solution.py:212
  45.5 18.6 %collective-permute-start.6 = (bf16[768,128]{1,0:T(8,128)(2,1)S(1)}, bf16[768,128]{1,0:T(8,128)(2,1)S(1)}, u32[]{:S(2)}, u32[]{:S(2)}) collective-permute-start(bf16[768,128]{1,0:T(8,128)(2,1)S(1)} %pad_maximum_fusion), channel_id=1, source_target_pairs={{0,448},{16,464},{32,480},{48,496},{64,0},{80,16},{96,32},{112,48}... | collective-permute-start | bytes 589832 | tf_op jit(solution)/shard_map/ppermute | solution.py:212
  78.8 49.0 %all-to-all-start.1 = ((bf16[32,24,128]{2,1,0:T(8,128)(2,1)}), bf16[32,24,128]{2,1,0:T(8,128)(2,1)S(1)}, u32[]{:S(2)}, u32[]{:S(2)}) async-start(bf16[32,24,128]{2,1,0:T(8,128)(2,1)} %shard_map.104), calls=%async_computation.1 | async-start | bytes 393216 | tf_op jit(solution)/shard_map/all_to_all | solution.py:206
  91.8 59.2 %copy-start.2 = (f32[8]{0:T(128)S(1)}, f32[8]{0:T(128)}, u32[]{:S(2)}) copy-start(f32[8]{0:T(128)} %param.15) | copy-start | bytes 100
  91.9 15.3 %collective-permute-start.10 = (bf16[3,256,128]{2,1,0:T(8,128)(2,1)S(1)}, bf16[3,256,128]{2,1,0:T(8,128)(2,1)S(1)}, u32[]{:S(2)}, u32[]{:S(2)}) collective-permute-start(bf16[3,256,128]{2,1,0:T(8,128)(2,1)S(1)} %get-tuple-element.17), channel_id=1, source_target_pairs={{0,32},{16,48},{32,64},{48,80},{64,96},{80,112},{96,128},{112,144}... | collective-permute-start | bytes 589832 | tf_op jit(solution)/shard_map/ppermute | solution.py:212
  95.1 19.6 %collective-permute-start.11 = (bf16[3,256,128]{2,1,0:T(8,128)(2,1)S(1)}, bf16[3,256,128]{2,1,0:T(8,128)(2,1)S(1)}, u32[]{:S(2)}, u32[]{:S(2)}) collective-permute-start(bf16[3,256,128]{2,1,0:T(8,128)(2,1)S(1)} %get-tuple-element.16), channel_id=1, source_target_pairs={{0,64},{16,80},{32,96},{48,112},{64,128},{80,144},{96,160},{112,17... | collective-permute-start | bytes 589832 | tf_op jit(solution)/shard_map/ppermute | solution.py:212
  99.1 15.6 %collective-permute-start.8 = (bf16[3,256,128]{2,1,0:T(8,128)(2,1)S(1)}, bf16[3,256,128]{2,1,0:T(8,128)(2,1)S(1)}, u32[]{:S(2)}, u32[]{:S(2)}) collective-permute-start(bf16[3,256,128]{2,1,0:T(8,128)(2,1)S(1)} %get-tuple-element.15), channel_id=1, source_target_pairs={{0,448},{16,464},{32,480},{48,496},{64,0},{80,16},{96,32},{112,48}... | collective-permute-start | bytes 589832 | tf_op jit(solution)/shard_map/ppermute | solution.py:212
  102.6 14.4 %collective-permute-start.9 = (bf16[3,256,128]{2,1,0:T(8,128)(2,1)S(1)}, bf16[3,256,128]{2,1,0:T(8,128)(2,1)S(1)}, u32[]{:S(2)}, u32[]{:S(2)}) collective-permute-start(bf16[3,256,128]{2,1,0:T(8,128)(2,1)S(1)} %get-tuple-element.18), channel_id=1, source_target_pairs={{0,480},{16,496},{32,0},{48,16},{64,32},{80,48},{96,64},{112,80},{... | collective-permute-start | bytes 589832 | tf_op jit(solution)/shard_map/ppermute | solution.py:212
  104.6 43.2 %collective-permute-start.12 = (bf16[256,128]{1,0:T(8,128)(2,1)S(1)}, bf16[256,128]{1,0:T(8,128)(2,1)S(1)}, u32[]{:S(2)}, u32[]{:S(2)}) collective-permute-start(bf16[256,128]{1,0:T(8,128)(2,1)S(1)} %slice_bitcast_fusion.7), channel_id=1, source_target_pairs={{256,0},{272,16},{288,32},{304,48},{320,64},{336,80},{352,96},{368... | collective-permute-start | bytes 196616 | tf_op jit(solution)/shard_map/ppermute | solution.py:212
  117.1 30.7 %collective-permute-start.13 = (bf16[256,128]{1,0:T(8,128)(2,1)S(1)}, bf16[256,128]{1,0:T(8,128)(2,1)S(1)}, u32[]{:S(2)}, u32[]{:S(2)}) collective-permute-start(bf16[256,128]{1,0:T(8,128)(2,1)S(1)} %get-tuple-element.19), channel_id=1, source_target_pairs={{0,352},{16,368},{32,384},{48,400},{64,416},{80,432},{96,448},{112... | collective-permute-start | bytes 196616 | tf_op jit(solution)/shard_map/ppermute | solution.py:212
  125.9 21.9 %collective-permute-start.14 = (bf16[256,128]{1,0:T(8,128)(2,1)S(1)}, bf16[256,128]{1,0:T(8,128)(2,1)S(1)}, u32[]{:S(2)}, u32[]{:S(2)}) collective-permute-start(bf16[256,128]{1,0:T(8,128)(2,1)S(1)} %get-tuple-element.20), channel_id=1, source_target_pairs={{0,160},{16,176},{32,192},{48,208},{64,224},{80,240},{96,256},{112... | collective-permute-start | bytes 196616 | tf_op jit(solution)/shard_map/ppermute | solution.py:212
  127.9 0.7 copy-start
  130.2 33.5 %all-to-all-start.2 = ((bf16[32,16,128]{2,1,0:T(8,128)(2,1)}), bf16[32,16,128]{2,1,0:T(8,128)(2,1)S(1)}, u32[]{:S(2)}, u32[]{:S(2)}) async-start(bf16[32,16,128]{2,1,0:T(8,128)(2,1)} %shard_map.105), calls=%async_computation.2 | async-start | bytes 262144 | tf_op jit(solution)/shard_map/all_to_all | solution.py:206
  147.9 5.0 %collective-permute-start.15 = (bf16[128,128]{1,0:T(8,128)(2,1)S(1)}, bf16[128,128]{1,0:T(8,128)(2,1)S(1)}, u32[]{:S(2)}, u32[]{:S(2)}) collective-permute-start(bf16[128,128]{1,0:T(8,128)(2,1)S(1)} %select_convert_fusion), channel_id=1, source_target_pairs={{0,1},{1,0},{2,3},{3,2},{4,5},{5,4},{6,7},{7,6},{8,9},{9,8},{10,11... | collective-permute-start | bytes 98312 | tf_op jit(solution)/shard_map/ppermute | solution.py:216
  163.7 0.7 copy-start.1

commit v4 on v3

--- a/solution.py
+++ b/solution.py
@@ -9,9 +9,9 @@
 from jax.sharding import PartitionSpec as P
 
 
-SEQ = ("z", "c")
+SEQ = ("hi", "lo", "c")
 HEAD = ("y", "xh", "xp")
-SIZES = (16, 2, 4, 2, 2)
+SIZES = (4, 4, 2, 4, 2, 2)
 NEAR = (-2, -1, 0, 1, 2)
 CHIPS = 16
 TOK = 128
@@ -56,9 +56,10 @@
         for z in (2 * j, 2 * j + 1):
             k = lax.rem(z - chip + 7 + CHIPS, CHIPS)
             near, far = lax.rem(k, 5), k // 5
+            rel = lax.rem(lax.rem(z, 4) - lax.rem(chip, 4) + 4, 4)
             for c in range(2):
                 held = jnp.where(k == 15, 60 + 2 * c, 12 * near + 6 * c + 2 * far)
-                yield held, 2 * CHIPS * c + 2 * jnp.where(k == 15, 15, 3 * near + far)
+                yield held, 2 * CHIPS * c + 8 * rel + 2 * (z // 4)
 
     def rows_at(j):
         return pl.ds(pl.multiple_of(j * 4 * TOK, 4 * TOK), 4 * TOK)
@@ -212,6 +213,11 @@
     return lax.ppermute(x, SEQ, route)
 
 
+def along_z_two(x):
+    route = [(2 * z + c, 2 * ((z + 2 - 4 * c) % CHIPS) + c) for z in range(CHIPS) for c in range(2)]
+    return lax.ppermute(x, SEQ, route)
+
+
 def swap_pair(x):
     return lax.ppermute(x, "xp", [(0, 1), (1, 0)])
 
@@ -225,7 +231,7 @@
 
 def step(queries, key_value, grad_out, ssm_grad, b_proj, c_proj, decay_log, skip_gain):
     keys_here = lax.axis_index("xp") == 0
-    pos = jnp.stack([lax.axis_index("z"), lax.axis_index("c")]).astype(jnp.int32)
+    pos = jnp.stack([lax.axis_index(("hi", "lo")), lax.axis_index("c")]).astype(jnp.int32)
     struct = jax.ShapeDtypeStruct
 
     other = swap_pair(key_value)
@@ -267,20 +273,15 @@
         raw=6,
     )
 
-    both = swap_all(dkv.reshape(2 * 4096, 128), "c").reshape(2, CHIPS, 2 * TOK, 128).astype(f32)
+    both = swap_all(dkv.reshape(2 * 4096, 128), "c").reshape(2, 4, 1024, 128).astype(f32)
     chip_sum = (both[0] + both[1]).astype(bf16)
-    parts = [chip_sum[6:9].astype(f32)]
-    for k, d in enumerate(NEAR):
-        if d:
-            parts.append(along_z(chip_sum[3 * k : 3 * k + 3], d).astype(f32))
-    three = (((parts[0] + parts[1]) + (parts[2] + parts[3])) + parts[4]).astype(bf16)
-    from_above = along_z(three[0], -5)
-    from_below = along_z(three[2], 5)
-    from_across = along_z(chip_sum[15], -8, 8)
-    own = (three[1].astype(f32) + from_across.astype(f32)) + (from_above.astype(f32) + from_below.astype(f32))
-    mine = jnp.where(keys_here, own[:TOK], own[TOK:])
-    other = jnp.where(keys_here, own[TOK:], own[:TOK]).astype(bf16)
-    other = swap_pair(other)
+    from_two = along_z_two(chip_sum[2])
+    from_before = along_z(chip_sum[1], 1)
+    from_after = along_z(chip_sum[3], -1)
+    near = (
+        (chip_sum[0].astype(f32) + from_before.astype(f32)) + (from_after.astype(f32) + from_two.astype(f32))
+    ).astype(bf16)
+    far = swap_all(near, ("hi", "xp")).reshape(8, TOK, 128)
     dx, peak_x = call(
         ssm_kernel,
         (struct((TOK, 512), f32), struct((8, 128), f32)),
@@ -292,7 +293,7 @@
         flow.reshape(512, 128),
     )
 
-    dkv_own = mine + other.astype(f32)
+    dkv_own = jnp.sum(far.astype(f32), axis=0)
     lane = lax.broadcasted_iota(jnp.int32, (1, 128), 1)
     early = jnp.where(lane == 0, peak_q[:1], peak_x[:1])
     early = lax.optimization_barrier(early)

time: 201 us -> 192 us (0.955)
  starting transfers between devices: 101 us -> 76.6 us
  waiting for transfers between devices: 23.3 us -> 32.1 us
  blocking collectives: 52.3 us -> 60.7 us
    all_to_all x2 -> x3, waiting for transfers between devices: 9.61 us -> 30.5 us  [swap_all(): return lax.all_to_all(x, axes, 0, 0, tiled=True)]
    ppermute x14 -> x9, starting transfers between devices: 64.3 us -> 46.1 us  [along_z(): return lax.ppermute(x, SEQ, route)]
    ppermute x14 -> x9, waiting for transfers between devices: 11.1 us -> 0.02 us  [along_z(): return lax.ppermute(x, SEQ, route)]
    all_to_all x2 -> x3, starting transfers between devices: 30.1 us -> 21.1 us  [swap_all(): return lax.all_to_all(x, axes, 0, 0, tiled=True)]
    all_to_all x3, blocking collectives: 35.8 us -> 44.2 us  [swap_all(): return lax.all_to_all(x, axes, 0, 0, tiled=True)]
    ppermute x0 -> x1, starting transfers between devices: none -> 5.45 us  [along_z_two(): return lax.ppermute(x, SEQ, route)]
    ppermute x2 -> x1, starting transfers between devices: 7.05 us -> 3.94 us  [swap_pair(): return lax.ppermute(x, 'xp', [(0, 1), (1, 0)])]
  transfers between devices with their start and end apart: 18 -> 14, of which waited for: 6 -> 4; matrix products, arithmetic and copies ran while one was open for 2% -> 2% of each run, Pallas kernels for 2% -> 4%
where the time goes in v4:
time: 192 us; the launch traced here: 191 us
  starting transfers between devices  76.6 us (40%)
  blocking collectives  60.7 us (32%)
  waiting for transfers between devices  32.1 us (17%)
  Pallas kernels  14.9 us (8%)
  other arithmetic  4.72 us (2%)
    ppermute x9, starting transfers between devices, along_z(): return lax.ppermute(x, SEQ, route)  46.1 us
    all_to_all x3, blocking collectives, swap_all(): return lax.all_to_all(x, axes, 0, 0, tiled=True)  44.2 us
    all_to_all x3, waiting for transfers between devices, swap_all(): return lax.all_to_all(x, axes, 0, 0, tiled=True)  30.5 us
    all_to_all x3, starting transfers between devices, swap_all(): return lax.all_to_all(x, axes, 0, 0, tiled=True)  21.1 us
    all_gather x6, blocking collectives, step(): lax.all_gather(piece, 'c', axis=0, tiled=True).reshape(-1, TOK, 128)  16.5 us
    pallas_call x5, Pallas kernels, call(): pl.pallas_call(body, out_shape=out_shape, in_specs=specs, out_specs=jax.t...  14.9 us
    ppermute x1, starting transfers between devices, along_z_two(): return lax.ppermute(x, SEQ, route)  5.45 us
    ppermute x1, starting transfers between devices, swap_pair(): return lax.ppermute(x, 'xp', [(0, 1), (1, 0)])  3.94 us
  transfers between devices with their start and end apart: 14, of which 4 were waited for; matrix products, arithmetic and copies ran while one was open for 2% of the time, Pallas kernels for 4%

profile of v4, /device:TPU:1, one launch (start us, length us, event | category | flops | bytes accessed | tf_op | source)
XLA Modules:
  0.0 191.3 jit_solution(11522058432535850626)
XLA Ops:
  0.6 3.9 %collective-permute-start = (bf16[128,128]{1,0:T(8,128)(2,1)}, bf16[128,128]{1,0:T(8,128)(2,1)S(1)}, u32[]{:S(2)}, u32[]{:S(2)}) collective-permute-start(bf16[128,128]{1,0:T(8,128)(2,1)} %param.9), channel_id=1, source_target_pairs={{0,1},{1,0},{2,3},{3,2},{4,5},{5,4},{6,7},{7,6},{8,9},{9,8},{10,11... | collective-permute-start | bytes 98312 | tf_op jit(solution)/shard_map/ppermute | solution.py:222
  4.6 1.5 collective-permute-done
  6.1 0.8 broadcast_select_fusion.1
  6.8 10.4 %collective-permute-start.1 = (bf16[256,128]{1,0:T(8,128)(2,1)S(1)}, bf16[256,128]{1,0:T(8,128)(2,1)S(1)}, u32[]{:S(2)}, u32[]{:S(2)}) collective-permute-start(bf16[256,128]{1,0:T(8,128)(2,1)S(1)} %pad_maximum_fusion.1), channel_id=1, source_target_pairs={{0,160},{16,176},{32,192},{48,208},{64,224},{80,240},{96,256},{112... | collective-permute-start | bytes 196616 | tf_op jit(solution)/shard_map/ppermute | solution.py:213
  17.3 5.9 %collective-permute-start.2 = (bf16[256,128]{1,0:T(8,128)(2,1)S(1)}, bf16[256,128]{1,0:T(8,128)(2,1)S(1)}, u32[]{:S(2)}, u32[]{:S(2)}) collective-permute-start(bf16[256,128]{1,0:T(8,128)(2,1)S(1)} %pad_maximum_fusion.1), channel_id=1, source_target_pairs={{0,352},{16,368},{32,384},{48,400},{64,416},{80,432},{96,448},{112... | collective-permute-start | bytes 196616 | tf_op jit(solution)/shard_map/ppermute | solution.py:213
  23.1 2.6 %shard_map.104 = bf16[32,24,128]{2,1,0:T(8,128)(2,1)} custom-call(bf16[128,512]{1,0:T(8,128)(2,1)} %dy_ref.3, bf16[128,128]{1,0:T(8,128)(2,1)} %c_ref.3, f32[8,128]{1,0:T(8,128)} %decay_ref.3), custom_call_target="tpu_custom_call" | custom-call | tf_op jit(solution)/shard_map/pallas_call | solution.py:197
  25.7 10.7 %collective-permute-start.7 = (bf16[256,128]{1,0:T(8,128)(2,1)S(1)}, bf16[256,128]{1,0:T(8,128)(2,1)S(1)}, u32[]{:S(2)}, u32[]{:S(2)}) collective-permute-start(bf16[256,128]{1,0:T(8,128)(2,1)S(1)} %pad_maximum_fusion.1), channel_id=1, source_target_pairs={{0,256},{16,272},{32,288},{48,304},{64,320},{80,336},{96,352},{112... | collective-permute-start | bytes 196616 | tf_op jit(solution)/shard_map/ppermute | solution.py:213
  36.5 0.0 collective-permute-done.2
  36.5 1.9 %collective-permute-start.3 = (bf16[768,128]{1,0:T(8,128)(2,1)S(1)}, bf16[768,128]{1,0:T(8,128)(2,1)S(1)}, u32[]{:S(2)}, u32[]{:S(2)}) collective-permute-start(bf16[768,128]{1,0:T(8,128)(2,1)S(1)} %pad_maximum_fusion), channel_id=1, source_target_pairs={{0,64},{16,80},{32,96},{48,112},{64,128},{80,144},{96,160},{112,17... | collective-permute-start | bytes 589832 | tf_op jit(solution)/shard_map/ppermute | solution.py:213
  38.4 0.6 pad_add_fusion.pos_ref
  39.0 3.1 %collective-permute-start.4 = (bf16[768,128]{1,0:T(8,128)(2,1)S(1)}, bf16[768,128]{1,0:T(8,128)(2,1)S(1)}, u32[]{:S(2)}, u32[]{:S(2)}) collective-permute-start(bf16[768,128]{1,0:T(8,128)(2,1)S(1)} %pad_maximum_fusion), channel_id=1, source_target_pairs={{0,32},{16,48},{32,64},{48,80},{64,96},{80,112},{96,128},{112,144}... | collective-permute-start | bytes 589832 | tf_op jit(solution)/shard_map/ppermute | solution.py:213
  42.1 3.4 %collective-permute-start.5 = (bf16[768,128]{1,0:T(8,128)(2,1)S(1)}, bf16[768,128]{1,0:T(8,128)(2,1)S(1)}, u32[]{:S(2)}, u32[]{:S(2)}) collective-permute-start(bf16[768,128]{1,0:T(8,128)(2,1)S(1)} %pad_maximum_fusion), channel_id=1, source_target_pairs={{0,480},{16,496},{32,0},{48,16},{64,32},{80,48},{96,64},{112,80},{... | collective-permute-start | bytes 589832 | tf_op jit(solution)/shard_map/ppermute | solution.py:213
  45.5 4.3 %collective-permute-start.6 = (bf16[768,128]{1,0:T(8,128)(2,1)S(1)}, bf16[768,128]{1,0:T(8,128)(2,1)S(1)}, u32[]{:S(2)}, u32[]{:S(2)}) collective-permute-start(bf16[768,128]{1,0:T(8,128)(2,1)S(1)} %pad_maximum_fusion), channel_id=1, source_target_pairs={{0,448},{16,464},{32,480},{48,496},{64,0},{80,16},{96,32},{112,48}... | collective-permute-start | bytes 589832 | tf_op jit(solution)/shard_map/ppermute | solution.py:213
  49.8 0.0 collective-permute-done.7
  49.8 5.5 %all_gather.23 = bf16[512,128]{1,0:T(8,128)(2,1)} all-gather(bf16[256,128]{1,0:T(8,128)(2,1)S(1)} %collective-permute-done.7), channel_id=1, replica_groups=mesh['hi'=4,'lo'=4,'c'=2,'y'=4,'xh'=2,'xp'=2] {'c'}, dimensions={0}, use_global_device_ids=true | all-gather | bytes 196608 | tf_op jit(solution)/shard_map/all_gather | solution.py:256
  55.2 2.2 %all_gather.20 = bf16[1536,128]{1,0:T(8,128)(2,1)} all-gather(bf16[768,128]{1,0:T(8,128)(2,1)S(1)} %pad_maximum_fusion), channel_id=1, replica_groups=mesh['hi'=4,'lo'=4,'c'=2,'y'=4,'xh'=2,'xp'=2] {'c'}, dimensions={0}, use_global_device_ids=true | all-gather | bytes 589824 | tf_op jit(solution)/shard_map/all_gather | solution.py:256
  57.5 0.0 collective-permute-done.3
  57.5 2.2 %all_gather.18 = bf16[1536,128]{1,0:T(8,128)(2,1)} all-gather(bf16[768,128]{1,0:T(8,128)(2,1)S(1)} %collective-permute-done.3), channel_id=1, replica_groups=mesh['hi'=4,'lo'=4,'c'=2,'y'=4,'xh'=2,'xp'=2] {'c'}, dimensions={0}, use_global_device_ids=true | all-gather | bytes 589824 | tf_op jit(solution)/shard_map/all_gather | solution.py:256
  59.7 0.0 collective-permute-done.4
  59.7 2.2 %all_gather.19 = bf16[1536,128]{1,0:T(8,128)(2,1)} all-gather(bf16[768,128]{1,0:T(8,128)(2,1)S(1)} %collective-permute-done.4), channel_id=1, replica_groups=mesh['hi'=4,'lo'=4,'c'=2,'y'=4,'xh'=2,'xp'=2] {'c'}, dimensions={0}, use_global_device_ids=true | all-gather | bytes 589824 | tf_op jit(solution)/shard_map/all_gather | solution.py:256
  61.9 2.2 %all_gather.21 = bf16[1536,128]{1,0:T(8,128)(2,1)} all-gather(bf16[768,128]{1,0:T(8,128)(2,1)S(1)} %collective-permute-done.5), channel_id=1, replica_groups=mesh['hi'=4,'lo'=4,'c'=2,'y'=4,'xh'=2,'xp'=2] {'c'}, dimensions={0}, use_global_device_ids=true | all-gather | bytes 589824 | tf_op jit(solution)/shard_map/all_gather | solution.py:256
  64.1 2.2 %all_gather.22 = bf16[1536,128]{1,0:T(8,128)(2,1)} all-gather(bf16[768,128]{1,0:T(8,128)(2,1)S(1)} %collective-permute-done.6), channel_id=1, replica_groups=mesh['hi'=4,'lo'=4,'c'=2,'y'=4,'xh'=2,'xp'=2] {'c'}, dimensions={0}, use_global_device_ids=true | all-gather | bytes 589824 | tf_op jit(solution)/shard_map/all_gather | solution.py:256
  66.3 5.9 %shard_map.103 = (f32[128,512]{1,0:T(8,128)}, bf16[64,128,128]{2,1,0:T(8,128)(2,1)}, f32[8,128]{1,0:T(8,128)}) custom-call(s32[2]{0:T(128)} %pad_add_fusion.pos_ref, bf16[128,512]{1,0:T(8,128)(2,1)} %q_ref.1, bf16[128,512]{1,0:T(8,128)(2,1)} %do_ref.1, bf16[12,128,128]{2,1,0:T(8,128)(2,1)} %bitcast.32, bf16[12,128,128]{2,1,0:T(8,128)(2,1)} %bitcast.33, ...), custom_call_target="tpu_custom_call" | custom-call | tf_op jit(solution)/shard_map/pallas_call | solution.py:197
  72.2 6.6 %all_to_all.42 = bf16[2,4096,128]{2,1,0:T(8,128)(2,1)S(1)} all-to-all(bf16[2,4096,128]{2,1,0:T(8,128)(2,1)} %bitcast.30), channel_id=1, replica_groups=mesh['hi'=4,'lo'=4,'c'=2,'y'=4,'xh'=2,'xp'=2] {'c'}, dimensions={0} | all-to-all | bytes 4194304 | tf_op jit(solution)/shard_map/all_to_all | solution.py:207
  78.8 12.5 %all-to-all-start.2 = ((bf16[32,24,128]{2,1,0:T(8,128)(2,1)}), bf16[32,24,128]{2,1,0:T(8,128)(2,1)S(1)}, u32[]{:S(2)}, u32[]{:S(2)}) async-start(bf16[32,24,128]{2,1,0:T(8,128)(2,1)} %shard_map.104), calls=%async_computation.2 | async-start | bytes 393216 | tf_op jit(solution)/shard_map/all_to_all | solution.py:207
  91.4 0.3 convert_element_type.33
  91.6 0.2 fusion
  91.8 0.0 copy-start.3
  91.9 0.1 slice_bitcast_fusion.2
  91.9 5.4 %collective-permute-start.10 = (bf16[1024,128]{1,0:T(8,128)(2,1)S(1)}, bf16[1024,128]{1,0:T(8,128)(2,1)S(1)}, u32[]{:S(2)}, u32[]{:S(2)}) collective-permute-start(bf16[1024,128]{1,0:T(8,128)(2,1)S(1)} %get-tuple-element.14), channel_id=1, source_target_pairs={{0,64},{16,464},{32,96},{48,496},{64,128},{80,16},{96,160},{112,48... | collective-permute-start | bytes 786440 | tf_op jit(solution)/shard_map/ppermute | solution.py:218
  97.4 2.2 %collective-permute-start.8 = (bf16[1024,128]{1,0:T(8,128)(2,1)S(1)}, bf16[1024,128]{1,0:T(8,128)(2,1)S(1)}, u32[]{:S(2)}, u32[]{:S(2)}) collective-permute-start(bf16[1024,128]{1,0:T(8,128)(2,1)S(1)} %get-tuple-element.13), channel_id=1, source_target_pairs={{0,32},{16,48},{32,64},{48,80},{64,96},{80,112},{96,128},{112,144}... | collective-permute-start | bytes 786440 | tf_op jit(solution)/shard_map/ppermute | solution.py:213
  99.6 4.3 %collective-permute-start.9 = (bf16[1024,128]{1,0:T(8,128)(2,1)S(1)}, bf16[1024,128]{1,0:T(8,128)(2,1)S(1)}, u32[]{:S(2)}, u32[]{:S(2)}) collective-permute-start(bf16[1024,128]{1,0:T(8,128)(2,1)S(1)} %get-tuple-element.15), channel_id=1, source_target_pairs={{0,480},{16,496},{32,0},{48,16},{64,32},{80,48},{96,64},{112,80},{... | collective-permute-start | bytes 786440 | tf_op jit(solution)/shard_map/ppermute | solution.py:213
  103.9 6.3 %all-to-all-done.2.state_ref = bf16[32,24,128]{2,1,0:T(8,128)(2,1)S(1)} async-done(((bf16[32,24,128]{2,1,0:T(8,128)(2,1)}), bf16[32,24,128]{2,1,0:T(8,128)(2,1)S(1)}, u32[]{:S(2)}, u32[]{:S(2)}) %all-to-all-start.2) | async-done | bytes 196640 | tf_op jit(solution)/shard_map/all_to_all | solution.py:207
  110.2 0.7 copy-done
  110.8 1.7 shard_map.105
  112.5 5.1 %all-to-all-start.3 = ((bf16[32,16,128]{2,1,0:T(8,128)(2,1)}), bf16[32,16,128]{2,1,0:T(8,128)(2,1)S(1)}, u32[]{:S(2)}, u32[]{:S(2)}) async-start(bf16[32,16,128]{2,1,0:T(8,128)(2,1)} %shard_map.105), calls=%async_computation.3 | async-start | bytes 262144 | tf_op jit(solution)/shard_map/all_to_all | solution.py:207
  117.7 0.8 fusion.2
  118.5 15.3 %all-to-all-done.3 = bf16[32,16,128]{2,1,0:T(8,128)(2,1)S(1)} async-done(((bf16[32,16,128]{2,1,0:T(8,128)(2,1)}), bf16[32,16,128]{2,1,0:T(8,128)(2,1)S(1)}, u32[]{:S(2)}, u32[]{:S(2)}) %all-to-all-start.3) | async-done | bytes 131104 | tf_op jit(solution)/shard_map/all_to_all | solution.py:207
  133.8 3.4 %all-to-all-start.1 = ((bf16[8,128,128]{2,1,0:T(8,128)(2,1)}), bf16[8,128,128]{2,1,0:T(8,128)(2,1)S(1)}, u32[]{:S(2)}, u32[]{:S(2)}) async-start(bf16[8,128,128]{2,1,0:T(8,128)(2,1)} %bitcast.14), calls=%async_computation.1 | async-start | bytes 524288 | tf_op jit(solution)/shard_map/all_to_all | solution.py:207
  137.3 0.7 copy.14.skip_ref
  137.9 2.9 %shard_map.106 = (f32[128,512]{1,0:T(8,128)}, f32[8,128]{1,0:T(8,128)}) custom-call(bf16[128,512]{1,0:T(8,128)(2,1)} %dy_ref.3, bf16[128,128]{1,0:T(8,128)(2,1)} %b_ref.1, bf16[128,128]{1,0:T(8,128)(2,1)} %c_ref.3, f32[8,128]{1,0:T(8,128)} %decay_ref.3, f32[8,1]{1,0:T(8,128)} %copy.14.skip_ref, bf16[512,128]{1,0:T(8,128)(2,1)} %bitcast.37), custom_call_target="tpu_custom_call" | custom-call | tf_op jit(solution)/shard_map/pallas_call | solution.py:197
  140.8 0.7 compare_select_fusion
  141.6 8.9 %all-to-all-done.1 = bf16[8,128,128]{2,1,0:T(8,128)(2,1)S(1)} async-done(((bf16[8,128,128]{2,1,0:T(8,128)(2,1)}), bf16[8,128,128]{2,1,0:T(8,128)(2,1)S(1)}, u32[]{:S(2)}, u32[]{:S(2)}) %all-to-all-start.1) | async-done | bytes 262176 | tf_op jit(solution)/shard_map/all_to_all | solution.py:207
  150.5 0.6 abs_reduce_fusion
  151.1 0.6 fusion.3
  151.8 24.5 %all_to_all.43 = f32[32,1,128]{2,1,0:T(1,128)S(1)} all-to-all(f32[32,1,128]{2,1,0:T(1,128)S(1)} %tile.4), channel_id=1, replica_groups=mesh['hi'=4,'lo'=4,'c'=2,'y'=4,'xh'=2,'xp'=2] {'hi','lo','c'}, dimensions={0} | all-to-all | bytes 32768 | tf_op jit(solution)/shard_map/all_to_all | solution.py:207
  176.4 13.0 %all_to_all.44 = f32[16,1,128]{2,1,0:T(1,128)} all-to-all(f32[16,1,128]{2,1,0:T(1,128)S(1)} %tile.5), channel_id=1, replica_groups=mesh['hi'=4,'lo'=4,'c'=2,'y'=4,'xh'=2,'xp'=2] {'y','xh','xp'}, dimensions={0} | all-to-all | bytes 16384 | tf_op jit(solution)/shard_map/all_to_all | solution.py:207
  189.4 1.9 shard_map.107
  (18 shorter events, 0.1 us)
Async XLA Ops:
  0.6 5.4 %collective-permute-start = (bf16[128,128]{1,0:T(8,128)(2,1)}, bf16[128,128]{1,0:T(8,128)(2,1)S(1)}, u32[]{:S(2)}, u32[]{:S(2)}) collective-permute-start(bf16[128,128]{1,0:T(8,128)(2,1)} %param.9), channel_id=1, source_target_pairs={{0,1},{1,0},{2,3},{3,2},{4,5},{5,4},{6,7},{7,6},{8,9},{9,8},{10,11... | collective-permute-start | bytes 98312 | tf_op jit(solution)/shard_map/ppermute | solution.py:222
  6.8 29.6 %collective-permute-start.1 = (bf16[256,128]{1,0:T(8,128)(2,1)S(1)}, bf16[256,128]{1,0:T(8,128)(2,1)S(1)}, u32[]{:S(2)}, u32[]{:S(2)}) collective-permute-start(bf16[256,128]{1,0:T(8,128)(2,1)S(1)} %pad_maximum_fusion.1), channel_id=1, source_target_pairs={{0,160},{16,176},{32,192},{48,208},{64,224},{80,240},{96,256},{112... | collective-permute-start | bytes 196616 | tf_op jit(solution)/shard_map/ppermute | solution.py:213
  17.3 19.2 %collective-permute-start.2 = (bf16[256,128]{1,0:T(8,128)(2,1)S(1)}, bf16[256,128]{1,0:T(8,128)(2,1)S(1)}, u32[]{:S(2)}, u32[]{:S(2)}) collective-permute-start(bf16[256,128]{1,0:T(8,128)(2,1)S(1)} %pad_maximum_fusion.1), channel_id=1, source_target_pairs={{0,352},{16,368},{32,384},{48,400},{64,416},{80,432},{96,448},{112... | collective-permute-start | bytes 196616 | tf_op jit(solution)/shard_map/ppermute | solution.py:213
  25.7 24.0 %collective-permute-start.7 = (bf16[256,128]{1,0:T(8,128)(2,1)S(1)}, bf16[256,128]{1,0:T(8,128)(2,1)S(1)}, u32[]{:S(2)}, u32[]{:S(2)}) collective-permute-start(bf16[256,128]{1,0:T(8,128)(2,1)S(1)} %pad_maximum_fusion.1), channel_id=1, source_target_pairs={{0,256},{16,272},{32,288},{48,304},{64,320},{80,336},{96,352},{112... | collective-permute-start | bytes 196616 | tf_op jit(solution)/shard_map/ppermute | solution.py:213
  36.5 21.0 %collective-permute-start.3 = (bf16[768,128]{1,0:T(8,128)(2,1)S(1)}, bf16[768,128]{1,0:T(8,128)(2,1)S(1)}, u32[]{:S(2)}, u32[]{:S(2)}) collective-permute-start(bf16[768,128]{1,0:T(8,128)(2,1)S(1)} %pad_maximum_fusion), channel_id=1, source_target_pairs={{0,64},{16,80},{32,96},{48,112},{64,128},{80,144},{96,160},{112,17... | collective-permute-start | bytes 589832 | tf_op jit(solution)/shard_map/ppermute | solution.py:213
  39.0 20.7 %collective-permute-start.4 = (bf16[768,128]{1,0:T(8,128)(2,1)S(1)}, bf16[768,128]{1,0:T(8,128)(2,1)S(1)}, u32[]{:S(2)}, u32[]{:S(2)}) collective-permute-start(bf16[768,128]{1,0:T(8,128)(2,1)S(1)} %pad_maximum_fusion), channel_id=1, source_target_pairs={{0,32},{16,48},{32,64},{48,80},{64,96},{80,112},{96,128},{112,144}... | collective-permute-start | bytes 589832 | tf_op jit(solution)/shard_map/ppermute | solution.py:213
  42.1 19.8 %collective-permute-start.5 = (bf16[768,128]{1,0:T(8,128)(2,1)S(1)}, bf16[768,128]{1,0:T(8,128)(2,1)S(1)}, u32[]{:S(2)}, u32[]{:S(2)}) collective-permute-start(bf16[768,128]{1,0:T(8,128)(2,1)S(1)} %pad_maximum_fusion), channel_id=1, source_target_pairs={{0,480},{16,496},{32,0},{48,16},{64,32},{80,48},{96,64},{112,80},{... | collective-permute-start | bytes 589832 | tf_op jit(solution)/shard_map/ppermute | solution.py:213
  45.5 18.6 %collective-permute-start.6 = (bf16[768,128]{1,0:T(8,128)(2,1)S(1)}, bf16[768,128]{1,0:T(8,128)(2,1)S(1)}, u32[]{:S(2)}, u32[]{:S(2)}) collective-permute-start(bf16[768,128]{1,0:T(8,128)(2,1)S(1)} %pad_maximum_fusion), channel_id=1, source_target_pairs={{0,448},{16,464},{32,480},{48,496},{64,0},{80,16},{96,32},{112,48}... | collective-permute-start | bytes 589832 | tf_op jit(solution)/shard_map/ppermute | solution.py:213
  78.8 31.3 %all-to-all-start.2 = ((bf16[32,24,128]{2,1,0:T(8,128)(2,1)}), bf16[32,24,128]{2,1,0:T(8,128)(2,1)S(1)}, u32[]{:S(2)}, u32[]{:S(2)}) async-start(bf16[32,24,128]{2,1,0:T(8,128)(2,1)} %shard_map.104), calls=%async_computation.2 | async-start | bytes 393216 | tf_op jit(solution)/shard_map/all_to_all | solution.py:207
  91.8 45.4 %copy-start.3 = (f32[8]{0:T(128)S(1)}, f32[8]{0:T(128)}, u32[]{:S(2)}) copy-start(f32[8]{0:T(128)} %param.15) | copy-start | bytes 100
  91.9 25.7 %collective-permute-start.10 = (bf16[1024,128]{1,0:T(8,128)(2,1)S(1)}, bf16[1024,128]{1,0:T(8,128)(2,1)S(1)}, u32[]{:S(2)}, u32[]{:S(2)}) collective-permute-start(bf16[1024,128]{1,0:T(8,128)(2,1)S(1)} %get-tuple-element.14), channel_id=1, source_target_pairs={{0,64},{16,464},{32,96},{48,496},{64,128},{80,16},{96,160},{112,48... | collective-permute-start | bytes 786440 | tf_op jit(solution)/shard_map/ppermute | solution.py:218
  97.4 20.3 %collective-permute-start.8 = (bf16[1024,128]{1,0:T(8,128)(2,1)S(1)}, bf16[1024,128]{1,0:T(8,128)(2,1)S(1)}, u32[]{:S(2)}, u32[]{:S(2)}) collective-permute-start(bf16[1024,128]{1,0:T(8,128)(2,1)S(1)} %get-tuple-element.13), channel_id=1, source_target_pairs={{0,32},{16,48},{32,64},{48,80},{64,96},{80,112},{96,128},{112,144}... | collective-permute-start | bytes 786440 | tf_op jit(solution)/shard_map/ppermute | solution.py:213
  99.6 18.1 %collective-permute-start.9 = (bf16[1024,128]{1,0:T(8,128)(2,1)S(1)}, bf16[1024,128]{1,0:T(8,128)(2,1)S(1)}, u32[]{:S(2)}, u32[]{:S(2)}) collective-permute-start(bf16[1024,128]{1,0:T(8,128)(2,1)S(1)} %get-tuple-element.15), channel_id=1, source_target_pairs={{0,480},{16,496},{32,0},{48,16},{64,32},{80,48},{96,64},{112,80},{... | collective-permute-start | bytes 786440 | tf_op jit(solution)/shard_map/ppermute | solution.py:213
  110.2 0.7 copy-start
  112.5 21.3 %all-to-all-start.3 = ((bf16[32,16,128]{2,1,0:T(8,128)(2,1)}), bf16[32,16,128]{2,1,0:T(8,128)(2,1)S(1)}, u32[]{:S(2)}, u32[]{:S(2)}) async-start(bf16[32,16,128]{2,1,0:T(8,128)(2,1)} %shard_map.105), calls=%async_computation.3 | async-start | bytes 262144 | tf_op jit(solution)/shard_map/all_to_all | solution.py:207
  133.8 4.1 %copy-start.2 = (bf16[32,16,128]{2,1,0:T(8,128)(2,1)}, bf16[32,16,128]{2,1,0:T(8,128)(2,1)S(1)}, u32[]{:S(2)}) copy-start(bf16[32,16,128]{2,1,0:T(8,128)(2,1)S(1)} %all-to-all-done.3) | copy-start | bytes 393220
  133.8 16.7 %all-to-all-start.1 = ((bf16[8,128,128]{2,1,0:T(8,128)(2,1)}), bf16[8,128,128]{2,1,0:T(8,128)(2,1)S(1)}, u32[]{:S(2)}, u32[]{:S(2)}) async-start(bf16[8,128,128]{2,1,0:T(8,128)(2,1)} %bitcast.14), calls=%async_computation.1 | async-start | bytes 524288 | tf_op jit(solution)/shard_map/all_to_all | solution.py:207
  150.5 38.9 %copy-start.1 = (f32[128,128]{1,0:T(8,128)}, f32[128,128]{1,0:T(8,128)S(1)}, u32[]{:S(2)}) copy-start(f32[128,128]{1,0:T(8,128)S(1)} %convert_reduce_fusion.dkv_ref) | copy-start | bytes 196612

commit v5 on v2

--- a/solution.py
+++ b/solution.py
@@ -17,6 +17,7 @@
 SSM_HEADS = 8
 SSM_DIM = 64
 SCALE = 1.0 / math.sqrt(128)
+LOG2 = SCALE * math.log2(math.e)
 EPSILON = 1e-6
 HIGHEST = lax.Precision.HIGHEST
 f32 = jnp.float32
@@ -36,12 +37,12 @@
     return jnp.concatenate([x[:, 128 * h : 128 * (h + 1)] for h in range(4)], axis=0)
 
 
-def attention_kernel(pos_ref, q_ref, do_ref, *refs):
-    pieces, (dq_ref, dkv_ref, peak_ref, kv_ref, p_ref, dp_ref, outt_ref, dqt_ref, sems) = refs[:4], refs[4:]
+def attention_kernel(q_ref, do_ref, *refs):
+    pieces, (dq_ref, dkv_ref, peak_ref, kv_ref, p_ref, dp_ref, top_ref, outt_ref, dqt_ref, sems) = refs[:4], refs[4:]
     copies = [pltpu.make_async_copy(piece, kv_ref.at[r], sems.at[r]) for r, piece in enumerate(pieces)]
     for copy in copies:
         copy.start()
-    chip, core = pos_ref[0], pos_ref[1]
+    chip, core = lax.axis_index(("hi", "lo")), lax.axis_index("c")
     lane_group = lax.rem(chip, 4)
     q = heads_to_rows(q_ref[...])
     do = heads_to_rows(do_ref[...])
@@ -62,7 +63,7 @@
         return pl.ds(pl.multiple_of(j * 4 * TOK, 4 * TOK), 4 * TOK)
 
     def keys_at(j, part):
-        return jnp.concatenate([kv_ref[rel, c, hi, part] for rel, c, hi in tiles(j)], axis=0)
+        return jnp.concatenate([kv_ref[rel, c, 2 * hi + part] for rel, c, hi in tiles(j)], axis=0)
 
     def store_at(j, part, x):
         for k, (rel, c, hi) in enumerate(tiles(j)):
@@ -73,30 +74,31 @@
 
     def score_step(j, carry, masked):
         old, total = carry
-        s = dot(keys_at(j, 0), q, NT) * SCALE
+        s = dot(keys_at(j, 0), q, NT)
+        dp_ref[rows_at(j), :] = dot(keys_at(j, 1), do, NT)
         if masked:
             key = lax.broadcasted_iota(jnp.int32, s.shape, 0) + j * 4 * TOK
             query = lax.rem(lax.broadcasted_iota(jnp.int32, s.shape, 1), TOK) + (2 * chip + core) * TOK
             s = jnp.where(key <= query, s, -1e30)
         top = jnp.maximum(old, jnp.max(partial_rows(s, jnp.max), axis=0, keepdims=True))
-        p_ref[rows_at(j), :] = s
-        return top, total * jnp.exp(old - top) + partial_rows(jnp.exp(s - top), jnp.sum)
+        e = jnp.exp2((s - top) * LOG2)
+        p_ref[rows_at(j), :] = e
+        top_ref[j] = jnp.broadcast_to(top, (8, width))
+        return top, total * jnp.exp2((old - top) * LOG2) + partial_rows(e, jnp.sum)
 
     for copy in copies:
         copy.wait()
     carry = score_step(steps - 1, (jnp.full((1, width), -1e30, f32), jnp.zeros((8, width), f32)), True)
     top, total = lax.fori_loop(0, steps - 1, lambda j, c: score_step(j, c, False), carry)
-    lse = top + jnp.log(jnp.sum(total, axis=0, keepdims=True))
+    inverse = 1.0 / jnp.sum(total, axis=0, keepdims=True)
     outt_ref[...] = jnp.zeros_like(outt_ref)
     dqt_ref[...] = jnp.zeros_like(dqt_ref)
 
     def output_step(j, _):
-        p = jnp.exp(p_ref[rows_at(j), :] - lse)
+        p = p_ref[rows_at(j), :] * (jnp.exp2((top_ref[j][:1] - top) * LOG2) * inverse)
         p_ref[rows_at(j), :] = p
         p_b = p.astype(bf16)
-        values = keys_at(j, 1)
-        outt_ref[...] += dot(values, p_b, TN)
-        dp_ref[rows_at(j), :] = dot(values, do, NT)
+        outt_ref[...] += dot(keys_at(j, 1), p_b, TN)
         store_at(j, 1, dot(p_b, do, NN).astype(bf16))
         return 0
 
@@ -160,7 +162,7 @@
         flow = state_ref[k, :16, :].astype(f32) + jnp.exp(total[:1] + total[1:2]) * flow
 
 
-def ssm_kernel(dy_ref, b_ref, c_ref, decay_ref, skip_ref, flow_ref, dx_ref, peak_ref):
+def ssm_kernel(dy_ref, b_ref, c_ref, decay_ref, skip_ref, flow_ref, peak_q_ref, dx_ref, peak_ref):
     decay = decay_ref[...]
     dy = dy_ref[...]
     wide = running_decay(decay)
@@ -184,7 +186,8 @@
             out = out + dot((pairs * weight).astype(bf16), kept, NN)
         dx_ref[:, cols] = out
         top = jnp.maximum(top, jnp.max(jnp.abs(out), keepdims=True))
-    peak_ref[...] = jnp.broadcast_to(top, peak_ref.shape)
+    lane = lax.broadcasted_iota(jnp.int32, peak_ref.shape, 1)
+    peak_ref[...] = jnp.where(lane == 0, peak_q_ref[...], top)
 
 
 def call(body, out_shape, *args, scratch=(), scalars=0, raw=0):
@@ -221,8 +224,6 @@
 
 
 def step(queries, key_value, grad_out, ssm_grad, b_proj, c_proj, decay_log, skip_gain):
-    chip = lax.axis_index(("hi", "lo"))
-    pos = jnp.stack([chip, lax.axis_index("c")]).astype(jnp.int32)
     struct = jax.ShapeDtypeStruct
 
     column = swap_all(jnp.tile(key_value, (8, 1)), ("hi", "xp"))
@@ -237,23 +238,22 @@
 
     pieces = []
     for piece in (column, after, two, before):
-        pieces.append(lax.all_gather(piece, "c", axis=0, tiled=True).reshape(2, 4, 2, TOK, 128))
+        pieces.append(lax.all_gather(piece, "c", axis=0, tiled=True).reshape(2, 8, TOK, 128))
     dq, dkv, peak_q = call(
         attention_kernel,
         (struct((TOK, 512), f32), struct((2, 4, 4, 2, TOK, 128), bf16), struct((8, 128), f32)),
-        pos,
         queries,
         grad_out,
         *pieces,
         scratch=(
-            pltpu.VMEM((4, 2, 4, 2, TOK, 128), bf16),
+            pltpu.VMEM((4, 2, 8, TOK, 128), bf16),
             pltpu.VMEM((256 * CHIPS, 512), f32),
             pltpu.VMEM((256 * CHIPS, 512), f32),
+            pltpu.VMEM((CHIPS // 2, 8, 512), f32),
             pltpu.VMEM((128, 512), f32),
             pltpu.VMEM((128, 512), f32),
             pltpu.SemaphoreType.DMA((4,)),
         ),
-        scalars=1,
         raw=4,
     )
 
@@ -266,7 +266,7 @@
         (chip_sum[0].astype(f32) + from_before.astype(f32)) + (from_after.astype(f32) + from_two.astype(f32))
     ).astype(bf16)
     far = swap_all(near, ("hi", "xp")).reshape(8, TOK, 128)
-    dx, peak_x = call(
+    dx, early = call(
         ssm_kernel,
         (struct((TOK, 512), f32), struct((8, 128), f32)),
         ssm_grad,
@@ -275,13 +275,12 @@
         decay_log,
         skip_gain.reshape(SSM_HEADS, 1),
         flow.reshape(512, 128),
+        peak_q,
     )
 
     dkv_own = jnp.sum(far.astype(f32), axis=0)
     lane = lax.broadcasted_iota(jnp.int32, (1, 128), 1)
-    early = jnp.where(lane == 0, peak_q[:1], peak_x[:1])
-    early = lax.optimization_barrier(early)
-    peaks = jnp.where(lane == 1, jnp.max(jnp.abs(dkv_own)), early)
+    peaks = jnp.where(lane == 1, jnp.max(jnp.abs(dkv_own)), early[:1])
     peaks = jnp.max(swap_all(jnp.tile(peaks, (32, 1)), SEQ), axis=0, keepdims=True)
     peaks = swap_all(jnp.tile(peaks, (16, 1)), HEAD)
     return call(

time: 190 us -> 190 us (level)
  transfers between devices with their start and end apart: 9 -> 9, of which waited for: 3 -> 3; matrix products, arithmetic and copies ran while one was open for 2% -> 1% of each run, Pallas kernels for 4% -> 4%
where the time goes in v5:
time: 190 us; the launch traced here: 189 us
  blocking collectives  90.1 us (47%)
  starting transfers between devices  44.4 us (23%)
  waiting for transfers between devices  32.9 us (17%)
  Pallas kernels  14.8 us (8%)
  other arithmetic  3.32 us (2%)
  local copies, waits for them, and re-layouts  2.23 us (1%)
    all_to_all x4, blocking collectives, swap_all(): return lax.all_to_all(x, axes, 0, 0, tiled=True)  74.3 us
    all_to_all x3, waiting for transfers between devices, swap_all(): return lax.all_to_all(x, axes, 0, 0, tiled=True)  32.9 us
    ppermute x6, starting transfers between devices, along_z(): return lax.ppermute(x, SEQ, route)  24.8 us
    all_to_all x3, starting transfers between devices, swap_all(): return lax.all_to_all(x, axes, 0, 0, tiled=True)  19.7 us
    all_gather x4, blocking collectives, step(): lax.all_gather(piece, 'c', axis=0, tiled=True).reshape(2, 8, TOK, 128)  15.8 us
    pallas_call x5, Pallas kernels, call(): pl.pallas_call(body, out_shape=out_shape, in_specs=specs, out_specs=jax.t...  14.8 us
  transfers between devices with their start and end apart: 9, of which 3 were waited for; matrix products, arithmetic and copies ran while one was open for 1% of the time, Pallas kernels for 4%

profile of v5, /device:TPU:1, one launch (start us, length us, event | category | flops | bytes accessed | tf_op | source)
XLA Modules:
  0.0 188.6 jit_solution(4425006564693408757)
XLA Ops:
  0.6 0.8 tile.6
  1.4 30.4 %all_to_all.51 = bf16[8,128,128]{2,1,0:T(8,128)(2,1)S(1)} all-to-all(bf16[8,128,128]{2,1,0:T(8,128)(2,1)S(1)} %tile.6), channel_id=1, replica_groups=mesh['hi'=4,'lo'=4,'c'=2,'y'=4,'xh'=2,'xp'=2] {'hi','xp'}, dimensions={0} | all-to-all | bytes 524288 | tf_op jit(solution)/shard_map/all_to_all | solution.py:207
  31.9 4.5 %collective-permute-start = (bf16[1024,128]{1,0:T(8,128)(2,1)S(1)}, bf16[1024,128]{1,0:T(8,128)(2,1)S(1)}, u32[]{:S(2)}, u32[]{:S(2)}) collective-permute-start(bf16[1024,128]{1,0:T(8,128)(2,1)S(1)} %bitcast.32), channel_id=1, source_target_pairs={{0,480},{16,496},{32,0},{48,16},{64,32},{80,48},{96,64},{112,80},{... | collective-permute-start | bytes 786440 | tf_op jit(solution)/shard_map/ppermute | solution.py:216
  36.4 2.6 %shard_map.104 = bf16[32,24,128]{2,1,0:T(8,128)(2,1)} custom-call(bf16[128,512]{1,0:T(8,128)(2,1)} %dy_ref.3, bf16[128,128]{1,0:T(8,128)(2,1)} %c_ref.3, f32[8,128]{1,0:T(8,128)} %decay_ref.3), custom_call_target="tpu_custom_call" | custom-call | tf_op jit(solution)/shard_map/pallas_call | solution.py:197
  39.0 6.2 %collective-permute-start.1 = (bf16[1024,128]{1,0:T(8,128)(2,1)S(1)}, bf16[1024,128]{1,0:T(8,128)(2,1)S(1)}, u32[]{:S(2)}, u32[]{:S(2)}) collective-permute-start(bf16[1024,128]{1,0:T(8,128)(2,1)S(1)} %bitcast.33), channel_id=1, source_target_pairs={{0,64},{16,464},{32,96},{48,496},{64,128},{80,16},{96,160},{112,48... | collective-permute-start | bytes 786440 | tf_op jit(solution)/shard_map/ppermute | solution.py:216
  45.1 3.4 %collective-permute-start.2 = (bf16[1024,128]{1,0:T(8,128)(2,1)S(1)}, bf16[1024,128]{1,0:T(8,128)(2,1)S(1)}, u32[]{:S(2)}, u32[]{:S(2)}) collective-permute-start(bf16[1024,128]{1,0:T(8,128)(2,1)S(1)} %bitcast.34), channel_id=1, source_target_pairs={{0,32},{16,48},{32,64},{48,80},{64,96},{80,112},{96,128},{112,144}... | collective-permute-start | bytes 786440 | tf_op jit(solution)/shard_map/ppermute | solution.py:216
  48.5 4.9 %all_gather.12 = bf16[2048,128]{1,0:T(8,128)(2,1)} all-gather(bf16[1024,128]{1,0:T(8,128)(2,1)S(1)} %bitcast.35), channel_id=1, replica_groups=mesh['hi'=4,'lo'=4,'c'=2,'y'=4,'xh'=2,'xp'=2] {'c'}, dimensions={0}, use_global_device_ids=true | all-gather | bytes 786432 | tf_op jit(solution)/shard_map/all_gather | solution.py:241
  53.4 0.0 collective-permute-done
  53.4 2.3 %all_gather.13 = bf16[2048,128]{1,0:T(8,128)(2,1)} all-gather(bf16[1024,128]{1,0:T(8,128)(2,1)S(1)} %collective-permute-done), channel_id=1, replica_groups=mesh['hi'=4,'lo'=4,'c'=2,'y'=4,'xh'=2,'xp'=2] {'c'}, dimensions={0}, use_global_device_ids=true | all-gather | bytes 786432 | tf_op jit(solution)/shard_map/all_gather | solution.py:241
  55.7 0.0 collective-permute-done.1
  55.7 4.8 %all_gather.14 = bf16[2048,128]{1,0:T(8,128)(2,1)} all-gather(bf16[1024,128]{1,0:T(8,128)(2,1)S(1)} %collective-permute-done.1), channel_id=1, replica_groups=mesh['hi'=4,'lo'=4,'c'=2,'y'=4,'xh'=2,'xp'=2] {'c'}, dimensions={0}, use_global_device_ids=true | all-gather | bytes 786432 | tf_op jit(solution)/shard_map/all_gather | solution.py:241
  60.5 0.0 collective-permute-done.2
  60.5 3.9 %all_gather.15 = bf16[2048,128]{1,0:T(8,128)(2,1)} all-gather(bf16[1024,128]{1,0:T(8,128)(2,1)S(1)} %collective-permute-done.2), channel_id=1, replica_groups=mesh['hi'=4,'lo'=4,'c'=2,'y'=4,'xh'=2,'xp'=2] {'c'}, dimensions={0}, use_global_device_ids=true | all-gather | bytes 786432 | tf_op jit(solution)/shard_map/all_gather | solution.py:241
  64.4 5.8 %shard_map.103 = (f32[128,512]{1,0:T(8,128)}, bf16[2,4,4,2,128,128]{5,4,3,2,1,0:T(8,128)(2,1)}, f32[8,128]{1,0:T(8,128)}) custom-call(bf16[128,512]{1,0:T(8,128)(2,1)} %q_ref.1, bf16[128,512]{1,0:T(8,128)(2,1)} %do_ref.1, bf16[2,8,128,128]{3,2,1,0:T(8,128)(2,1)} %bitcast.28, bf16[2,8,128,128]{3,2,1,0:T(8,128)(2,1)} %bitcast.29, ...), custom_call_target="tpu_custom_call" | custom-call | tf_op jit(solution)/shard_map/pallas_call | solution.py:197
  70.1 6.6 %all_to_all.52 = bf16[2,4096,128]{2,1,0:T(8,128)(2,1)S(1)} all-to-all(bf16[2,4096,128]{2,1,0:T(8,128)(2,1)} %bitcast.27), channel_id=1, replica_groups=mesh['hi'=4,'lo'=4,'c'=2,'y'=4,'xh'=2,'xp'=2] {'c'}, dimensions={0} | all-to-all | bytes 4194304 | tf_op jit(solution)/shard_map/all_to_all | solution.py:207
  76.8 10.8 %all-to-all-start.3 = ((bf16[32,24,128]{2,1,0:T(8,128)(2,1)}), bf16[32,24,128]{2,1,0:T(8,128)(2,1)S(1)}, u32[]{:S(2)}, u32[]{:S(2)}) async-start(bf16[32,24,128]{2,1,0:T(8,128)(2,1)} %shard_map.104), calls=%async_computation.3 | async-start | bytes 393216 | tf_op jit(solution)/shard_map/all_to_all | solution.py:207
  87.6 0.3 convert_element_type.33
  87.8 0.2 fusion
  88.1 0.0 copy-start.3
  88.1 0.1 slice_bitcast_fusion.2
  88.1 3.3 %collective-permute-start.3 = (bf16[1024,128]{1,0:T(8,128)(2,1)S(1)}, bf16[1024,128]{1,0:T(8,128)(2,1)S(1)}, u32[]{:S(2)}, u32[]{:S(2)}) collective-permute-start(bf16[1024,128]{1,0:T(8,128)(2,1)S(1)} %get-tuple-element.13), channel_id=1, source_target_pairs={{0,32},{16,48},{32,64},{48,80},{64,96},{80,112},{96,128},{112,144}... | collective-permute-start | bytes 786440 | tf_op jit(solution)/shard_map/ppermute | solution.py:216
  91.4 3.2 %collective-permute-start.4 = (bf16[1024,128]{1,0:T(8,128)(2,1)S(1)}, bf16[1024,128]{1,0:T(8,128)(2,1)S(1)}, u32[]{:S(2)}, u32[]{:S(2)}) collective-permute-start(bf16[1024,128]{1,0:T(8,128)(2,1)S(1)} %get-tuple-element.15), channel_id=1, source_target_pairs={{0,480},{16,496},{32,0},{48,16},{64,32},{80,48},{96,64},{112,80},{... | collective-permute-start | bytes 786440 | tf_op jit(solution)/shard_map/ppermute | solution.py:216
  94.6 4.2 %collective-permute-start.5 = (bf16[1024,128]{1,0:T(8,128)(2,1)S(1)}, bf16[1024,128]{1,0:T(8,128)(2,1)S(1)}, u32[]{:S(2)}, u32[]{:S(2)}) collective-permute-start(bf16[1024,128]{1,0:T(8,128)(2,1)S(1)} %get-tuple-element.14), channel_id=1, source_target_pairs={{0,64},{16,464},{32,96},{48,496},{64,128},{80,16},{96,160},{112,48... | collective-permute-start | bytes 786440 | tf_op jit(solution)/shard_map/ppermute | solution.py:216
  98.9 7.5 %all-to-all-done.3.state_ref = bf16[32,24,128]{2,1,0:T(8,128)(2,1)S(1)} async-done(((bf16[32,24,128]{2,1,0:T(8,128)(2,1)}), bf16[32,24,128]{2,1,0:T(8,128)(2,1)S(1)}, u32[]{:S(2)}, u32[]{:S(2)}) %all-to-all-start.3) | async-done | bytes 196640 | tf_op jit(solution)/shard_map/all_to_all | solution.py:207
  106.3 0.0 copy-start
  106.3 0.7 copy-done
  107.0 1.7 shard_map.105
  108.7 5.2 %all-to-all-start.4 = ((bf16[32,16,128]{2,1,0:T(8,128)(2,1)}), bf16[32,16,128]{2,1,0:T(8,128)(2,1)S(1)}, u32[]{:S(2)}, u32[]{:S(2)}) async-start(bf16[32,16,128]{2,1,0:T(8,128)(2,1)} %shard_map.105), calls=%async_computation.4 | async-start | bytes 262144 | tf_op jit(solution)/shard_map/all_to_all | solution.py:207
  113.9 0.0 collective-permute-done.3
  113.9 0.0 collective-permute-done.4
  113.9 0.0 collective-permute-done.5
  113.9 0.8 fusion.2
  114.7 15.3 %all-to-all-done.4 = bf16[32,16,128]{2,1,0:T(8,128)(2,1)S(1)} async-done(((bf16[32,16,128]{2,1,0:T(8,128)(2,1)}), bf16[32,16,128]{2,1,0:T(8,128)(2,1)S(1)}, u32[]{:S(2)}, u32[]{:S(2)}) %all-to-all-start.4) | async-done | bytes 131104 | tf_op jit(solution)/shard_map/all_to_all | solution.py:207
  130.0 0.0 copy-start.2
  130.1 3.7 %all-to-all-start.2 = ((bf16[8,128,128]{2,1,0:T(8,128)(2,1)}), bf16[8,128,128]{2,1,0:T(8,128)(2,1)S(1)}, u32[]{:S(2)}, u32[]{:S(2)}) async-start(bf16[8,128,128]{2,1,0:T(8,128)(2,1)} %bitcast.11), calls=%async_computation.2 | async-start | bytes 524288 | tf_op jit(solution)/shard_map/all_to_all | solution.py:207
  133.7 0.0 copy-done.3
  133.7 0.7 copy.14.skip_ref
  134.4 0.0 copy-done.2
  134.4 2.9 %shard_map.106 = (f32[128,512]{1,0:T(8,128)}, f32[8,128]{1,0:T(8,128)}) custom-call(bf16[128,512]{1,0:T(8,128)(2,1)} %dy_ref.3, bf16[128,128]{1,0:T(8,128)(2,1)} %b_ref.1, bf16[128,128]{1,0:T(8,128)(2,1)} %c_ref.3, f32[8,128]{1,0:T(8,128)} %decay_ref.3, f32[8,1]{1,0:T(8,128)} %copy.14.skip_ref, bf16[512,128]{1,0:T(8,128)(2,1)} %bitcast.36, ...), custom_call_target="tpu_custom_call" | custom-call | tf_op jit(solution)/shard_map/pallas_call | solution.py:197
  137.3 10.1 %all-to-all-done.2 = bf16[8,128,128]{2,1,0:T(8,128)(2,1)S(1)} async-done(((bf16[8,128,128]{2,1,0:T(8,128)(2,1)}), bf16[8,128,128]{2,1,0:T(8,128)(2,1)S(1)}, u32[]{:S(2)}, u32[]{:S(2)}) %all-to-all-start.2) | async-done | bytes 262176 | tf_op jit(solution)/shard_map/all_to_all | solution.py:207
  147.5 0.0 copy-start.1
  147.5 0.6 abs_reduce_fusion
  148.1 1.3 fusion.3
  149.4 24.4 %all_to_all.53 = f32[32,1,128]{2,1,0:T(1,128)S(1)} all-to-all(f32[32,1,128]{2,1,0:T(1,128)S(1)} %tile.7), channel_id=1, replica_groups=mesh['hi'=4,'lo'=4,'c'=2,'y'=4,'xh'=2,'xp'=2] {'hi','lo','c'}, dimensions={0} | all-to-all | bytes 32768 | tf_op jit(solution)/shard_map/all_to_all | solution.py:207
  173.9 12.8 %all_to_all.54 = f32[16,1,128]{2,1,0:T(1,128)} all-to-all(f32[16,1,128]{2,1,0:T(1,128)S(1)} %tile.8), channel_id=1, replica_groups=mesh['hi'=4,'lo'=4,'c'=2,'y'=4,'xh'=2,'xp'=2] {'y','xh','xp'}, dimensions={0} | all-to-all | bytes 16384 | tf_op jit(solution)/shard_map/all_to_all | solution.py:207
  186.7 0.0 copy-done.1
  186.7 1.9 shard_map.107
  (4 shorter events, 0.1 us)
Async XLA Ops:
  31.9 21.5 %collective-permute-start = (bf16[1024,128]{1,0:T(8,128)(2,1)S(1)}, bf16[1024,128]{1,0:T(8,128)(2,1)S(1)}, u32[]{:S(2)}, u32[]{:S(2)}) collective-permute-start(bf16[1024,128]{1,0:T(8,128)(2,1)S(1)} %bitcast.32), channel_id=1, source_target_pairs={{0,480},{16,496},{32,0},{48,16},{64,32},{80,48},{96,64},{112,80},{... | collective-permute-start | bytes 786440 | tf_op jit(solution)/shard_map/ppermute | solution.py:216
  39.0 16.7 %collective-permute-start.1 = (bf16[1024,128]{1,0:T(8,128)(2,1)S(1)}, bf16[1024,128]{1,0:T(8,128)(2,1)S(1)}, u32[]{:S(2)}, u32[]{:S(2)}) collective-permute-start(bf16[1024,128]{1,0:T(8,128)(2,1)S(1)} %bitcast.33), channel_id=1, source_target_pairs={{0,64},{16,464},{32,96},{48,496},{64,128},{80,16},{96,160},{112,48... | collective-permute-start | bytes 786440 | tf_op jit(solution)/shard_map/ppermute | solution.py:216
  45.1 15.4 %collective-permute-start.2 = (bf16[1024,128]{1,0:T(8,128)(2,1)S(1)}, bf16[1024,128]{1,0:T(8,128)(2,1)S(1)}, u32[]{:S(2)}, u32[]{:S(2)}) collective-permute-start(bf16[1024,128]{1,0:T(8,128)(2,1)S(1)} %bitcast.34), channel_id=1, source_target_pairs={{0,32},{16,48},{32,64},{48,80},{64,96},{80,112},{96,128},{112,144}... | collective-permute-start | bytes 786440 | tf_op jit(solution)/shard_map/ppermute | solution.py:216
  76.8 29.6 %all-to-all-start.3 = ((bf16[32,24,128]{2,1,0:T(8,128)(2,1)}), bf16[32,24,128]{2,1,0:T(8,128)(2,1)S(1)}, u32[]{:S(2)}, u32[]{:S(2)}) async-start(bf16[32,24,128]{2,1,0:T(8,128)(2,1)} %shard_map.104), calls=%async_computation.3 | async-start | bytes 393216 | tf_op jit(solution)/shard_map/all_to_all | solution.py:207
  88.1 45.7 %copy-start.3 = (f32[8]{0:T(128)S(1)}, f32[8]{0:T(128)}, u32[]{:S(2)}) copy-start(f32[8]{0:T(128)} %param.15) | copy-start | bytes 100
  88.1 25.7 %collective-permute-start.3 = (bf16[1024,128]{1,0:T(8,128)(2,1)S(1)}, bf16[1024,128]{1,0:T(8,128)(2,1)S(1)}, u32[]{:S(2)}, u32[]{:S(2)}) collective-permute-start(bf16[1024,128]{1,0:T(8,128)(2,1)S(1)} %get-tuple-element.13), channel_id=1, source_target_pairs={{0,32},{16,48},{32,64},{48,80},{64,96},{80,112},{96,128},{112,144}... | collective-permute-start | bytes 786440 | tf_op jit(solution)/shard_map/ppermute | solution.py:216
  91.4 22.5 %collective-permute-start.4 = (bf16[1024,128]{1,0:T(8,128)(2,1)S(1)}, bf16[1024,128]{1,0:T(8,128)(2,1)S(1)}, u32[]{:S(2)}, u32[]{:S(2)}) collective-permute-start(bf16[1024,128]{1,0:T(8,128)(2,1)S(1)} %get-tuple-element.15), channel_id=1, source_target_pairs={{0,480},{16,496},{32,0},{48,16},{64,32},{80,48},{96,64},{112,80},{... | collective-permute-start | bytes 786440 | tf_op jit(solution)/shard_map/ppermute | solution.py:216
  94.6 19.2 %collective-permute-start.5 = (bf16[1024,128]{1,0:T(8,128)(2,1)S(1)}, bf16[1024,128]{1,0:T(8,128)(2,1)S(1)}, u32[]{:S(2)}, u32[]{:S(2)}) collective-permute-start(bf16[1024,128]{1,0:T(8,128)(2,1)S(1)} %get-tuple-element.14), channel_id=1, source_target_pairs={{0,64},{16,464},{32,96},{48,496},{64,128},{80,16},{96,160},{112,48... | collective-permute-start | bytes 786440 | tf_op jit(solution)/shard_map/ppermute | solution.py:216
  106.3 0.7 copy-start
  108.7 21.4 %all-to-all-start.4 = ((bf16[32,16,128]{2,1,0:T(8,128)(2,1)}), bf16[32,16,128]{2,1,0:T(8,128)(2,1)S(1)}, u32[]{:S(2)}, u32[]{:S(2)}) async-start(bf16[32,16,128]{2,1,0:T(8,128)(2,1)} %shard_map.105), calls=%async_computation.4 | async-start | bytes 262144 | tf_op jit(solution)/shard_map/all_to_all | solution.py:207
  130.0 4.4 %copy-start.2 = (bf16[32,16,128]{2,1,0:T(8,128)(2,1)}, bf16[32,16,128]{2,1,0:T(8,128)(2,1)S(1)}, u32[]{:S(2)}) copy-start(bf16[32,16,128]{2,1,0:T(8,128)(2,1)S(1)} %all-to-all-done.4) | copy-start | bytes 393220
  130.1 17.4 %all-to-all-start.2 = ((bf16[8,128,128]{2,1,0:T(8,128)(2,1)}), bf16[8,128,128]{2,1,0:T(8,128)(2,1)S(1)}, u32[]{:S(2)}, u32[]{:S(2)}) async-start(bf16[8,128,128]{2,1,0:T(8,128)(2,1)} %bitcast.11), calls=%async_computation.2 | async-start | bytes 524288 | tf_op jit(solution)/shard_map/all_to_all | solution.py:207
  147.5 39.2 %copy-start.1 = (f32[128,128]{1,0:T(8,128)}, f32[128,128]{1,0:T(8,128)S(1)}, u32[]{:S(2)}) copy-start(f32[128,128]{1,0:T(8,128)S(1)} %convert_reduce_fusion.dkv_ref) | copy-start | bytes 196612

commit v6 on v5

--- a/solution.py
+++ b/solution.py
@@ -48,7 +48,8 @@
     do = heads_to_rows(do_ref[...])
     width = q.shape[0]
 
-    steps = chip // 2 + 1
+    pairs = chip // 4 + 1
+    diagonal = chip // 2
 
     def place(z):
         return lax.rem(lax.rem(z, 4) - lane_group + 4, 4), z // 4
@@ -70,56 +71,80 @@
             dkv_ref[c, rel, hi, part] = x[TOK * k : TOK * (k + 1)]
 
     def partial_rows(x, op):
-        return op(x.reshape(4 * TOK // 8, 8, width), axis=0)
+        return op(x.reshape(x.shape[0] // 8, 8, width), axis=0)
 
     def score_step(j, carry, masked):
+        for half in range(2):
+            carry = half_step(j, half, carry, masked)
+        return carry
+
+    def half_step(j, half, carry, masked):
         old, total = carry
-        s = dot(keys_at(j, 0), q, NT)
-        dp_ref[rows_at(j), :] = dot(keys_at(j, 1), do, NT)
+        rows = pl.ds(pl.multiple_of(j * 4 * TOK, 4 * TOK) + 2 * half * TOK, 2 * TOK)
+        held = list(tiles(j))[2 * half : 2 * half + 2]
+        keys, values = (
+            jnp.concatenate([kv_ref[rel, c, 2 * hi + part] for rel, c, hi in held], axis=0) for part in range(2)
+        )
+        s = dot(keys, q, NT)
+        dp_ref[rows, :] = dot(values, do, NT)
         if masked:
-            key = lax.broadcasted_iota(jnp.int32, s.shape, 0) + j * 4 * TOK
+            key = lax.broadcasted_iota(jnp.int32, s.shape, 0) + (j * 4 + 2 * half) * TOK
             query = lax.rem(lax.broadcasted_iota(jnp.int32, s.shape, 1), TOK) + (2 * chip + core) * TOK
             s = jnp.where(key <= query, s, -1e30)
         top = jnp.maximum(old, jnp.max(partial_rows(s, jnp.max), axis=0, keepdims=True))
         e = jnp.exp2((s - top) * LOG2)
-        p_ref[rows_at(j), :] = e
-        top_ref[j] = jnp.broadcast_to(top, (8, width))
+        p_ref[rows, :] = e
+        top_ref[2 * j + half] = jnp.broadcast_to(top, (8, width))
         return top, total * jnp.exp2((old - top) * LOG2) + partial_rows(e, jnp.sum)
 
     for copy in copies:
         copy.wait()
-    carry = score_step(steps - 1, (jnp.full((1, width), -1e30, f32), jnp.zeros((8, width), f32)), True)
-    top, total = lax.fori_loop(0, steps - 1, lambda j, c: score_step(j, c, False), carry)
+    carry = (jnp.full((1, width), -1e30, f32), jnp.zeros((8, width), f32))
+    carry = lax.fori_loop(diagonal, 2 * pairs, lambda j, c: score_step(j, c, True), carry)
+    carry = lax.cond(
+        diagonal % 2 == 1, lambda c: score_step(diagonal - 1, c, False), lambda c: c, carry
+    )
+    top, total = lax.fori_loop(
+        0, diagonal // 2, lambda i, c: score_step(2 * i + 1, score_step(2 * i, c, False), False), carry
+    )
     inverse = 1.0 / jnp.sum(total, axis=0, keepdims=True)
     outt_ref[...] = jnp.zeros_like(outt_ref)
     dqt_ref[...] = jnp.zeros_like(dqt_ref)
 
-    def output_step(j, _):
-        p = p_ref[rows_at(j), :] * (jnp.exp2((top_ref[j][:1] - top) * LOG2) * inverse)
-        p_ref[rows_at(j), :] = p
-        p_b = p.astype(bf16)
-        outt_ref[...] += dot(keys_at(j, 1), p_b, TN)
-        store_at(j, 1, dot(p_b, do, NN).astype(bf16))
+    def output_step(i, _):
+        step = jnp.zeros(outt_ref.shape, f32)
+        for j in (2 * i, 2 * i + 1):
+            scales = [jnp.exp2((top_ref[2 * j + half][:1] - top) * LOG2) * inverse for half in range(2)]
+            p = p_ref[rows_at(j), :]
+            p = jnp.concatenate([p[: 2 * TOK] * scales[0], p[2 * TOK :] * scales[1]], axis=0)
+            p_ref[rows_at(j), :] = p
+            p_b = p.astype(bf16)
+            step = step + dot(keys_at(j, 1), p_b, TN)
+            store_at(j, 1, dot(p_b, do, NN).astype(bf16))
+        outt_ref[...] += step
         return 0
 
-    lax.fori_loop(0, steps, output_step, 0)
+    lax.fori_loop(0, pairs, output_step, 0)
     dot_rows = jnp.concatenate([do_ref[:, 128 * h : 128 * (h + 1)].astype(f32).T for h in range(4)], axis=1)
     delta = jnp.sum(dot_rows * outt_ref[...].astype(bf16).astype(f32), axis=0, keepdims=True)
 
-    def gradient_step(j, _):
-        ds = (p_ref[rows_at(j), :] * (dp_ref[rows_at(j), :] - delta)).astype(bf16)
-        store_at(j, 0, (dot(ds, q, NN) * SCALE).astype(bf16))
-        dqt_ref[...] += dot(keys_at(j, 0), ds, TN)
+    def gradient_step(i, _):
+        step = jnp.zeros(dqt_ref.shape, f32)
+        for j in (2 * i, 2 * i + 1):
+            ds = (p_ref[rows_at(j), :] * (dp_ref[rows_at(j), :] - delta)).astype(bf16)
+            store_at(j, 0, (dot(ds, q, NN) * SCALE).astype(bf16))
+            step = step + dot(keys_at(j, 0), ds, TN)
+        dqt_ref[...] += step
         return 0
 
-    lax.fori_loop(0, steps, gradient_step, 0)
+    lax.fori_loop(0, pairs, gradient_step, 0)
 
     def clear_step(j, _):
         for part in range(2):
             store_at(j, part, jnp.zeros((4 * TOK, 128), bf16))
         return 0
 
-    lax.fori_loop(steps, CHIPS // 2, clear_step, 0)
+    lax.fori_loop(2 * pairs, CHIPS // 2, clear_step, 0)
     dqt = dqt_ref[...] * SCALE
     for h in range(4):
         dq_ref[:, 128 * h : 128 * (h + 1)] = dqt[:, TOK * h : TOK * (h + 1)].T
@@ -249,7 +274,7 @@
             pltpu.VMEM((4, 2, 8, TOK, 128), bf16),
             pltpu.VMEM((256 * CHIPS, 512), f32),
             pltpu.VMEM((256 * CHIPS, 512), f32),
-            pltpu.VMEM((CHIPS // 2, 8, 512), f32),
+            pltpu.VMEM((CHIPS, 8, 512), f32),
             pltpu.VMEM((128, 512), f32),
             pltpu.VMEM((128, 512), f32),
             pltpu.SemaphoreType.DMA((4,)),

time: 190 us -> 188 us (0.989)
  blocking collectives: 90.1 us -> 86.8 us
  waiting for transfers between devices: 32.9 us -> 35.9 us
  starting transfers between devices: 44.4 us -> 42.2 us
    all_to_all x4, blocking collectives: 74.3 us -> 70.9 us  [swap_all(): return lax.all_to_all(x, axes, 0, 0, tiled=True)]
    all_to_all x3, waiting for transfers between devices: 32.9 us -> 35.9 us  [swap_all(): return lax.all_to_all(x, axes, 0, 0, tiled=True)]
    all_to_all x3, starting transfers between devices: 19.7 us -> 17.5 us  [swap_all(): return lax.all_to_all(x, axes, 0, 0, tiled=True)]
where the time goes in v6:
time: 188 us; the launch traced here: 187 us
  blocking collectives  86.8 us (46%)
  starting transfers between devices  42.2 us (22%)
  waiting for transfers between devices  35.9 us (19%)
  Pallas kernels  15.7 us (8%)
  other arithmetic  3.32 us (2%)
  local copies, waits for them, and re-layouts  2.23 us (1%)
    all_to_all x4, blocking collectives, swap_all(): return lax.all_to_all(x, axes, 0, 0, tiled=True)  70.9 us
    all_to_all x3, waiting for transfers between devices, swap_all(): return lax.all_to_all(x, axes, 0, 0, tiled=True)  35.9 us
    ppermute x6, starting transfers between devices, along_z(): return lax.ppermute(x, SEQ, route)  24.8 us
    all_to_all x3, starting transfers between devices, swap_all(): return lax.all_to_all(x, axes, 0, 0, tiled=True)  17.5 us
    all_gather x4, blocking collectives, step(): lax.all_gather(piece, 'c', axis=0, tiled=True).reshape(2, 8, TOK, 128)  15.8 us
    pallas_call x5, Pallas kernels, call(): pl.pallas_call(body, out_shape=out_shape, in_specs=specs, out_specs=jax.t...  15.7 us
  transfers between devices with their start and end apart: 9, of which 3 were waited for; matrix products, arithmetic and copies ran while one was open for 1% of the time, Pallas kernels for 4%

profile of v6, /device:TPU:1, one launch (start us, length us, event | category | flops | bytes accessed | tf_op | source)
XLA Modules:
  0.0 186.9 jit_solution(11226272628975763794)
XLA Ops:
  0.6 0.8 tile.6
  1.4 30.4 %all_to_all.51 = bf16[8,128,128]{2,1,0:T(8,128)(2,1)S(1)} all-to-all(bf16[8,128,128]{2,1,0:T(8,128)(2,1)S(1)} %tile.6), channel_id=1, replica_groups=mesh['hi'=4,'lo'=4,'c'=2,'y'=4,'xh'=2,'xp'=2] {'hi','xp'}, dimensions={0} | all-to-all | bytes 524288 | tf_op jit(solution)/shard_map/all_to_all | solution.py:232
  31.9 4.5 %collective-permute-start = (bf16[1024,128]{1,0:T(8,128)(2,1)S(1)}, bf16[1024,128]{1,0:T(8,128)(2,1)S(1)}, u32[]{:S(2)}, u32[]{:S(2)}) collective-permute-start(bf16[1024,128]{1,0:T(8,128)(2,1)S(1)} %bitcast.32), channel_id=1, source_target_pairs={{0,480},{16,496},{32,0},{48,16},{64,32},{80,48},{96,64},{112,80},{... | collective-permute-start | bytes 786440 | tf_op jit(solution)/shard_map/ppermute | solution.py:241
  36.4 2.6 %shard_map.104 = bf16[32,24,128]{2,1,0:T(8,128)(2,1)} custom-call(bf16[128,512]{1,0:T(8,128)(2,1)} %dy_ref.3, bf16[128,128]{1,0:T(8,128)(2,1)} %c_ref.3, f32[8,128]{1,0:T(8,128)} %decay_ref.3), custom_call_target="tpu_custom_call" | custom-call | tf_op jit(solution)/shard_map/pallas_call | solution.py:222
  39.0 6.2 %collective-permute-start.1 = (bf16[1024,128]{1,0:T(8,128)(2,1)S(1)}, bf16[1024,128]{1,0:T(8,128)(2,1)S(1)}, u32[]{:S(2)}, u32[]{:S(2)}) collective-permute-start(bf16[1024,128]{1,0:T(8,128)(2,1)S(1)} %bitcast.33), channel_id=1, source_target_pairs={{0,64},{16,464},{32,96},{48,496},{64,128},{80,16},{96,160},{112,48... | collective-permute-start | bytes 786440 | tf_op jit(solution)/shard_map/ppermute | solution.py:241
  45.1 3.4 %collective-permute-start.2 = (bf16[1024,128]{1,0:T(8,128)(2,1)S(1)}, bf16[1024,128]{1,0:T(8,128)(2,1)S(1)}, u32[]{:S(2)}, u32[]{:S(2)}) collective-permute-start(bf16[1024,128]{1,0:T(8,128)(2,1)S(1)} %bitcast.34), channel_id=1, source_target_pairs={{0,32},{16,48},{32,64},{48,80},{64,96},{80,112},{96,128},{112,144}... | collective-permute-start | bytes 786440 | tf_op jit(solution)/shard_map/ppermute | solution.py:241
  48.5 4.9 %all_gather.12 = bf16[2048,128]{1,0:T(8,128)(2,1)} all-gather(bf16[1024,128]{1,0:T(8,128)(2,1)S(1)} %bitcast.35), channel_id=1, replica_groups=mesh['hi'=4,'lo'=4,'c'=2,'y'=4,'xh'=2,'xp'=2] {'c'}, dimensions={0}, use_global_device_ids=true | all-gather | bytes 786432 | tf_op jit(solution)/shard_map/all_gather | solution.py:266
  53.4 0.0 collective-permute-done
  53.4 2.3 %all_gather.13 = bf16[2048,128]{1,0:T(8,128)(2,1)} all-gather(bf16[1024,128]{1,0:T(8,128)(2,1)S(1)} %collective-permute-done), channel_id=1, replica_groups=mesh['hi'=4,'lo'=4,'c'=2,'y'=4,'xh'=2,'xp'=2] {'c'}, dimensions={0}, use_global_device_ids=true | all-gather | bytes 786432 | tf_op jit(solution)/shard_map/all_gather | solution.py:266
  55.7 0.0 collective-permute-done.1
  55.7 4.8 %all_gather.14 = bf16[2048,128]{1,0:T(8,128)(2,1)} all-gather(bf16[1024,128]{1,0:T(8,128)(2,1)S(1)} %collective-permute-done.1), channel_id=1, replica_groups=mesh['hi'=4,'lo'=4,'c'=2,'y'=4,'xh'=2,'xp'=2] {'c'}, dimensions={0}, use_global_device_ids=true | all-gather | bytes 786432 | tf_op jit(solution)/shard_map/all_gather | solution.py:266
  60.5 0.0 collective-permute-done.2
  60.5 3.9 %all_gather.15 = bf16[2048,128]{1,0:T(8,128)(2,1)} all-gather(bf16[1024,128]{1,0:T(8,128)(2,1)S(1)} %collective-permute-done.2), channel_id=1, replica_groups=mesh['hi'=4,'lo'=4,'c'=2,'y'=4,'xh'=2,'xp'=2] {'c'}, dimensions={0}, use_global_device_ids=true | all-gather | bytes 786432 | tf_op jit(solution)/shard_map/all_gather | solution.py:266
  64.4 6.7 %shard_map.103 = (f32[128,512]{1,0:T(8,128)}, bf16[2,4,4,2,128,128]{5,4,3,2,1,0:T(8,128)(2,1)}, f32[8,128]{1,0:T(8,128)}) custom-call(bf16[128,512]{1,0:T(8,128)(2,1)} %q_ref.1, bf16[128,512]{1,0:T(8,128)(2,1)} %do_ref.1, bf16[2,8,128,128]{3,2,1,0:T(8,128)(2,1)} %bitcast.28, bf16[2,8,128,128]{3,2,1,0:T(8,128)(2,1)} %bitcast.29, ...), custom_call_target="tpu_custom_call" | custom-call | tf_op jit(solution)/shard_map/pallas_call | solution.py:222
  71.0 6.6 %all_to_all.52 = bf16[2,4096,128]{2,1,0:T(8,128)(2,1)S(1)} all-to-all(bf16[2,4096,128]{2,1,0:T(8,128)(2,1)} %bitcast.27), channel_id=1, replica_groups=mesh['hi'=4,'lo'=4,'c'=2,'y'=4,'xh'=2,'xp'=2] {'c'}, dimensions={0} | all-to-all | bytes 4194304 | tf_op jit(solution)/shard_map/all_to_all | solution.py:232
  77.7 8.9 %all-to-all-start.3 = ((bf16[32,24,128]{2,1,0:T(8,128)(2,1)}), bf16[32,24,128]{2,1,0:T(8,128)(2,1)S(1)}, u32[]{:S(2)}, u32[]{:S(2)}) async-start(bf16[32,24,128]{2,1,0:T(8,128)(2,1)} %shard_map.104), calls=%async_computation.3 | async-start | bytes 393216 | tf_op jit(solution)/shard_map/all_to_all | solution.py:232
  86.6 0.3 convert_element_type.33
  86.8 0.2 fusion
  87.1 0.0 copy-start.3
  87.1 0.1 slice_bitcast_fusion.2
  87.1 3.3 %collective-permute-start.3 = (bf16[1024,128]{1,0:T(8,128)(2,1)S(1)}, bf16[1024,128]{1,0:T(8,128)(2,1)S(1)}, u32[]{:S(2)}, u32[]{:S(2)}) collective-permute-start(bf16[1024,128]{1,0:T(8,128)(2,1)S(1)} %get-tuple-element.13), channel_id=1, source_target_pairs={{0,32},{16,48},{32,64},{48,80},{64,96},{80,112},{96,128},{112,144}... | collective-permute-start | bytes 786440 | tf_op jit(solution)/shard_map/ppermute | solution.py:241
  90.4 3.2 %collective-permute-start.4 = (bf16[1024,128]{1,0:T(8,128)(2,1)S(1)}, bf16[1024,128]{1,0:T(8,128)(2,1)S(1)}, u32[]{:S(2)}, u32[]{:S(2)}) collective-permute-start(bf16[1024,128]{1,0:T(8,128)(2,1)S(1)} %get-tuple-element.15), channel_id=1, source_target_pairs={{0,480},{16,496},{32,0},{48,16},{64,32},{80,48},{96,64},{112,80},{... | collective-permute-start | bytes 786440 | tf_op jit(solution)/shard_map/ppermute | solution.py:241
  93.6 4.2 %collective-permute-start.5 = (bf16[1024,128]{1,0:T(8,128)(2,1)S(1)}, bf16[1024,128]{1,0:T(8,128)(2,1)S(1)}, u32[]{:S(2)}, u32[]{:S(2)}) collective-permute-start(bf16[1024,128]{1,0:T(8,128)(2,1)S(1)} %get-tuple-element.14), channel_id=1, source_target_pairs={{0,64},{16,464},{32,96},{48,496},{64,128},{80,16},{96,160},{112,48... | collective-permute-start | bytes 786440 | tf_op jit(solution)/shard_map/ppermute | solution.py:241
  97.9 7.5 %all-to-all-done.3.state_ref = bf16[32,24,128]{2,1,0:T(8,128)(2,1)S(1)} async-done(((bf16[32,24,128]{2,1,0:T(8,128)(2,1)}), bf16[32,24,128]{2,1,0:T(8,128)(2,1)S(1)}, u32[]{:S(2)}, u32[]{:S(2)}) %all-to-all-start.3) | async-done | bytes 196640 | tf_op jit(solution)/shard_map/all_to_all | solution.py:232
  105.3 0.0 copy-start
  105.4 0.7 copy-done
  106.0 1.7 shard_map.105
  107.7 5.2 %all-to-all-start.4 = ((bf16[32,16,128]{2,1,0:T(8,128)(2,1)}), bf16[32,16,128]{2,1,0:T(8,128)(2,1)S(1)}, u32[]{:S(2)}, u32[]{:S(2)}) async-start(bf16[32,16,128]{2,1,0:T(8,128)(2,1)} %shard_map.105), calls=%async_computation.4 | async-start | bytes 262144 | tf_op jit(solution)/shard_map/all_to_all | solution.py:232
  112.9 0.0 collective-permute-done.3
  112.9 0.0 collective-permute-done.4
  112.9 0.0 collective-permute-done.5
  112.9 0.8 fusion.2
  113.7 15.3 %all-to-all-done.4 = bf16[32,16,128]{2,1,0:T(8,128)(2,1)S(1)} async-done(((bf16[32,16,128]{2,1,0:T(8,128)(2,1)}), bf16[32,16,128]{2,1,0:T(8,128)(2,1)S(1)}, u32[]{:S(2)}, u32[]{:S(2)}) %all-to-all-start.4) | async-done | bytes 131104 | tf_op jit(solution)/shard_map/all_to_all | solution.py:232
  129.1 0.0 copy-start.2
  129.1 3.4 %all-to-all-start.2 = ((bf16[8,128,128]{2,1,0:T(8,128)(2,1)}), bf16[8,128,128]{2,1,0:T(8,128)(2,1)S(1)}, u32[]{:S(2)}, u32[]{:S(2)}) async-start(bf16[8,128,128]{2,1,0:T(8,128)(2,1)} %bitcast.11), calls=%async_computation.2 | async-start | bytes 524288 | tf_op jit(solution)/shard_map/all_to_all | solution.py:232
  132.5 0.0 copy-done.3
  132.5 0.7 copy.14.skip_ref
  133.2 0.0 copy-done.2
  133.2 2.9 %shard_map.106 = (f32[128,512]{1,0:T(8,128)}, f32[8,128]{1,0:T(8,128)}) custom-call(bf16[128,512]{1,0:T(8,128)(2,1)} %dy_ref.3, bf16[128,128]{1,0:T(8,128)(2,1)} %b_ref.1, bf16[128,128]{1,0:T(8,128)(2,1)} %c_ref.3, f32[8,128]{1,0:T(8,128)} %decay_ref.3, f32[8,1]{1,0:T(8,128)} %copy.14.skip_ref, bf16[512,128]{1,0:T(8,128)(2,1)} %bitcast.36, ...), custom_call_target="tpu_custom_call" | custom-call | tf_op jit(solution)/shard_map/pallas_call | solution.py:222
  136.0 13.1 %all-to-all-done.2 = bf16[8,128,128]{2,1,0:T(8,128)(2,1)S(1)} async-done(((bf16[8,128,128]{2,1,0:T(8,128)(2,1)}), bf16[8,128,128]{2,1,0:T(8,128)(2,1)S(1)}, u32[]{:S(2)}, u32[]{:S(2)}) %all-to-all-start.2) | async-done | bytes 262176 | tf_op jit(solution)/shard_map/all_to_all | solution.py:232
  149.1 0.0 copy-start.1
  149.2 0.6 abs_reduce_fusion
  149.8 1.3 fusion.3
  151.1 21.1 %all_to_all.53 = f32[32,1,128]{2,1,0:T(1,128)S(1)} all-to-all(f32[32,1,128]{2,1,0:T(1,128)S(1)} %tile.7), channel_id=1, replica_groups=mesh['hi'=4,'lo'=4,'c'=2,'y'=4,'xh'=2,'xp'=2] {'hi','lo','c'}, dimensions={0} | all-to-all | bytes 32768 | tf_op jit(solution)/shard_map/all_to_all | solution.py:232
  172.2 12.8 %all_to_all.54 = f32[16,1,128]{2,1,0:T(1,128)} all-to-all(f32[16,1,128]{2,1,0:T(1,128)S(1)} %tile.8), channel_id=1, replica_groups=mesh['hi'=4,'lo'=4,'c'=2,'y'=4,'xh'=2,'xp'=2] {'y','xh','xp'}, dimensions={0} | all-to-all | bytes 16384 | tf_op jit(solution)/shard_map/all_to_all | solution.py:232
  185.0 0.0 copy-done.1
  185.0 1.9 %shard_map.107 = (bf16[128,512]{1,0:T(8,128)(2,1)}, bf16[128,128]{1,0:T(8,128)(2,1)}, bf16[128,512]{1,0:T(8,128)(2,1)}) custom-call(f32[16,128]{1,0:T(8,128)} %bitcast.38, f32[128,512]{1,0:T(8,128)} %get-tuple-element.11.dq_ref, f32[128,128]{1,0:T(8,128)} %copy-done.1, f32[128,512]{1,0:T(8,128)} %get-tuple-element.12.dx_ref), custom_call_target="tpu_custom_call" | custom-call | tf_op jit(solution)/shard_map/pallas_call | solution.py:222
  (4 shorter events, 0.1 us)
Async XLA Ops:
  31.9 21.5 %collective-permute-start = (bf16[1024,128]{1,0:T(8,128)(2,1)S(1)}, bf16[1024,128]{1,0:T(8,128)(2,1)S(1)}, u32[]{:S(2)}, u32[]{:S(2)}) collective-permute-start(bf16[1024,128]{1,0:T(8,128)(2,1)S(1)} %bitcast.32), channel_id=1, source_target_pairs={{0,480},{16,496},{32,0},{48,16},{64,32},{80,48},{96,64},{112,80},{... | collective-permute-start | bytes 786440 | tf_op jit(solution)/shard_map/ppermute | solution.py:241
  39.0 16.7 %collective-permute-start.1 = (bf16[1024,128]{1,0:T(8,128)(2,1)S(1)}, bf16[1024,128]{1,0:T(8,128)(2,1)S(1)}, u32[]{:S(2)}, u32[]{:S(2)}) collective-permute-start(bf16[1024,128]{1,0:T(8,128)(2,1)S(1)} %bitcast.33), channel_id=1, source_target_pairs={{0,64},{16,464},{32,96},{48,496},{64,128},{80,16},{96,160},{112,48... | collective-permute-start | bytes 786440 | tf_op jit(solution)/shard_map/ppermute | solution.py:241
  45.1 15.4 %collective-permute-start.2 = (bf16[1024,128]{1,0:T(8,128)(2,1)S(1)}, bf16[1024,128]{1,0:T(8,128)(2,1)S(1)}, u32[]{:S(2)}, u32[]{:S(2)}) collective-permute-start(bf16[1024,128]{1,0:T(8,128)(2,1)S(1)} %bitcast.34), channel_id=1, source_target_pairs={{0,32},{16,48},{32,64},{48,80},{64,96},{80,112},{96,128},{112,144}... | collective-permute-start | bytes 786440 | tf_op jit(solution)/shard_map/ppermute | solution.py:241
  77.7 27.7 %all-to-all-start.3 = ((bf16[32,24,128]{2,1,0:T(8,128)(2,1)}), bf16[32,24,128]{2,1,0:T(8,128)(2,1)S(1)}, u32[]{:S(2)}, u32[]{:S(2)}) async-start(bf16[32,24,128]{2,1,0:T(8,128)(2,1)} %shard_map.104), calls=%async_computation.3 | async-start | bytes 393216 | tf_op jit(solution)/shard_map/all_to_all | solution.py:232
  87.1 45.4 %copy-start.3 = (f32[8]{0:T(128)S(1)}, f32[8]{0:T(128)}, u32[]{:S(2)}) copy-start(f32[8]{0:T(128)} %param.15) | copy-start | bytes 100
  87.1 25.7 %collective-permute-start.3 = (bf16[1024,128]{1,0:T(8,128)(2,1)S(1)}, bf16[1024,128]{1,0:T(8,128)(2,1)S(1)}, u32[]{:S(2)}, u32[]{:S(2)}) collective-permute-start(bf16[1024,128]{1,0:T(8,128)(2,1)S(1)} %get-tuple-element.13), channel_id=1, source_target_pairs={{0,32},{16,48},{32,64},{48,80},{64,96},{80,112},{96,128},{112,144}... | collective-permute-start | bytes 786440 | tf_op jit(solution)/shard_map/ppermute | solution.py:241
  90.4 22.5 %collective-permute-start.4 = (bf16[1024,128]{1,0:T(8,128)(2,1)S(1)}, bf16[1024,128]{1,0:T(8,128)(2,1)S(1)}, u32[]{:S(2)}, u32[]{:S(2)}) collective-permute-start(bf16[1024,128]{1,0:T(8,128)(2,1)S(1)} %get-tuple-element.15), channel_id=1, source_target_pairs={{0,480},{16,496},{32,0},{48,16},{64,32},{80,48},{96,64},{112,80},{... | collective-permute-start | bytes 786440 | tf_op jit(solution)/shard_map/ppermute | solution.py:241
  93.6 19.2 %collective-permute-start.5 = (bf16[1024,128]{1,0:T(8,128)(2,1)S(1)}, bf16[1024,128]{1,0:T(8,128)(2,1)S(1)}, u32[]{:S(2)}, u32[]{:S(2)}) collective-permute-start(bf16[1024,128]{1,0:T(8,128)(2,1)S(1)} %get-tuple-element.14), channel_id=1, source_target_pairs={{0,64},{16,464},{32,96},{48,496},{64,128},{80,16},{96,160},{112,48... | collective-permute-start | bytes 786440 | tf_op jit(solution)/shard_map/ppermute | solution.py:241
  105.3 0.7 copy-start
  107.7 21.4 %all-to-all-start.4 = ((bf16[32,16,128]{2,1,0:T(8,128)(2,1)}), bf16[32,16,128]{2,1,0:T(8,128)(2,1)S(1)}, u32[]{:S(2)}, u32[]{:S(2)}) async-start(bf16[32,16,128]{2,1,0:T(8,128)(2,1)} %shard_map.105), calls=%async_computation.4 | async-start | bytes 262144 | tf_op jit(solution)/shard_map/all_to_all | solution.py:232
  129.1 4.1 %copy-start.2 = (bf16[32,16,128]{2,1,0:T(8,128)(2,1)}, bf16[32,16,128]{2,1,0:T(8,128)(2,1)S(1)}, u32[]{:S(2)}) copy-start(bf16[32,16,128]{2,1,0:T(8,128)(2,1)S(1)} %all-to-all-done.4) | copy-start | bytes 393220
  129.1 20.0 %all-to-all-start.2 = ((bf16[8,128,128]{2,1,0:T(8,128)(2,1)}), bf16[8,128,128]{2,1,0:T(8,128)(2,1)S(1)}, u32[]{:S(2)}, u32[]{:S(2)}) async-start(bf16[8,128,128]{2,1,0:T(8,128)(2,1)} %bitcast.11), calls=%async_computation.2 | async-start | bytes 524288 | tf_op jit(solution)/shard_map/all_to_all | solution.py:232
  149.1 35.9 %copy-start.1 = (f32[128,128]{1,0:T(8,128)}, f32[128,128]{1,0:T(8,128)S(1)}, u32[]{:S(2)}) copy-start(f32[128,128]{1,0:T(8,128)S(1)} %convert_reduce_fusion.dkv_ref) | copy-start | bytes 196612

commit v7 on v6

--- a/solution.py
+++ b/solution.py
@@ -212,7 +212,7 @@
         dx_ref[:, cols] = out
         top = jnp.maximum(top, jnp.max(jnp.abs(out), keepdims=True))
     lane = lax.broadcasted_iota(jnp.int32, peak_ref.shape, 1)
-    peak_ref[...] = jnp.where(lane == 0, peak_q_ref[...], top)
+    peak_ref[...] = jnp.where(lane == 0, peak_q_ref[:1], top)
 
 
 def call(body, out_shape, *args, scratch=(), scalars=0, raw=0):
@@ -293,7 +293,7 @@
     far = swap_all(near, ("hi", "xp")).reshape(8, TOK, 128)
     dx, early = call(
         ssm_kernel,
-        (struct((TOK, 512), f32), struct((8, 128), f32)),
+        (struct((TOK, 512), f32), struct((1, 128), f32)),
         ssm_grad,
         b_proj,
         c_proj,
@@ -305,7 +305,7 @@
 
     dkv_own = jnp.sum(far.astype(f32), axis=0)
     lane = lax.broadcasted_iota(jnp.int32, (1, 128), 1)
-    peaks = jnp.where(lane == 1, jnp.max(jnp.abs(dkv_own)), early[:1])
+    peaks = jnp.where(lane == 1, jnp.max(jnp.abs(dkv_own)), early)
     peaks = jnp.max(swap_all(jnp.tile(peaks, (32, 1)), SEQ), axis=0, keepdims=True)
     peaks = swap_all(jnp.tile(peaks, (16, 1)), HEAD)
     return call(

time: 188 us -> 188 us (level)
  no operation moved by 1% of the time
where the time goes in v7:
time: 188 us; the launch traced here: 187 us
  blocking collectives  86.8 us (46%)
  starting transfers between devices  42.2 us (22%)
  waiting for transfers between devices  35.9 us (19%)
  Pallas kernels  15.7 us (8%)
  other arithmetic  3.24 us (2%)
  local copies, waits for them, and re-layouts  2.23 us (1%)
    all_to_all x4, blocking collectives, swap_all(): return lax.all_to_all(x, axes, 0, 0, tiled=True)  70.9 us
    all_to_all x3, waiting for transfers between devices, swap_all(): return lax.all_to_all(x, axes, 0, 0, tiled=True)  35.9 us
    ppermute x6, starting transfers between devices, along_z(): return lax.ppermute(x, SEQ, route)  24.8 us
    all_to_all x3, starting transfers between devices, swap_all(): return lax.all_to_all(x, axes, 0, 0, tiled=True)  17.5 us
    all_gather x4, blocking collectives, step(): lax.all_gather(piece, 'c', axis=0, tiled=True).reshape(2, 8, TOK, 128)  15.8 us
    pallas_call x5, Pallas kernels, call(): pl.pallas_call(body, out_shape=out_shape, in_specs=specs, out_specs=jax.t...  15.7 us
  transfers between devices with their start and end apart: 9, of which 3 were waited for; matrix products, arithmetic and copies ran while one was open for 1% of the time, Pallas kernels for 4%

profile of v7, /device:TPU:1, one launch (start us, length us, event | category | flops | bytes accessed | tf_op | source)
XLA Modules:
  0.0 186.8 jit_solution(2090636872952886181)
XLA Ops:
  0.6 0.8 tile.6
  1.4 30.4 %all_to_all.51 = bf16[8,128,128]{2,1,0:T(8,128)(2,1)S(1)} all-to-all(bf16[8,128,128]{2,1,0:T(8,128)(2,1)S(1)} %tile.6), channel_id=1, replica_groups=mesh['hi'=4,'lo'=4,'c'=2,'y'=4,'xh'=2,'xp'=2] {'hi','xp'}, dimensions={0} | all-to-all | bytes 524288 | tf_op jit(solution)/shard_map/all_to_all | solution.py:232
  31.9 4.5 %collective-permute-start = (bf16[1024,128]{1,0:T(8,128)(2,1)S(1)}, bf16[1024,128]{1,0:T(8,128)(2,1)S(1)}, u32[]{:S(2)}, u32[]{:S(2)}) collective-permute-start(bf16[1024,128]{1,0:T(8,128)(2,1)S(1)} %bitcast.32), channel_id=1, source_target_pairs={{0,480},{16,496},{32,0},{48,16},{64,32},{80,48},{96,64},{112,80},{... | collective-permute-start | bytes 786440 | tf_op jit(solution)/shard_map/ppermute | solution.py:241
  36.4 2.6 %shard_map.104 = bf16[32,24,128]{2,1,0:T(8,128)(2,1)} custom-call(bf16[128,512]{1,0:T(8,128)(2,1)} %dy_ref.3, bf16[128,128]{1,0:T(8,128)(2,1)} %c_ref.3, f32[8,128]{1,0:T(8,128)} %decay_ref.3), custom_call_target="tpu_custom_call" | custom-call | tf_op jit(solution)/shard_map/pallas_call | solution.py:222
  39.0 6.2 %collective-permute-start.1 = (bf16[1024,128]{1,0:T(8,128)(2,1)S(1)}, bf16[1024,128]{1,0:T(8,128)(2,1)S(1)}, u32[]{:S(2)}, u32[]{:S(2)}) collective-permute-start(bf16[1024,128]{1,0:T(8,128)(2,1)S(1)} %bitcast.33), channel_id=1, source_target_pairs={{0,64},{16,464},{32,96},{48,496},{64,128},{80,16},{96,160},{112,48... | collective-permute-start | bytes 786440 | tf_op jit(solution)/shard_map/ppermute | solution.py:241
  45.1 3.4 %collective-permute-start.2 = (bf16[1024,128]{1,0:T(8,128)(2,1)S(1)}, bf16[1024,128]{1,0:T(8,128)(2,1)S(1)}, u32[]{:S(2)}, u32[]{:S(2)}) collective-permute-start(bf16[1024,128]{1,0:T(8,128)(2,1)S(1)} %bitcast.34), channel_id=1, source_target_pairs={{0,32},{16,48},{32,64},{48,80},{64,96},{80,112},{96,128},{112,144}... | collective-permute-start | bytes 786440 | tf_op jit(solution)/shard_map/ppermute | solution.py:241
  48.5 4.9 %all_gather.12 = bf16[2048,128]{1,0:T(8,128)(2,1)} all-gather(bf16[1024,128]{1,0:T(8,128)(2,1)S(1)} %bitcast.35), channel_id=1, replica_groups=mesh['hi'=4,'lo'=4,'c'=2,'y'=4,'xh'=2,'xp'=2] {'c'}, dimensions={0}, use_global_device_ids=true | all-gather | bytes 786432 | tf_op jit(solution)/shard_map/all_gather | solution.py:266
  53.4 0.0 collective-permute-done
  53.4 2.3 %all_gather.13 = bf16[2048,128]{1,0:T(8,128)(2,1)} all-gather(bf16[1024,128]{1,0:T(8,128)(2,1)S(1)} %collective-permute-done), channel_id=1, replica_groups=mesh['hi'=4,'lo'=4,'c'=2,'y'=4,'xh'=2,'xp'=2] {'c'}, dimensions={0}, use_global_device_ids=true | all-gather | bytes 786432 | tf_op jit(solution)/shard_map/all_gather | solution.py:266
  55.7 0.0 collective-permute-done.1
  55.7 4.8 %all_gather.14 = bf16[2048,128]{1,0:T(8,128)(2,1)} all-gather(bf16[1024,128]{1,0:T(8,128)(2,1)S(1)} %collective-permute-done.1), channel_id=1, replica_groups=mesh['hi'=4,'lo'=4,'c'=2,'y'=4,'xh'=2,'xp'=2] {'c'}, dimensions={0}, use_global_device_ids=true | all-gather | bytes 786432 | tf_op jit(solution)/shard_map/all_gather | solution.py:266
  60.5 0.0 collective-permute-done.2
  60.5 3.9 %all_gather.15 = bf16[2048,128]{1,0:T(8,128)(2,1)} all-gather(bf16[1024,128]{1,0:T(8,128)(2,1)S(1)} %collective-permute-done.2), channel_id=1, replica_groups=mesh['hi'=4,'lo'=4,'c'=2,'y'=4,'xh'=2,'xp'=2] {'c'}, dimensions={0}, use_global_device_ids=true | all-gather | bytes 786432 | tf_op jit(solution)/shard_map/all_gather | solution.py:266
  64.4 6.7 %shard_map.103 = (f32[128,512]{1,0:T(8,128)}, bf16[2,4,4,2,128,128]{5,4,3,2,1,0:T(8,128)(2,1)}, f32[8,128]{1,0:T(8,128)}) custom-call(bf16[128,512]{1,0:T(8,128)(2,1)} %q_ref.1, bf16[128,512]{1,0:T(8,128)(2,1)} %do_ref.1, bf16[2,8,128,128]{3,2,1,0:T(8,128)(2,1)} %bitcast.28, bf16[2,8,128,128]{3,2,1,0:T(8,128)(2,1)} %bitcast.29, ...), custom_call_target="tpu_custom_call" | custom-call | tf_op jit(solution)/shard_map/pallas_call | solution.py:222
  71.0 6.6 %all_to_all.52 = bf16[2,4096,128]{2,1,0:T(8,128)(2,1)S(1)} all-to-all(bf16[2,4096,128]{2,1,0:T(8,128)(2,1)} %bitcast.27), channel_id=1, replica_groups=mesh['hi'=4,'lo'=4,'c'=2,'y'=4,'xh'=2,'xp'=2] {'c'}, dimensions={0} | all-to-all | bytes 4194304 | tf_op jit(solution)/shard_map/all_to_all | solution.py:232
  77.7 8.9 %all-to-all-start.3 = ((bf16[32,24,128]{2,1,0:T(8,128)(2,1)}), bf16[32,24,128]{2,1,0:T(8,128)(2,1)S(1)}, u32[]{:S(2)}, u32[]{:S(2)}) async-start(bf16[32,24,128]{2,1,0:T(8,128)(2,1)} %shard_map.104), calls=%async_computation.3 | async-start | bytes 393216 | tf_op jit(solution)/shard_map/all_to_all | solution.py:232
  86.6 0.3 convert_element_type.33
  86.8 0.2 fusion
  87.1 0.0 copy-start.3
  87.1 0.1 slice_bitcast_fusion.2
  87.1 3.3 %collective-permute-start.3 = (bf16[1024,128]{1,0:T(8,128)(2,1)S(1)}, bf16[1024,128]{1,0:T(8,128)(2,1)S(1)}, u32[]{:S(2)}, u32[]{:S(2)}) collective-permute-start(bf16[1024,128]{1,0:T(8,128)(2,1)S(1)} %get-tuple-element.13), channel_id=1, source_target_pairs={{0,32},{16,48},{32,64},{48,80},{64,96},{80,112},{96,128},{112,144}... | collective-permute-start | bytes 786440 | tf_op jit(solution)/shard_map/ppermute | solution.py:241
  90.4 3.2 %collective-permute-start.4 = (bf16[1024,128]{1,0:T(8,128)(2,1)S(1)}, bf16[1024,128]{1,0:T(8,128)(2,1)S(1)}, u32[]{:S(2)}, u32[]{:S(2)}) collective-permute-start(bf16[1024,128]{1,0:T(8,128)(2,1)S(1)} %get-tuple-element.15), channel_id=1, source_target_pairs={{0,480},{16,496},{32,0},{48,16},{64,32},{80,48},{96,64},{112,80},{... | collective-permute-start | bytes 786440 | tf_op jit(solution)/shard_map/ppermute | solution.py:241
  93.6 4.2 %collective-permute-start.5 = (bf16[1024,128]{1,0:T(8,128)(2,1)S(1)}, bf16[1024,128]{1,0:T(8,128)(2,1)S(1)}, u32[]{:S(2)}, u32[]{:S(2)}) collective-permute-start(bf16[1024,128]{1,0:T(8,128)(2,1)S(1)} %get-tuple-element.14), channel_id=1, source_target_pairs={{0,64},{16,464},{32,96},{48,496},{64,128},{80,16},{96,160},{112,48... | collective-permute-start | bytes 786440 | tf_op jit(solution)/shard_map/ppermute | solution.py:241
  97.9 7.5 %all-to-all-done.3.state_ref = bf16[32,24,128]{2,1,0:T(8,128)(2,1)S(1)} async-done(((bf16[32,24,128]{2,1,0:T(8,128)(2,1)}), bf16[32,24,128]{2,1,0:T(8,128)(2,1)S(1)}, u32[]{:S(2)}, u32[]{:S(2)}) %all-to-all-start.3) | async-done | bytes 196640 | tf_op jit(solution)/shard_map/all_to_all | solution.py:232
  105.3 0.0 copy-start
  105.4 0.7 copy-done
  106.0 1.7 shard_map.105
  107.7 5.2 %all-to-all-start.4 = ((bf16[32,16,128]{2,1,0:T(8,128)(2,1)}), bf16[32,16,128]{2,1,0:T(8,128)(2,1)S(1)}, u32[]{:S(2)}, u32[]{:S(2)}) async-start(bf16[32,16,128]{2,1,0:T(8,128)(2,1)} %shard_map.105), calls=%async_computation.4 | async-start | bytes 262144 | tf_op jit(solution)/shard_map/all_to_all | solution.py:232
  112.9 0.0 collective-permute-done.3
  112.9 0.0 collective-permute-done.4
  112.9 0.0 collective-permute-done.5
  112.9 0.8 fusion.2
  113.7 15.3 %all-to-all-done.4 = bf16[32,16,128]{2,1,0:T(8,128)(2,1)S(1)} async-done(((bf16[32,16,128]{2,1,0:T(8,128)(2,1)}), bf16[32,16,128]{2,1,0:T(8,128)(2,1)S(1)}, u32[]{:S(2)}, u32[]{:S(2)}) %all-to-all-start.4) | async-done | bytes 131104 | tf_op jit(solution)/shard_map/all_to_all | solution.py:232
  129.1 0.0 copy-start.2
  129.1 3.4 %all-to-all-start.2 = ((bf16[8,128,128]{2,1,0:T(8,128)(2,1)}), bf16[8,128,128]{2,1,0:T(8,128)(2,1)S(1)}, u32[]{:S(2)}, u32[]{:S(2)}) async-start(bf16[8,128,128]{2,1,0:T(8,128)(2,1)} %bitcast.11), calls=%async_computation.2 | async-start | bytes 524288 | tf_op jit(solution)/shard_map/all_to_all | solution.py:232
  132.5 0.0 copy-done.3
  132.5 0.7 copy.14.skip_ref
  133.2 0.0 copy-done.2
  133.2 2.9 %shard_map.106 = (f32[128,512]{1,0:T(8,128)}, f32[1,128]{1,0:T(1,128)}) custom-call(bf16[128,512]{1,0:T(8,128)(2,1)} %dy_ref.3, bf16[128,128]{1,0:T(8,128)(2,1)} %b_ref.1, bf16[128,128]{1,0:T(8,128)(2,1)} %c_ref.3, f32[8,128]{1,0:T(8,128)} %decay_ref.3, f32[8,1]{1,0:T(8,128)} %copy.14.skip_ref, bf16[512,128]{1,0:T(8,128)(2,1)} %bitcast.36, ...), custom_call_target="tpu_custom_call" | custom-call | tf_op jit(solution)/shard_map/pallas_call | solution.py:222
  136.0 13.1 %all-to-all-done.2 = bf16[8,128,128]{2,1,0:T(8,128)(2,1)S(1)} async-done(((bf16[8,128,128]{2,1,0:T(8,128)(2,1)}), bf16[8,128,128]{2,1,0:T(8,128)(2,1)S(1)}, u32[]{:S(2)}, u32[]{:S(2)}) %all-to-all-start.2) | async-done | bytes 262176 | tf_op jit(solution)/shard_map/all_to_all | solution.py:232
  149.1 0.0 copy-start.1
  149.2 0.6 abs_reduce_fusion
  149.8 1.3 fusion.3
  151.0 21.1 %all_to_all.53 = f32[32,1,128]{2,1,0:T(1,128)S(1)} all-to-all(f32[32,1,128]{2,1,0:T(1,128)S(1)} %tile.7), channel_id=1, replica_groups=mesh['hi'=4,'lo'=4,'c'=2,'y'=4,'xh'=2,'xp'=2] {'hi','lo','c'}, dimensions={0} | all-to-all | bytes 32768 | tf_op jit(solution)/shard_map/all_to_all | solution.py:232
  172.1 12.8 %all_to_all.54 = f32[16,1,128]{2,1,0:T(1,128)} all-to-all(f32[16,1,128]{2,1,0:T(1,128)S(1)} %tile.8), channel_id=1, replica_groups=mesh['hi'=4,'lo'=4,'c'=2,'y'=4,'xh'=2,'xp'=2] {'y','xh','xp'}, dimensions={0} | all-to-all | bytes 16384 | tf_op jit(solution)/shard_map/all_to_all | solution.py:232
  184.9 0.0 copy-done.1
  184.9 1.9 %shard_map.107 = (bf16[128,512]{1,0:T(8,128)(2,1)}, bf16[128,128]{1,0:T(8,128)(2,1)}, bf16[128,512]{1,0:T(8,128)(2,1)}) custom-call(f32[16,128]{1,0:T(8,128)} %bitcast.38, f32[128,512]{1,0:T(8,128)} %get-tuple-element.11.dq_ref, f32[128,128]{1,0:T(8,128)} %copy-done.1, f32[128,512]{1,0:T(8,128)} %get-tuple-element.12.dx_ref), custom_call_target="tpu_custom_call" | custom-call | tf_op jit(solution)/shard_map/pallas_call | solution.py:222
  (4 shorter events, 0.1 us)
Async XLA Ops:
  31.9 21.5 %collective-permute-start = (bf16[1024,128]{1,0:T(8,128)(2,1)S(1)}, bf16[1024,128]{1,0:T(8,128)(2,1)S(1)}, u32[]{:S(2)}, u32[]{:S(2)}) collective-permute-start(bf16[1024,128]{1,0:T(8,128)(2,1)S(1)} %bitcast.32), channel_id=1, source_target_pairs={{0,480},{16,496},{32,0},{48,16},{64,32},{80,48},{96,64},{112,80},{... | collective-permute-start | bytes 786440 | tf_op jit(solution)/shard_map/ppermute | solution.py:241
  39.0 16.7 %collective-permute-start.1 = (bf16[1024,128]{1,0:T(8,128)(2,1)S(1)}, bf16[1024,128]{1,0:T(8,128)(2,1)S(1)}, u32[]{:S(2)}, u32[]{:S(2)}) collective-permute-start(bf16[1024,128]{1,0:T(8,128)(2,1)S(1)} %bitcast.33), channel_id=1, source_target_pairs={{0,64},{16,464},{32,96},{48,496},{64,128},{80,16},{96,160},{112,48... | collective-permute-start | bytes 786440 | tf_op jit(solution)/shard_map/ppermute | solution.py:241
  45.1 15.4 %collective-permute-start.2 = (bf16[1024,128]{1,0:T(8,128)(2,1)S(1)}, bf16[1024,128]{1,0:T(8,128)(2,1)S(1)}, u32[]{:S(2)}, u32[]{:S(2)}) collective-permute-start(bf16[1024,128]{1,0:T(8,128)(2,1)S(1)} %bitcast.34), channel_id=1, source_target_pairs={{0,32},{16,48},{32,64},{48,80},{64,96},{80,112},{96,128},{112,144}... | collective-permute-start | bytes 786440 | tf_op jit(solution)/shard_map/ppermute | solution.py:241
  77.7 27.7 %all-to-all-start.3 = ((bf16[32,24,128]{2,1,0:T(8,128)(2,1)}), bf16[32,24,128]{2,1,0:T(8,128)(2,1)S(1)}, u32[]{:S(2)}, u32[]{:S(2)}) async-start(bf16[32,24,128]{2,1,0:T(8,128)(2,1)} %shard_map.104), calls=%async_computation.3 | async-start | bytes 393216 | tf_op jit(solution)/shard_map/all_to_all | solution.py:232
  87.1 45.4 %copy-start.3 = (f32[8]{0:T(128)S(1)}, f32[8]{0:T(128)}, u32[]{:S(2)}) copy-start(f32[8]{0:T(128)} %param.15) | copy-start | bytes 100
  87.1 25.7 %collective-permute-start.3 = (bf16[1024,128]{1,0:T(8,128)(2,1)S(1)}, bf16[1024,128]{1,0:T(8,128)(2,1)S(1)}, u32[]{:S(2)}, u32[]{:S(2)}) collective-permute-start(bf16[1024,128]{1,0:T(8,128)(2,1)S(1)} %get-tuple-element.13), channel_id=1, source_target_pairs={{0,32},{16,48},{32,64},{48,80},{64,96},{80,112},{96,128},{112,144}... | collective-permute-start | bytes 786440 | tf_op jit(solution)/shard_map/ppermute | solution.py:241
  90.4 22.5 %collective-permute-start.4 = (bf16[1024,128]{1,0:T(8,128)(2,1)S(1)}, bf16[1024,128]{1,0:T(8,128)(2,1)S(1)}, u32[]{:S(2)}, u32[]{:S(2)}) collective-permute-start(bf16[1024,128]{1,0:T(8,128)(2,1)S(1)} %get-tuple-element.15), channel_id=1, source_target_pairs={{0,480},{16,496},{32,0},{48,16},{64,32},{80,48},{96,64},{112,80},{... | collective-permute-start | bytes 786440 | tf_op jit(solution)/shard_map/ppermute | solution.py:241
  93.6 19.2 %collective-permute-start.5 = (bf16[1024,128]{1,0:T(8,128)(2,1)S(1)}, bf16[1024,128]{1,0:T(8,128)(2,1)S(1)}, u32[]{:S(2)}, u32[]{:S(2)}) collective-permute-start(bf16[1024,128]{1,0:T(8,128)(2,1)S(1)} %get-tuple-element.14), channel_id=1, source_target_pairs={{0,64},{16,464},{32,96},{48,496},{64,128},{80,16},{96,160},{112,48... | collective-permute-start | bytes 786440 | tf_op jit(solution)/shard_map/ppermute | solution.py:241
  105.3 0.7 copy-start
  107.7 21.4 %all-to-all-start.4 = ((bf16[32,16,128]{2,1,0:T(8,128)(2,1)}), bf16[32,16,128]{2,1,0:T(8,128)(2,1)S(1)}, u32[]{:S(2)}, u32[]{:S(2)}) async-start(bf16[32,16,128]{2,1,0:T(8,128)(2,1)} %shard_map.105), calls=%async_computation.4 | async-start | bytes 262144 | tf_op jit(solution)/shard_map/all_to_all | solution.py:232
  129.1 4.1 %copy-start.2 = (bf16[32,16,128]{2,1,0:T(8,128)(2,1)}, bf16[32,16,128]{2,1,0:T(8,128)(2,1)S(1)}, u32[]{:S(2)}) copy-start(bf16[32,16,128]{2,1,0:T(8,128)(2,1)S(1)} %all-to-all-done.4) | copy-start | bytes 393220
  129.1 20.0 %all-to-all-start.2 = ((bf16[8,128,128]{2,1,0:T(8,128)(2,1)}), bf16[8,128,128]{2,1,0:T(8,128)(2,1)S(1)}, u32[]{:S(2)}, u32[]{:S(2)}) async-start(bf16[8,128,128]{2,1,0:T(8,128)(2,1)} %bitcast.11), calls=%async_computation.2 | async-start | bytes 524288 | tf_op jit(solution)/shard_map/all_to_all | solution.py:232
  149.1 35.8 %copy-start.1 = (f32[128,128]{1,0:T(8,128)}, f32[128,128]{1,0:T(8,128)S(1)}, u32[]{:S(2)}) copy-start(f32[128,128]{1,0:T(8,128)S(1)} %convert_reduce_fusion.dkv_ref) | copy-start | bytes 196612

commit v8 on v7

--- a/solution.py
+++ b/solution.py
@@ -48,8 +48,8 @@
     do = heads_to_rows(do_ref[...])
     width = q.shape[0]
 
-    pairs = chip // 4 + 1
     diagonal = chip // 2
+    pairs = (diagonal + 1) // 2
 
     def place(z):
         return lax.rem(lax.rem(z, 4) - lane_group + 4, 4), z // 4
@@ -100,7 +100,7 @@
     for copy in copies:
         copy.wait()
     carry = (jnp.full((1, width), -1e30, f32), jnp.zeros((8, width), f32))
-    carry = lax.fori_loop(diagonal, 2 * pairs, lambda j, c: score_step(j, c, True), carry)
+    carry = score_step(diagonal, carry, True)
     carry = lax.cond(
         diagonal % 2 == 1, lambda c: score_step(diagonal - 1, c, False), lambda c: c, carry
     )
@@ -111,9 +111,16 @@
     outt_ref[...] = jnp.zeros_like(outt_ref)
     dqt_ref[...] = jnp.zeros_like(dqt_ref)
 
-    def output_step(i, _):
+    def in_pairs(body):
+        lax.fori_loop(0, pairs, lambda i, _: body((2 * i, 2 * i + 1)), 0)
+
+        @pl.when(diagonal % 2 == 0)
+        def _():
+            body((diagonal,))
+
+    def output_step(blocks):
         step = jnp.zeros(outt_ref.shape, f32)
-        for j in (2 * i, 2 * i + 1):
+        for j in blocks:
             scales = [jnp.exp2((top_ref[2 * j + half][:1] - top) * LOG2) * inverse for half in range(2)]
             p = p_ref[rows_at(j), :]
             p = jnp.concatenate([p[: 2 * TOK] * scales[0], p[2 * TOK :] * scales[1]], axis=0)
@@ -124,27 +131,27 @@
         outt_ref[...] += step
         return 0
 
-    lax.fori_loop(0, pairs, output_step, 0)
+    in_pairs(output_step)
     dot_rows = jnp.concatenate([do_ref[:, 128 * h : 128 * (h + 1)].astype(f32).T for h in range(4)], axis=1)
     delta = jnp.sum(dot_rows * outt_ref[...].astype(bf16).astype(f32), axis=0, keepdims=True)
 
-    def gradient_step(i, _):
+    def gradient_step(blocks):
         step = jnp.zeros(dqt_ref.shape, f32)
-        for j in (2 * i, 2 * i + 1):
+        for j in blocks:
             ds = (p_ref[rows_at(j), :] * (dp_ref[rows_at(j), :] - delta)).astype(bf16)
             store_at(j, 0, (dot(ds, q, NN) * SCALE).astype(bf16))
             step = step + dot(keys_at(j, 0), ds, TN)
         dqt_ref[...] += step
         return 0
 
-    lax.fori_loop(0, pairs, gradient_step, 0)
+    in_pairs(gradient_step)
 
     def clear_step(j, _):
         for part in range(2):
             store_at(j, part, jnp.zeros((4 * TOK, 128), bf16))
         return 0
 
-    lax.fori_loop(2 * pairs, CHIPS // 2, clear_step, 0)
+    lax.fori_loop(diagonal + 1, CHIPS // 2, clear_step, 0)
     dqt = dqt_ref[...] * SCALE
     for h in range(4):
         dq_ref[:, 128 * h : 128 * (h + 1)] = dqt[:, TOK * h : TOK * (h + 1)].T

time: 188 us -> 187 us (level)
  blocking collectives: 86.8 us -> 90.3 us
  waiting for transfers between devices: 35.9 us -> 32.5 us
    all_to_all x4, blocking collectives: 70.9 us -> 74.4 us  [swap_all(): return lax.all_to_all(x, axes, 0, 0, tiled=True)]
    all_to_all x3, waiting for transfers between devices: 35.9 us -> 32.4 us  [swap_all(): return lax.all_to_all(x, axes, 0, 0, tiled=True)]
where the time goes in v8:
time: 187 us; the launch traced here: 186 us
  blocking collectives  90.3 us (48%)
  starting transfers between devices  42.2 us (23%)
  waiting for transfers between devices  32.5 us (17%)
  Pallas kernels  14.7 us (8%)
  other arithmetic  3.24 us (2%)
  local copies, waits for them, and re-layouts  2.23 us (1%)
    all_to_all x4, blocking collectives, swap_all(): return lax.all_to_all(x, axes, 0, 0, tiled=True)  74.4 us
    all_to_all x3, waiting for transfers between devices, swap_all(): return lax.all_to_all(x, axes, 0, 0, tiled=True)  32.4 us
    ppermute x6, starting transfers between devices, along_z(): return lax.ppermute(x, SEQ, route)  24.8 us
    all_to_all x3, starting transfers between devices, swap_all(): return lax.all_to_all(x, axes, 0, 0, tiled=True)  17.4 us
    all_gather x4, blocking collectives, step(): lax.all_gather(piece, 'c', axis=0, tiled=True).reshape(2, 8, TOK, 128)  15.8 us
    pallas_call x5, Pallas kernels, call(): pl.pallas_call(body, out_shape=out_shape, in_specs=specs, out_specs=jax.t...  14.7 us
  transfers between devices with their start and end apart: 9, of which 3 were waited for; matrix products, arithmetic and copies ran while one was open for 1% of the time, Pallas kernels for 4%

profile of v8, /device:TPU:1, one launch (start us, length us, event | category | flops | bytes accessed | tf_op | source)
XLA Modules:
  0.0 185.9 jit_solution(7214679729475057609)
XLA Ops:
  0.6 0.8 tile.6
  1.4 30.4 %all_to_all.51 = bf16[8,128,128]{2,1,0:T(8,128)(2,1)S(1)} all-to-all(bf16[8,128,128]{2,1,0:T(8,128)(2,1)S(1)} %tile.6), channel_id=1, replica_groups=mesh['hi'=4,'lo'=4,'c'=2,'y'=4,'xh'=2,'xp'=2] {'hi','xp'}, dimensions={0} | all-to-all | bytes 524288 | tf_op jit(solution)/shard_map/all_to_all | solution.py:239
  31.9 4.5 %collective-permute-start = (bf16[1024,128]{1,0:T(8,128)(2,1)S(1)}, bf16[1024,128]{1,0:T(8,128)(2,1)S(1)}, u32[]{:S(2)}, u32[]{:S(2)}) collective-permute-start(bf16[1024,128]{1,0:T(8,128)(2,1)S(1)} %bitcast.32), channel_id=1, source_target_pairs={{0,480},{16,496},{32,0},{48,16},{64,32},{80,48},{96,64},{112,80},{... | collective-permute-start | bytes 786440 | tf_op jit(solution)/shard_map/ppermute | solution.py:248
  36.4 2.6 %shard_map.104 = bf16[32,24,128]{2,1,0:T(8,128)(2,1)} custom-call(bf16[128,512]{1,0:T(8,128)(2,1)} %dy_ref.3, bf16[128,128]{1,0:T(8,128)(2,1)} %c_ref.3, f32[8,128]{1,0:T(8,128)} %decay_ref.3), custom_call_target="tpu_custom_call" | custom-call | tf_op jit(solution)/shard_map/pallas_call | solution.py:229
  39.0 6.2 %collective-permute-start.1 = (bf16[1024,128]{1,0:T(8,128)(2,1)S(1)}, bf16[1024,128]{1,0:T(8,128)(2,1)S(1)}, u32[]{:S(2)}, u32[]{:S(2)}) collective-permute-start(bf16[1024,128]{1,0:T(8,128)(2,1)S(1)} %bitcast.33), channel_id=1, source_target_pairs={{0,64},{16,464},{32,96},{48,496},{64,128},{80,16},{96,160},{112,48... | collective-permute-start | bytes 786440 | tf_op jit(solution)/shard_map/ppermute | solution.py:248
  45.1 3.4 %collective-permute-start.2 = (bf16[1024,128]{1,0:T(8,128)(2,1)S(1)}, bf16[1024,128]{1,0:T(8,128)(2,1)S(1)}, u32[]{:S(2)}, u32[]{:S(2)}) collective-permute-start(bf16[1024,128]{1,0:T(8,128)(2,1)S(1)} %bitcast.34), channel_id=1, source_target_pairs={{0,32},{16,48},{32,64},{48,80},{64,96},{80,112},{96,128},{112,144}... | collective-permute-start | bytes 786440 | tf_op jit(solution)/shard_map/ppermute | solution.py:248
  48.5 4.9 %all_gather.12 = bf16[2048,128]{1,0:T(8,128)(2,1)} all-gather(bf16[1024,128]{1,0:T(8,128)(2,1)S(1)} %bitcast.35), channel_id=1, replica_groups=mesh['hi'=4,'lo'=4,'c'=2,'y'=4,'xh'=2,'xp'=2] {'c'}, dimensions={0}, use_global_device_ids=true | all-gather | bytes 786432 | tf_op jit(solution)/shard_map/all_gather | solution.py:273
  53.4 0.0 collective-permute-done
  53.4 2.3 %all_gather.13 = bf16[2048,128]{1,0:T(8,128)(2,1)} all-gather(bf16[1024,128]{1,0:T(8,128)(2,1)S(1)} %collective-permute-done), channel_id=1, replica_groups=mesh['hi'=4,'lo'=4,'c'=2,'y'=4,'xh'=2,'xp'=2] {'c'}, dimensions={0}, use_global_device_ids=true | all-gather | bytes 786432 | tf_op jit(solution)/shard_map/all_gather | solution.py:273
  55.7 0.0 collective-permute-done.1
  55.7 4.8 %all_gather.14 = bf16[2048,128]{1,0:T(8,128)(2,1)} all-gather(bf16[1024,128]{1,0:T(8,128)(2,1)S(1)} %collective-permute-done.1), channel_id=1, replica_groups=mesh['hi'=4,'lo'=4,'c'=2,'y'=4,'xh'=2,'xp'=2] {'c'}, dimensions={0}, use_global_device_ids=true | all-gather | bytes 786432 | tf_op jit(solution)/shard_map/all_gather | solution.py:273
  60.5 0.0 collective-permute-done.2
  60.5 3.9 %all_gather.15 = bf16[2048,128]{1,0:T(8,128)(2,1)} all-gather(bf16[1024,128]{1,0:T(8,128)(2,1)S(1)} %collective-permute-done.2), channel_id=1, replica_groups=mesh['hi'=4,'lo'=4,'c'=2,'y'=4,'xh'=2,'xp'=2] {'c'}, dimensions={0}, use_global_device_ids=true | all-gather | bytes 786432 | tf_op jit(solution)/shard_map/all_gather | solution.py:273
  64.4 5.7 %shard_map.103 = (f32[128,512]{1,0:T(8,128)}, bf16[2,4,4,2,128,128]{5,4,3,2,1,0:T(8,128)(2,1)}, f32[8,128]{1,0:T(8,128)}) custom-call(bf16[128,512]{1,0:T(8,128)(2,1)} %q_ref.1, bf16[128,512]{1,0:T(8,128)(2,1)} %do_ref.1, bf16[2,8,128,128]{3,2,1,0:T(8,128)(2,1)} %bitcast.28, bf16[2,8,128,128]{3,2,1,0:T(8,128)(2,1)} %bitcast.29, ...), custom_call_target="tpu_custom_call" | custom-call | tf_op jit(solution)/shard_map/pallas_call | solution.py:229
  70.1 6.6 %all_to_all.52 = bf16[2,4096,128]{2,1,0:T(8,128)(2,1)S(1)} all-to-all(bf16[2,4096,128]{2,1,0:T(8,128)(2,1)} %bitcast.27), channel_id=1, replica_groups=mesh['hi'=4,'lo'=4,'c'=2,'y'=4,'xh'=2,'xp'=2] {'c'}, dimensions={0} | all-to-all | bytes 4194304 | tf_op jit(solution)/shard_map/all_to_all | solution.py:239
  76.7 8.9 %all-to-all-start.3 = ((bf16[32,24,128]{2,1,0:T(8,128)(2,1)}), bf16[32,24,128]{2,1,0:T(8,128)(2,1)S(1)}, u32[]{:S(2)}, u32[]{:S(2)}) async-start(bf16[32,24,128]{2,1,0:T(8,128)(2,1)} %shard_map.104), calls=%async_computation.3 | async-start | bytes 393216 | tf_op jit(solution)/shard_map/all_to_all | solution.py:239
  85.6 0.3 convert_element_type.33
  85.9 0.2 fusion
  86.1 0.0 copy-start.3
  86.1 0.1 slice_bitcast_fusion.2
  86.2 3.3 %collective-permute-start.3 = (bf16[1024,128]{1,0:T(8,128)(2,1)S(1)}, bf16[1024,128]{1,0:T(8,128)(2,1)S(1)}, u32[]{:S(2)}, u32[]{:S(2)}) collective-permute-start(bf16[1024,128]{1,0:T(8,128)(2,1)S(1)} %get-tuple-element.13), channel_id=1, source_target_pairs={{0,32},{16,48},{32,64},{48,80},{64,96},{80,112},{96,128},{112,144}... | collective-permute-start | bytes 786440 | tf_op jit(solution)/shard_map/ppermute | solution.py:248
  89.4 3.2 %collective-permute-start.4 = (bf16[1024,128]{1,0:T(8,128)(2,1)S(1)}, bf16[1024,128]{1,0:T(8,128)(2,1)S(1)}, u32[]{:S(2)}, u32[]{:S(2)}) collective-permute-start(bf16[1024,128]{1,0:T(8,128)(2,1)S(1)} %get-tuple-element.15), channel_id=1, source_target_pairs={{0,480},{16,496},{32,0},{48,16},{64,32},{80,48},{96,64},{112,80},{... | collective-permute-start | bytes 786440 | tf_op jit(solution)/shard_map/ppermute | solution.py:248
  92.7 4.2 %collective-permute-start.5 = (bf16[1024,128]{1,0:T(8,128)(2,1)S(1)}, bf16[1024,128]{1,0:T(8,128)(2,1)S(1)}, u32[]{:S(2)}, u32[]{:S(2)}) collective-permute-start(bf16[1024,128]{1,0:T(8,128)(2,1)S(1)} %get-tuple-element.14), channel_id=1, source_target_pairs={{0,64},{16,464},{32,96},{48,496},{64,128},{80,16},{96,160},{112,48... | collective-permute-start | bytes 786440 | tf_op jit(solution)/shard_map/ppermute | solution.py:248
  96.9 7.5 %all-to-all-done.3.state_ref = bf16[32,24,128]{2,1,0:T(8,128)(2,1)S(1)} async-done(((bf16[32,24,128]{2,1,0:T(8,128)(2,1)}), bf16[32,24,128]{2,1,0:T(8,128)(2,1)S(1)}, u32[]{:S(2)}, u32[]{:S(2)}) %all-to-all-start.3) | async-done | bytes 196640 | tf_op jit(solution)/shard_map/all_to_all | solution.py:239
  104.4 0.0 copy-start
  104.4 0.7 copy-done
  105.0 1.7 shard_map.105
  106.7 5.2 %all-to-all-start.4 = ((bf16[32,16,128]{2,1,0:T(8,128)(2,1)}), bf16[32,16,128]{2,1,0:T(8,128)(2,1)S(1)}, u32[]{:S(2)}, u32[]{:S(2)}) async-start(bf16[32,16,128]{2,1,0:T(8,128)(2,1)} %shard_map.105), calls=%async_computation.4 | async-start | bytes 262144 | tf_op jit(solution)/shard_map/all_to_all | solution.py:239
  111.9 0.0 collective-permute-done.3
  111.9 0.0 collective-permute-done.4
  111.9 0.0 collective-permute-done.5
  111.9 0.8 fusion.2
  112.8 15.3 %all-to-all-done.4 = bf16[32,16,128]{2,1,0:T(8,128)(2,1)S(1)} async-done(((bf16[32,16,128]{2,1,0:T(8,128)(2,1)}), bf16[32,16,128]{2,1,0:T(8,128)(2,1)S(1)}, u32[]{:S(2)}, u32[]{:S(2)}) %all-to-all-start.4) | async-done | bytes 131104 | tf_op jit(solution)/shard_map/all_to_all | solution.py:239
  128.1 0.0 copy-start.2
  128.1 3.4 %all-to-all-start.2 = ((bf16[8,128,128]{2,1,0:T(8,128)(2,1)}), bf16[8,128,128]{2,1,0:T(8,128)(2,1)S(1)}, u32[]{:S(2)}, u32[]{:S(2)}) async-start(bf16[8,128,128]{2,1,0:T(8,128)(2,1)} %bitcast.11), calls=%async_computation.2 | async-start | bytes 524288 | tf_op jit(solution)/shard_map/all_to_all | solution.py:239
  131.5 0.0 copy-done.3
  131.5 0.7 copy.14.skip_ref
  132.2 0.0 copy-done.2
  132.2 2.9 %shard_map.106 = (f32[128,512]{1,0:T(8,128)}, f32[1,128]{1,0:T(1,128)}) custom-call(bf16[128,512]{1,0:T(8,128)(2,1)} %dy_ref.3, bf16[128,128]{1,0:T(8,128)(2,1)} %b_ref.1, bf16[128,128]{1,0:T(8,128)(2,1)} %c_ref.3, f32[8,128]{1,0:T(8,128)} %decay_ref.3, f32[8,1]{1,0:T(8,128)} %copy.14.skip_ref, bf16[512,128]{1,0:T(8,128)(2,1)} %bitcast.36, ...), custom_call_target="tpu_custom_call" | custom-call | tf_op jit(solution)/shard_map/pallas_call | solution.py:229
  135.1 9.7 %all-to-all-done.2 = bf16[8,128,128]{2,1,0:T(8,128)(2,1)S(1)} async-done(((bf16[8,128,128]{2,1,0:T(8,128)(2,1)}), bf16[8,128,128]{2,1,0:T(8,128)(2,1)S(1)}, u32[]{:S(2)}, u32[]{:S(2)}) %all-to-all-start.2) | async-done | bytes 262176 | tf_op jit(solution)/shard_map/all_to_all | solution.py:239
  144.8 0.0 copy-start.1
  144.8 0.6 abs_reduce_fusion
  145.4 1.3 fusion.3
  146.6 24.6 %all_to_all.53 = f32[32,1,128]{2,1,0:T(1,128)S(1)} all-to-all(f32[32,1,128]{2,1,0:T(1,128)S(1)} %tile.7), channel_id=1, replica_groups=mesh['hi'=4,'lo'=4,'c'=2,'y'=4,'xh'=2,'xp'=2] {'hi','lo','c'}, dimensions={0} | all-to-all | bytes 32768 | tf_op jit(solution)/shard_map/all_to_all | solution.py:239
  171.2 12.8 %all_to_all.54 = f32[16,1,128]{2,1,0:T(1,128)} all-to-all(f32[16,1,128]{2,1,0:T(1,128)S(1)} %tile.8), channel_id=1, replica_groups=mesh['hi'=4,'lo'=4,'c'=2,'y'=4,'xh'=2,'xp'=2] {'y','xh','xp'}, dimensions={0} | all-to-all | bytes 16384 | tf_op jit(solution)/shard_map/all_to_all | solution.py:239
  184.0 0.0 copy-done.1
  184.0 1.9 %shard_map.107 = (bf16[128,512]{1,0:T(8,128)(2,1)}, bf16[128,128]{1,0:T(8,128)(2,1)}, bf16[128,512]{1,0:T(8,128)(2,1)}) custom-call(f32[16,128]{1,0:T(8,128)} %bitcast.38, f32[128,512]{1,0:T(8,128)} %get-tuple-element.11.dq_ref, f32[128,128]{1,0:T(8,128)} %copy-done.1, f32[128,512]{1,0:T(8,128)} %get-tuple-element.12.dx_ref), custom_call_target="tpu_custom_call" | custom-call | tf_op jit(solution)/shard_map/pallas_call | solution.py:229
  (4 shorter events, 0.1 us)
Async XLA Ops:
  31.9 21.5 %collective-permute-start = (bf16[1024,128]{1,0:T(8,128)(2,1)S(1)}, bf16[1024,128]{1,0:T(8,128)(2,1)S(1)}, u32[]{:S(2)}, u32[]{:S(2)}) collective-permute-start(bf16[1024,128]{1,0:T(8,128)(2,1)S(1)} %bitcast.32), channel_id=1, source_target_pairs={{0,480},{16,496},{32,0},{48,16},{64,32},{80,48},{96,64},{112,80},{... | collective-permute-start | bytes 786440 | tf_op jit(solution)/shard_map/ppermute | solution.py:248
  39.0 16.7 %collective-permute-start.1 = (bf16[1024,128]{1,0:T(8,128)(2,1)S(1)}, bf16[1024,128]{1,0:T(8,128)(2,1)S(1)}, u32[]{:S(2)}, u32[]{:S(2)}) collective-permute-start(bf16[1024,128]{1,0:T(8,128)(2,1)S(1)} %bitcast.33), channel_id=1, source_target_pairs={{0,64},{16,464},{32,96},{48,496},{64,128},{80,16},{96,160},{112,48... | collective-permute-start | bytes 786440 | tf_op jit(solution)/shard_map/ppermute | solution.py:248
  45.1 15.4 %collective-permute-start.2 = (bf16[1024,128]{1,0:T(8,128)(2,1)S(1)}, bf16[1024,128]{1,0:T(8,128)(2,1)S(1)}, u32[]{:S(2)}, u32[]{:S(2)}) collective-permute-start(bf16[1024,128]{1,0:T(8,128)(2,1)S(1)} %bitcast.34), channel_id=1, source_target_pairs={{0,32},{16,48},{32,64},{48,80},{64,96},{80,112},{96,128},{112,144}... | collective-permute-start | bytes 786440 | tf_op jit(solution)/shard_map/ppermute | solution.py:248
  76.7 27.7 %all-to-all-start.3 = ((bf16[32,24,128]{2,1,0:T(8,128)(2,1)}), bf16[32,24,128]{2,1,0:T(8,128)(2,1)S(1)}, u32[]{:S(2)}, u32[]{:S(2)}) async-start(bf16[32,24,128]{2,1,0:T(8,128)(2,1)} %shard_map.104), calls=%async_computation.3 | async-start | bytes 393216 | tf_op jit(solution)/shard_map/all_to_all | solution.py:239
  86.1 45.4 %copy-start.3 = (f32[8]{0:T(128)S(1)}, f32[8]{0:T(128)}, u32[]{:S(2)}) copy-start(f32[8]{0:T(128)} %param.15) | copy-start | bytes 100
  86.2 25.7 %collective-permute-start.3 = (bf16[1024,128]{1,0:T(8,128)(2,1)S(1)}, bf16[1024,128]{1,0:T(8,128)(2,1)S(1)}, u32[]{:S(2)}, u32[]{:S(2)}) collective-permute-start(bf16[1024,128]{1,0:T(8,128)(2,1)S(1)} %get-tuple-element.13), channel_id=1, source_target_pairs={{0,32},{16,48},{32,64},{48,80},{64,96},{80,112},{96,128},{112,144}... | collective-permute-start | bytes 786440 | tf_op jit(solution)/shard_map/ppermute | solution.py:248
  89.4 22.5 %collective-permute-start.4 = (bf16[1024,128]{1,0:T(8,128)(2,1)S(1)}, bf16[1024,128]{1,0:T(8,128)(2,1)S(1)}, u32[]{:S(2)}, u32[]{:S(2)}) collective-permute-start(bf16[1024,128]{1,0:T(8,128)(2,1)S(1)} %get-tuple-element.15), channel_id=1, source_target_pairs={{0,480},{16,496},{32,0},{48,16},{64,32},{80,48},{96,64},{112,80},{... | collective-permute-start | bytes 786440 | tf_op jit(solution)/shard_map/ppermute | solution.py:248
  92.7 19.2 %collective-permute-start.5 = (bf16[1024,128]{1,0:T(8,128)(2,1)S(1)}, bf16[1024,128]{1,0:T(8,128)(2,1)S(1)}, u32[]{:S(2)}, u32[]{:S(2)}) collective-permute-start(bf16[1024,128]{1,0:T(8,128)(2,1)S(1)} %get-tuple-element.14), channel_id=1, source_target_pairs={{0,64},{16,464},{32,96},{48,496},{64,128},{80,16},{96,160},{112,48... | collective-permute-start | bytes 786440 | tf_op jit(solution)/shard_map/ppermute | solution.py:248
  104.4 0.7 copy-start
  106.7 21.4 %all-to-all-start.4 = ((bf16[32,16,128]{2,1,0:T(8,128)(2,1)}), bf16[32,16,128]{2,1,0:T(8,128)(2,1)S(1)}, u32[]{:S(2)}, u32[]{:S(2)}) async-start(bf16[32,16,128]{2,1,0:T(8,128)(2,1)} %shard_map.105), calls=%async_computation.4 | async-start | bytes 262144 | tf_op jit(solution)/shard_map/all_to_all | solution.py:239
  128.1 4.1 %copy-start.2 = (bf16[32,16,128]{2,1,0:T(8,128)(2,1)}, bf16[32,16,128]{2,1,0:T(8,128)(2,1)S(1)}, u32[]{:S(2)}) copy-start(bf16[32,16,128]{2,1,0:T(8,128)(2,1)S(1)} %all-to-all-done.4) | copy-start | bytes 393220
  128.1 16.6 %all-to-all-start.2 = ((bf16[8,128,128]{2,1,0:T(8,128)(2,1)}), bf16[8,128,128]{2,1,0:T(8,128)(2,1)S(1)}, u32[]{:S(2)}, u32[]{:S(2)}) async-start(bf16[8,128,128]{2,1,0:T(8,128)(2,1)} %bitcast.11), calls=%async_computation.2 | async-start | bytes 524288 | tf_op jit(solution)/shard_map/all_to_all | solution.py:239
  144.8 39.3 %copy-start.1 = (f32[128,128]{1,0:T(8,128)}, f32[128,128]{1,0:T(8,128)S(1)}, u32[]{:S(2)}) copy-start(f32[128,128]{1,0:T(8,128)S(1)} %convert_reduce_fusion.dkv_ref) | copy-start | bytes 196612
